TPU v7x, 32 devices: a whole 2x2x4 slice. The times are simulated.
32 devices in a mesh: rep: 4 (over y, core), seq: 2 (over x), ctx: 4 (over z).
Axes of the slice: x: 2, y: 2, z: 4, core: 2. Of those that a mesh axis runs over, the one named last changes fastest.
Arguments:
- tokens: bfloat16 [8192, 2048], P(('rep', 'seq', 'ctx')), may hold values from -6 to 6
- cotangent: bfloat16 [8192, 2048], P(('rep', 'seq', 'ctx')), may hold values from -6 to 6
- document_index: int32 [8192], P(('rep', 'seq')), may hold values from 0 to 10, as said below
- padding_token_mask: int32 [8192], P(('rep', 'seq')), may hold values from 0 to 1, as said below
- attention_gain: bfloat16 [2048], P(('seq', 'ctx')), may hold values from 0.099609375 to 1.8984375
- projection_weight: bfloat16 [2048, 6144], P(('seq', 'ctx')), may hold values from -0.125 to 0.125
- head_gain: bfloat16 [2, 128], replicated, may hold values from 0.099609375 to 1.8984375
- out_weight: bfloat16 [2048, 2048], P(('seq', 'ctx')), may hold values from -2 to 2
- feedforward_gain: bfloat16 [2048], P(('seq', 'ctx')), may hold values from 0.099609375 to 1.8984375
- gate_weight: bfloat16 [2048, 6144], P(('seq', 'ctx')), may hold values from -0.125 to 0.125
- up_weight: bfloat16 [2048, 6144], P(('seq', 'ctx')), may hold values from -0.125 to 0.125
- down_weight: bfloat16 [2048, 6144], P(('seq', 'ctx')), may hold values from -0.078125 to 0.078125
Outputs:
- layer_out: bfloat16 [8192, 2048], P(('rep', 'seq', 'ctx'))
- tokens_grad: bfloat16 [8192, 2048], P(('rep', 'seq', 'ctx'))
- attention_gain_grad: float32 [2048], P(('seq', 'ctx'))
- proj_weight_grad: float32 [2048, 6144], P(('seq', 'ctx'))
- head_gain_grad: float32 [2, 128], replicated
- out_weight_grad: float32 [2048, 2048], P(('seq', 'ctx'))
- feedforward_gain_grad: float32 [2048], P(('seq', 'ctx'))
- gate_weight_grad: float32 [2048, 6144], P(('seq', 'ctx'))
- up_weight_grad: float32 [2048, 6144], P(('seq', 'ctx'))
- down_weight_grad: float32 [2048, 6144], P(('seq', 'ctx'))
Inputs may be any that keep to these rules, and one draw needn't show every extreme that they name: `document_index`: along each sequence of 1024 tokens the ids never fall. `padding_token_mask`: the zeros of a sequence form one run at its end.
All inputs are finite; a program needn't handle non-finite values.
Results may differ from a plain program's by a relative error of at most 0.02.
Values may be sent and summed in bfloat16 or wider, within the bound.
A program may use at most 640 MiB of HBM per device.

v0:
```python
import jax
import jax.numpy as jnp
from jax import lax
from jax.sharding import PartitionSpec as P

QUERY_HEADS = 16
KEY_VALUE_HEADS = 8
HEAD_SIZE = 128


norm_epsilon = 1e-06
rope_base = 1000000.0
masked_value = -1e30
contract_rows = (((0,), (0,)), ((), ()))
contract_cols = (((1,), (1,)), ((), ()))


def rope_tables(positions):
    half_size = HEAD_SIZE // 2
    frequency = rope_base ** (-2.0 * jnp.arange(half_size, dtype=jnp.float32) / HEAD_SIZE)
    angles = positions.astype(jnp.float32)[:, None, None] * frequency[None, None, :]
    return (jnp.cos(angles), jnp.sin(angles))


def rotate(value_rows, cosine_table, sine_table):
    half_size = value_rows.shape[-1] // 2
    first_half = value_rows[..., :half_size]
    second_half = value_rows[..., half_size:]
    return jnp.concatenate(
        [
            first_half * cosine_table - second_half * sine_table,
            second_half * cosine_table + first_half * sine_table,
        ],
        axis=-1,
    )


def inverse_rotation(grads, cosine_table, sine_table):
    half_size = grads.shape[-1] // 2
    first_half = grads[..., :half_size]
    second_half = grads[..., half_size:]
    return jnp.concatenate(
        [
            first_half * cosine_table + second_half * sine_table,
            second_half * cosine_table - first_half * sine_table,
        ],
        axis=-1,
    )


def head_norm(value_rows, gain):
    root_factor = lax.rsqrt(
        jnp.mean(value_rows * value_rows, axis=-1, keepdims=True) + norm_epsilon
    )
    unit_values = value_rows * root_factor
    return (unit_values * gain, unit_values, root_factor)


def norm_back(grad_out, unit_values, root_factor, gain):
    scaled = grad_out * gain
    return root_factor * (
        scaled - unit_values * jnp.mean(scaled * unit_values, axis=-1, keepdims=True)
    )


def over_replicas(grad_parts):
    return (
        lax.psum(grad_parts[0].astype(jnp.bfloat16), "rep").astype(jnp.float32),
        lax.psum(grad_parts[1].astype(jnp.bfloat16), "rep").astype(jnp.float32),
    )


def per_device(
    tokens,
    cotangent,
    document_index,
    padding_token_mask,
    attention_gain,
    projection_weight,
    head_gain,
    out_weight,
    feedforward_gain,
    gate_weight,
    up_weight,
    down_weight,
):
    token_rows = tokens.shape[0]
    sequence_length = document_index.shape[0]
    shard_rows = projection_weight.shape[0]
    proj_width = projection_weight.shape[1]
    ff_width = gate_weight.shape[1]
    query_total_width = QUERY_HEADS * HEAD_SIZE
    key_total_width = KEY_VALUE_HEADS * HEAD_SIZE
    query_group_width = QUERY_HEADS // KEY_VALUE_HEADS
    score_scale = HEAD_SIZE ** (-0.5)
    tokens_wide = tokens.astype(jnp.float32)
    root_attn = lax.rsqrt(jnp.mean(tokens_wide * tokens_wide, axis=1, keepdims=True) + norm_epsilon)
    unit_attn = tokens_wide * root_attn
    gain_piece = lax.all_gather(attention_gain, ("seq", "ctx"), axis=0, tiled=True)
    weight_piece = lax.all_gather(projection_weight, ("seq", "ctx"), axis=0, tiled=True)
    columns = unit_attn
    normed = (columns * gain_piece.astype(jnp.float32)).astype(jnp.bfloat16)
    result = (
        jnp.dot(normed, weight_piece, preferred_element_type=jnp.float32),
        gain_piece.astype(jnp.float32),
        normed,
    )
    folded_proj = result
    projected_rows = folded_proj[0]
    gain_attn_full = folded_proj[1]
    normed_attn = folded_proj[2]
    queries_raw = projected_rows[:, :query_total_width].reshape(token_rows, QUERY_HEADS, HEAD_SIZE)
    gate_logits = projected_rows[:, query_total_width : 2 * query_total_width]
    keys_raw = projected_rows[
        :, 2 * query_total_width : 2 * query_total_width + key_total_width
    ].reshape(token_rows, KEY_VALUE_HEADS, HEAD_SIZE)
    values_raw = projected_rows[:, 2 * query_total_width + key_total_width :]
    first_row = lax.axis_index("ctx") * token_rows
    positions = first_row + jnp.arange(token_rows, dtype=jnp.int32)
    cosine_table, sine_table = rope_tables(positions)
    head_gain_wide = head_gain.astype(jnp.float32)
    query_normed, query_unit, query_root = head_norm(queries_raw, head_gain_wide[0])
    key_normed, key_unit, key_root = head_norm(keys_raw, head_gain_wide[1])
    query_low = (
        rotate(query_normed, cosine_table, sine_table)
        .astype(jnp.bfloat16)
        .reshape(token_rows, KEY_VALUE_HEADS, query_group_width, HEAD_SIZE)
    )
    key_low = (
        rotate(key_normed, cosine_table, sine_table)
        .astype(jnp.bfloat16)
        .reshape(token_rows, key_total_width)
    )
    value_low = values_raw.astype(jnp.bfloat16)
    every_key, every_value = (
        lax.all_gather(key_low, "ctx", axis=0, tiled=True),
        lax.all_gather(value_low, "ctx", axis=0, tiled=True),
    )
    every_key = every_key.reshape(sequence_length, KEY_VALUE_HEADS, HEAD_SIZE)
    every_value = every_value.reshape(sequence_length, KEY_VALUE_HEADS, HEAD_SIZE)
    seg_here = lax.dynamic_slice_in_dim(document_index, first_row, token_rows, 0)
    pad_here = lax.dynamic_slice_in_dim(padding_token_mask, first_row, token_rows, 0)
    key_places = jnp.arange(sequence_length, dtype=jnp.int32)
    allowed = (seg_here[:, None] == document_index[None, :]) & (
        key_places[None, :] <= positions[:, None]
    ) & (padding_token_mask[None, :] == 1) | (key_places[None, :] == positions[:, None])

    def masked_scores():
        raw_scores = (
            jnp.einsum("qhgd,khd->hgqk", query_low, every_key, preferred_element_type=jnp.float32)
            * score_scale
        )
        return jnp.where(allowed[None, None], raw_scores, masked_value)

    scores = masked_scores()
    peak = jnp.max(scores, axis=3, keepdims=True)
    exp_scores = jnp.exp(scores - peak)
    denominator = jnp.sum(exp_scores, axis=3, keepdims=True)
    log_total = peak + jnp.log(denominator)
    probs_low = (exp_scores / denominator).astype(jnp.bfloat16)
    attended_rows = jnp.einsum(
        "hgqk,khd->qhgd", probs_low, every_value, preferred_element_type=jnp.float32
    ).reshape(token_rows, query_total_width)
    gate_activations = jax.nn.sigmoid(gate_logits)
    mixed_heads = (attended_rows * gate_activations).astype(jnp.bfloat16)
    columns = lax.dot_general(
        mixed_heads,
        lax.all_gather(out_weight, ("seq", "ctx"), axis=0, tiled=True),
        contract_cols,
        preferred_element_type=jnp.float32,
    )
    result = (columns,)
    folded_out = result
    resid_mid = tokens_wide + folded_out[0]
    root_mlp = lax.rsqrt(jnp.mean(resid_mid * resid_mid, axis=1, keepdims=True) + norm_epsilon)
    unit_mlp = resid_mid * root_mlp
    gain_piece = lax.all_gather(feedforward_gain, ("seq", "ctx"), axis=0, tiled=True)
    gate_piece = lax.all_gather(gate_weight, ("seq", "ctx"), axis=0, tiled=True)
    up_piece = lax.all_gather(up_weight, ("seq", "ctx"), axis=0, tiled=True)
    columns = unit_mlp
    normed = (columns * gain_piece.astype(jnp.float32)).astype(jnp.bfloat16)
    result = (
        jnp.dot(normed, gate_piece, preferred_element_type=jnp.float32),
        jnp.dot(normed, up_piece, preferred_element_type=jnp.float32),
        gain_piece.astype(jnp.float32),
        normed,
    )
    folded_mlp = result
    gate_lin = folded_mlp[0]
    up_lin = folded_mlp[1]
    gain_mlp_full = folded_mlp[2]
    normed_mlp = folded_mlp[3]
    gate_sig = jax.nn.sigmoid(gate_lin)
    silu_gate = gate_lin * gate_sig
    hidden_low = (silu_gate * up_lin).astype(jnp.bfloat16)
    columns = lax.dot_general(
        hidden_low,
        lax.all_gather(down_weight, ("seq", "ctx"), axis=0, tiled=True),
        contract_cols,
        preferred_element_type=jnp.float32,
    )
    result = (columns,)
    layer_out = (resid_mid + result[0]).astype(jnp.bfloat16)
    masked_grad = cotangent.astype(jnp.float32) * pad_here.astype(jnp.float32)[:, None]
    d_out_low = masked_grad.astype(jnp.bfloat16)
    columns = d_out_low
    d_hidden = jnp.dot(
        columns,
        lax.all_gather(down_weight, ("seq", "ctx"), axis=0, tiled=True),
        preferred_element_type=jnp.float32,
    )
    d_gate_low = (d_hidden * up_lin * gate_sig * (1.0 + gate_lin * (1.0 - gate_sig))).astype(
        jnp.bfloat16
    )
    d_up_low = (d_hidden * silu_gate).astype(jnp.bfloat16)
    gate_piece = lax.all_gather(gate_weight, ("seq", "ctx"), axis=0, tiled=True)
    up_piece = lax.all_gather(up_weight, ("seq", "ctx"), axis=0, tiled=True)
    columns = lax.dot_general(
        d_gate_low, gate_piece, contract_cols, preferred_element_type=jnp.float32
    ) + lax.dot_general(d_up_low, up_piece, contract_cols, preferred_element_type=jnp.float32)
    d_normed_mlp = columns
    normed_rows = normed_mlp
    grad_rows = d_out_low
    mlp_grads = lax.psum_scatter(
        jnp.concatenate(
            [
                lax.dot_general(
                    normed_rows, d_gate_low, contract_rows, preferred_element_type=jnp.float32
                ),
                lax.dot_general(
                    normed_rows, d_up_low, contract_rows, preferred_element_type=jnp.float32
                ),
                lax.dot_general(
                    grad_rows, hidden_low, contract_rows, preferred_element_type=jnp.float32
                ),
            ],
            axis=1,
        ).astype(jnp.bfloat16),
        ("seq", "ctx"),
        scatter_dimension=0,
        tiled=True,
    ).astype(jnp.float32)
    gain_mlp_term = jnp.sum(d_normed_mlp * unit_mlp, axis=0)
    d_resid_mid = masked_grad + norm_back(d_normed_mlp, unit_mlp, root_mlp, gain_mlp_full)
    d_attn_low = d_resid_mid.astype(jnp.bfloat16)
    columns = d_attn_low
    mixed_gradient = jnp.dot(
        columns,
        lax.all_gather(out_weight, ("seq", "ctx"), axis=0, tiled=True),
        preferred_element_type=jnp.float32,
    )
    d_gate_logits = mixed_gradient * attended_rows * gate_activations * (1.0 - gate_activations)
    d_attended_low = (
        (mixed_gradient * gate_activations)
        .astype(jnp.bfloat16)
        .reshape(token_rows, KEY_VALUE_HEADS, query_group_width, HEAD_SIZE)
    )
    probs = jnp.exp(masked_scores() - log_total)
    d_probs = jnp.einsum(
        "qhgd,khd->hgqk", d_attended_low, every_value, preferred_element_type=jnp.float32
    )
    value_term = jnp.einsum(
        "hgqk,qhgd->khd", probs_low, d_attended_low, preferred_element_type=jnp.float32
    )
    delta = jnp.sum(probs * d_probs, axis=3, keepdims=True)
    d_scores_low = (probs * (d_probs - delta)).astype(jnp.bfloat16)
    d_queries = (
        jnp.einsum("hgqk,khd->qhgd", d_scores_low, every_key, preferred_element_type=jnp.float32)
        * score_scale
    )
    key_term = (
        jnp.einsum("hgqk,qhgd->khd", d_scores_low, query_low, preferred_element_type=jnp.float32)
        * score_scale
    )
    key_gradient, d_values = (
        lax.psum_scatter(
            key_term.reshape(sequence_length, key_total_width).astype(jnp.bfloat16),
            "ctx",
            scatter_dimension=0,
            tiled=True,
        ).astype(jnp.float32),
        lax.psum_scatter(
            value_term.reshape(sequence_length, key_total_width).astype(jnp.bfloat16),
            "ctx",
            scatter_dimension=0,
            tiled=True,
        ).astype(jnp.float32),
    )
    d_query_normed = inverse_rotation(
        d_queries.reshape(token_rows, QUERY_HEADS, HEAD_SIZE), cosine_table, sine_table
    )
    normed_key_gradient = inverse_rotation(
        key_gradient.reshape(token_rows, KEY_VALUE_HEADS, HEAD_SIZE), cosine_table, sine_table
    )
    head_term = jnp.stack(
        [
            jnp.sum(d_query_normed * query_unit, axis=(0, 1)),
            jnp.sum(normed_key_gradient * key_unit, axis=(0, 1)),
        ]
    )
    d_query_raw = norm_back(d_query_normed, query_unit, query_root, head_gain_wide[0])
    d_key_raw = norm_back(normed_key_gradient, key_unit, key_root, head_gain_wide[1])
    d_proj_low = jnp.concatenate(
        [
            d_query_raw.reshape(token_rows, query_total_width),
            d_gate_logits,
            d_key_raw.reshape(token_rows, key_total_width),
            d_values,
        ],
        axis=1,
    ).astype(jnp.bfloat16)
    columns = lax.dot_general(
        d_proj_low,
        lax.all_gather(projection_weight, ("seq", "ctx"), axis=0, tiled=True),
        contract_cols,
        preferred_element_type=jnp.float32,
    )
    normed_rows = normed_attn
    grad_rows = d_attn_low
    attn_grads = lax.psum_scatter(
        jnp.concatenate(
            [
                lax.dot_general(
                    normed_rows, d_proj_low, contract_rows, preferred_element_type=jnp.float32
                ),
                lax.dot_general(
                    grad_rows, mixed_heads, contract_rows, preferred_element_type=jnp.float32
                ),
            ],
            axis=1,
        ).astype(jnp.bfloat16),
        ("seq", "ctx"),
        scatter_dimension=0,
        tiled=True,
    ).astype(jnp.float32)
    gain_attn_term = jnp.sum(columns * unit_attn, axis=0)
    tokens_grad = (d_resid_mid + norm_back(columns, unit_attn, root_attn, gain_attn_full)).astype(
        jnp.bfloat16
    )
    sum_attn_gain, sum_mlp_gain, sum_head_gain = lax.psum(
        (gain_attn_term, gain_mlp_term, head_term), ("rep", "seq", "ctx")
    )
    mlp_grads, attn_grads = over_replicas((mlp_grads, attn_grads))
    group_rank = lax.axis_index(("seq", "ctx"))
    attention_gain_grad = lax.dynamic_slice_in_dim(
        sum_attn_gain, group_rank * shard_rows, shard_rows, 0
    )
    feedforward_gain_grad = lax.dynamic_slice_in_dim(
        sum_mlp_gain, group_rank * shard_rows, shard_rows, 0
    )
    return (
        layer_out,
        tokens_grad,
        attention_gain_grad,
        attn_grads[:, :proj_width],
        sum_head_gain,
        attn_grads[:, proj_width:],
        feedforward_gain_grad,
        mlp_grads[:, :ff_width],
        mlp_grads[:, ff_width : 2 * ff_width],
        mlp_grads[:, 2 * ff_width :],
    )


def solution(mesh):
    in_specs = (
        P(("rep", "seq", "ctx"), None),
        P(("rep", "seq", "ctx"), None),
        P(("rep", "seq")),
        P(("rep", "seq")),
        P(("seq", "ctx")),
        P(("seq", "ctx"), None),
        P(),
        P(("seq", "ctx"), None),
        P(("seq", "ctx")),
        P(("seq", "ctx"), None),
        P(("seq", "ctx"), None),
        P(("seq", "ctx"), None),
    )
    out_specs = (
        P(("rep", "seq", "ctx"), None),
        P(("rep", "seq", "ctx"), None),
        P(("seq", "ctx")),
        P(("seq", "ctx"), None),
        P(),
        P(("seq", "ctx"), None),
        P(("seq", "ctx")),
        P(("seq", "ctx"), None),
        P(("seq", "ctx"), None),
        P(("seq", "ctx"), None),
    )
    return jax.shard_map(
        per_device, mesh=mesh, in_specs=in_specs, out_specs=out_specs, check_vma=False
    )
```

profile of v0, /device:TPU:0, one launch (start us, length us, event | category | flops | bytes accessed | tf_op | source)
XLA Modules:
  0.0 4382.5 jit_solution(18146430784652032975)
XLA Ops:
  8.0 22.4 all-gather
  30.7 462.0 %all-gather.10.cloned.1.call-done = bf16[2048,6144]{1,0:T(8,128)(2,1)} async-done(((bf16[256,6144]{1,0:T(8,128)(2,1)}), bf16[2048,6144]{1,0:T(8,128)(2,1)}) %all-gather.10.cloned.1.call-update) | async-done | bytes 25165840 | tf_op jit(solution)/shard_map/all_gather | solution.py:100
  492.8 11.7 fusion.46
  516.4 20.9 all-gather.1
  545.0 10.4 all-gather.12.cloned.1.call-done
  557.7 45.0 %all-gather.14.cloned.1.call-done = bf16[1024,1024]{0,1:T(8,128)(2,1)} async-done(((bf16[256,1024]{0,1:T(8,128)(2,1)}), bf16[1024,1024]{0,1:T(8,128)(2,1)}) %all-gather.14.cloned.1.call-update) | async-done | bytes 2097168 | tf_op jit(solution)/shard_map/all_gather | solution.py:136
  602.7 12.2 fusion.56
  640.5 87.4 %all-gather.16.cloned.1.call-done = bf16[2048,2048]{1,0:T(8,128)(2,1)} async-done(((bf16[256,2048]{1,0:T(8,128)(2,1)}), bf16[2048,2048]{1,0:T(8,128)(2,1)}) %all-gather.16.cloned.1.call-update) | async-done | bytes 8388624 | tf_op jit(solution)/shard_map/all_gather | solution.py:168
  734.4 473.5 %all-gather.18.cloned.1.call-done = bf16[2048,6144]{1,0:T(8,128)(2,1)} async-done(((bf16[256,6144]{1,0:T(8,128)(2,1)}), bf16[2048,6144]{1,0:T(8,128)(2,1)}) %all-gather.18.cloned.1.call-update) | async-done | bytes 25165840 | tf_op jit(solution)/shard_map/all_gather | solution.py:178
  1207.9 14.3 fusion.57
  1222.2 468.7 %all-gather.20.cloned.1.call-done = bf16[2048,6144]{1,0:T(8,128)(2,1)} async-done(((bf16[256,6144]{1,0:T(8,128)(2,1)}), bf16[2048,6144]{1,0:T(8,128)(2,1)}) %all-gather.20.cloned.1.call-update) | async-done | bytes 25165840 | tf_op jit(solution)/shard_map/all_gather | solution.py:179
  1690.9 14.3 fusion.58
  1705.3 468.9 %all-gather.22.cloned.1.call-done = bf16[2048,6144]{1,0:T(8,128)(2,1)} async-done(((bf16[256,6144]{1,0:T(8,128)(2,1)}), bf16[2048,6144]{1,0:T(8,128)(2,1)}) %all-gather.22.cloned.1.call-update) | async-done | bytes 25165840 | tf_op jit(solution)/shard_map/all_gather | solution.py:198
  2174.1 19.1 multiply_convert_fusion
  2193.2 13.5 fusion.59
  2206.7 15.2 multiply_reduce_fusion
  2224.4 8.6 multiply_convert_fusion.3
  2234.1 14.6 fusion
  2251.1 10.1 fusion.2
  2325.4 34.5 reduce-scatter.7.cloned.1.call-done
  2359.9 12.6 convolution_convert_fusion.3
  2372.5 22.9 pad_maximum_fusion.1
  2396.6 13.9 convolution_convert_fusion.1
  2410.5 14.0 convolution_convert_fusion.2
  2424.5 14.2 convolution_convert_fusion
  2438.7 50.8 %pad_maximum_fusion = bf16[2048,18432]{1,0:T(8,128)(2,1)} fusion(bf16[2048,6144]{1,0:T(8,128)(2,1)} %convolution_convert_fusion, bf16[2048,6144]{1,0:T(8,128)(2,1)} %convolution_convert_fusion.1, bf16[2048,6144]{1,0:T(8,128)(2,1)} %convolution_convert_fusion.2), kind=kLoop, calls=%fused_computation | loop fusion | flops 226492416 | bytes 150994944 | tf_op jit(solution)/shard_map/concatenate | solution.py:225
  2489.5 448.2 %reduce-scatter.9.cloned.1.call-done = bf16[256,8192]{1,0:T(8,128)(2,1)} async-done(((bf16[2048,8192]{1,0:T(8,128)(2,1)}), bf16[256,8192]{1,0:T(8,128)(2,1)}) %reduce-scatter.9.cloned.1.call-update) | async-done | bytes 4194320 | tf_op jit(solution)/shard_map/reduce_scatter | solution.py:320
  2937.7 1180.7 %reduce-scatter.11.cloned.1.call-done = bf16[256,18432]{1,0:T(8,128)(2,1)} async-done(((bf16[2048,18432]{1,0:T(8,128)(2,1)}), bf16[256,18432]{1,0:T(8,128)(2,1)}) %reduce-scatter.11.cloned.1.call-update) | async-done | bytes 9437200 | tf_op jit(solution)/shard_map/reduce_scatter | solution.py:224
  4120.0 15.0 fusion.10
  4135.1 14.9 fusion.17
  4150.0 40.8 all-reduce
  4195.1 164.5 %all-reduce.4.cloned.1.call-done = (bf16[256,8192]{1,0:T(8,128)(2,1)}, bf16[256,18432]{1,0:T(8,128)(2,1)}) async-done(((bf16[256,8192]{1,0:T(8,128)(2,1)}, bf16[256,18432]{1,0:T(8,128)(2,1)}), (bf16[256,8192]{1,0:T(8,128)(2,1)}, bf16[256,18432]{1,0:T(8,128)(2,1)})) %all-reduce.4.cloned.1.call-update) | async-done | bytes 13631504 | tf_op jit(solution)/shard_map/psum | solution.py:69
  (229 shorter events, 147.2 us)
Async XLA Ops:
  7.2 23.2 copy-start.16
  7.2 485.6 %all-gather.10.cloned.1.call-start = ((), (), s32[]{:S(2)}) async-start(), calls=%async_computation.4 | async-start | bytes 28311552 | tf_op jit(solution)/shard_map/all_gather | solution.py:100
  7.9 547.5 %all-gather.12.cloned.1.call-start = ((), (), s32[]{:S(2)}) async-start(), calls=%async_computation.5 | async-start | bytes 2621440 | tf_op jit(solution)/shard_map/all_gather | solution.py:137
  30.4 474.1 %copy-start.36 = (f32[8,1,256]{2,1,0:T(1,128)}, f32[8,1,256]{2,1,0:T(1,128)S(1)}, u32[]{:S(2)}) copy-start(f32[8,1,256]{2,1,0:T(1,128)S(1)} %convert_element_type.136) | copy-start | bytes 24580
  30.7 473.8 %copy-start.38 = (f32[256]{0:T(256)}, f32[256]{0:T(256)S(1)}, u32[]{:S(2)}) copy-start(f32[256]{0:T(256)S(1)} %add_rsqrt_fusion.3) | copy-start | bytes 3076
  508.1 94.6 %all-gather.14.cloned.1.call-start = ((), (), s32[]{:S(2)}) async-start(), calls=%async_computation.6 | async-start | bytes 2621440 | tf_op jit(solution)/shard_map/all_gather | solution.py:136
  508.2 32.9 copy-start.49
  508.8 33.9 copy-start.27
  508.8 33.9 copy-start.29
  513.8 214.1 %all-gather.16.cloned.1.call-start = ((), (), s32[]{:S(2)}) async-start(), calls=%async_computation.7 | async-start | bytes 9437184 | tf_op jit(solution)/shard_map/all_gather | solution.py:168
  514.4 693.5 %all-gather.18.cloned.1.call-start = ((), (), s32[]{:S(2)}) async-start(), calls=%async_computation.8 | async-start | bytes 28311552 | tf_op jit(solution)/shard_map/all_gather | solution.py:178
  515.0 22.3 copy-start.52
  515.0 22.4 copy-start.53
  515.0 1175.9 %all-gather.20.cloned.1.call-start = ((), (), s32[]{:S(2)}) async-start(), calls=%async_computation.9 | async-start | bytes 28311552 | tf_op jit(solution)/shard_map/all_gather | solution.py:179
  515.6 1658.5 %all-gather.22.cloned.1.call-start = ((), (), s32[]{:S(2)}) async-start(), calls=%async_computation.10 | async-start | bytes 28311552 | tf_op jit(solution)/shard_map/all_gather | solution.py:198
  516.3 1797.7 %reduce-scatter.5.cloned.1.call-start = ((), (), s32[]{:S(2)}) async-start(), calls=%async_computation.11 | async-start | bytes 2621440 | tf_op jit(solution)/shard_map/reduce_scatter | solution.py:276
  543.7 59.0 %copy-start.14 = (bf16[256,16,64]{2,0,1:T(8,128)(2,1)}, bf16[256,16,64]{2,0,1:T(8,128)(2,1)S(1)}, u32[]{:S(2)}) copy-start(bf16[256,16,64]{2,0,1:T(8,128)(2,1)S(1)} %copy.80) | copy-start | bytes 1572868
  557.7 73.0 %copy-start.7 = (bf16[128,8,8,128]{3,2,1,0:T(8,128)(2,1)}, bf16[128,8,8,128]{3,2,1,0:T(8,128)(2,1)S(1)}, u32[]{:S(2)}) copy-start(bf16[128,8,8,128]{3,2,1,0:T(8,128)(2,1)S(1)} %copy.123) | copy-start | bytes 6291460
  636.6 91.3 %copy-start.17 = (bf16[256,2048]{1,0:T(8,128)(2,1)S(1)}, bf16[256,2048]{1,0:T(8,128)(2,1)}, u32[]{:S(2)}) copy-start(bf16[256,2048]{1,0:T(8,128)(2,1)} %param.12) | copy-start | bytes 3145732
  734.1 1487.8 %copy-start.19 = (f32[256,2048]{1,0:T(8,128)}, f32[256,2048]{1,0:T(8,128)S(1)}, u32[]{:S(2)}) copy-start(f32[256,2048]{1,0:T(8,128)S(1)} %get-tuple-element.54) | copy-start | bytes 6291460
  734.4 956.6 %copy-start.11 = (bf16[256,2048]{1,0:T(8,128)(2,1)}, bf16[256,2048]{1,0:T(8,128)(2,1)S(1)}, u32[]{:S(2)}) copy-start(bf16[256,2048]{1,0:T(8,128)(2,1)S(1)} %multiply_convert_fusion.5) | copy-start | bytes 3145732
  2234.1 17.1 slice-start.3
  2269.0 90.8 %reduce-scatter.7.cloned.1.call-start = ((), (), s32[]{:S(2)}) async-start(), calls=%async_computation.12 | async-start | bytes 2621440 | tf_op jit(solution)/shard_map/reduce_scatter | solution.py:282
  2281.9 655.8 %reduce-scatter.9.cloned.1.call-start = ((), (), s32[]{:S(2)}) async-start(), calls=%async_computation.13 | async-start | bytes 37748736 | tf_op jit(solution)/shard_map/reduce_scatter | solution.py:320
  2303.4 56.5 %copy-start.25 = (bf16[256,2048]{1,0:T(8,128)(2,1)}, bf16[256,2048]{1,0:T(8,128)(2,1)S(1)}, u32[]{:S(2)}) copy-start(bf16[256,2048]{1,0:T(8,128)(2,1)S(1)} %get-tuple-element.27) | copy-start | bytes 3145732
  2322.3 37.6 copy-start.18
  2322.3 37.6 copy-start.37
  2322.3 37.6 copy-start.39
  2325.3 47.1 %copy-start.31 = (bf16[256,1024]{1,0:T(8,128)(2,1)}, bf16[256,1024]{1,0:T(8,128)(2,1)S(1)}, u32[]{:S(2)}) copy-start(bf16[256,1024]{1,0:T(8,128)(2,1)S(1)} %get-tuple-element.32) | copy-start | bytes 1572868
  2395.4 1723.1 %reduce-scatter.11.cloned.1.call-start = ((), (), s32[]{:S(2)}) async-start(), calls=%async_computation.14 | async-start | bytes 84934656 | tf_op jit(solution)/shard_map/reduce_scatter | solution.py:224
  2489.5 1870.2 %all-reduce.4.cloned.1.call-start = ((), (), s32[]{:S(2)}) async-start(), calls=%async_computation.15 | async-start | bytes 27262976 | tf_op jit(solution)/shard_map/psum | solution.py:69
  4135.1 56.9 %copy-start.6 = (f32[256,2048]{1,0:T(8,128)S(1)}, f32[256,2048]{1,0:T(8,128)}, u32[]{:S(2)}) copy-start(f32[256,2048]{1,0:T(8,128)} %copy-done.4) | copy-start | bytes 6291460
  (41 other events, 264.6 us)
Sparse Core Ops, SparseCore 0:
  9.6 483.1 all-gather.9
  508.2 47.1 all-gather.11
  557.6 45.0 all-gather.13
  604.7 123.1 all-gather.15
  729.3 478.5 all-gather.17
  1209.3 481.6 all-gather.19
  1692.5 481.6 all-gather.21
  2269.1 44.8 reduce-scatter.4
  2316.5 43.3 reduce-scatter.6
  2395.5 542.1 reduce-scatter.8
  2941.6 1176.8 reduce-scatter.10
  4121.1 238.5 all-reduce.3
where the time goes:
time: 4390 us; the launch traced here: 4380 us
  waiting for transfers between devices  3850 us (88%)
  matrix products  243 us (6%)
  other arithmetic  130 us (3%)
  blocking collectives  84 us (2%)
  local copies, waits for them, and re-layouts  57.2 us (1%)
    reduce_scatter x1, waiting for transfers between devices, per_device(): lax.psum_scatter(jnp.concatenate([lax.dot_general(normed_rows, d_gate_low...  1180 us
    all_gather x1, waiting for transfers between devices, per_device(): gate_piece = lax.all_gather(gate_weight, ('seq', 'ctx'), axis=0, tiled=True)  474 us
    all_gather x1, waiting for transfers between devices, per_device(): lax.all_gather(down_weight, ('seq', 'ctx'), axis=0, tiled=True)  469 us
    all_gather x1, waiting for transfers between devices, per_device(): up_piece = lax.all_gather(up_weight, ('seq', 'ctx'), axis=0, tiled=True)  469 us
    all_gather x1, waiting for transfers between devices, per_device(): lax.all_gather(projection_weight, ('seq', 'ctx'), axis=0, tiled=True)  462 us
    reduce_scatter x1, waiting for transfers between devices, per_device(): lax.psum_scatter(jnp.concatenate([lax.dot_general(normed_rows, d_proj_low...  448 us
    psum x1, waiting for transfers between devices, over_replicas(): lax.psum(grad_parts[1].astype(jnp.bfloat16), 'rep').astype(jnp.float32)  165 us
  transfers between devices with their start and end apart: 12, of which 12 were waited for; matrix products, arithmetic and copies ran while one was open for 6% of the time, Pallas kernels for 0%

commit v1 on v0

v1 whole, which is shorter than its diff:
```python
import functools

import jax
import jax.numpy as jnp
from jax import lax
from jax.experimental import pallas as pl
from jax.experimental.pallas import tpu as pltpu
from jax.sharding import Mesh
from jax.sharding import PartitionSpec as P

QUERY_HEADS = 16
KEY_VALUE_HEADS = 8
HEAD_SIZE = 128

norm_epsilon = 1e-06
rope_base = 1000000.0
masked_value = -1e30
contract_rows = (((0,), (0,)), ((), ()))
contract_cols = (((1,), (1,)), ((), ()))

MESH = pl.DeviceIdType.MESH
VMEM_LIMIT = 48 * 1024 * 1024

PLANE = ("row", "core", "seq")
EVERY = ("far", "row", "core", "seq", "ctx")


def rotate(value_rows, cosine_table, sine_table):
    half_size = value_rows.shape[-1] // 2
    first_half = value_rows[..., :half_size]
    second_half = value_rows[..., half_size:]
    return jnp.concatenate(
        [
            first_half * cosine_table - second_half * sine_table,
            second_half * cosine_table + first_half * sine_table,
        ],
        axis=-1,
    )


def head_norm(value_rows, gain):
    root_factor = lax.rsqrt(
        jnp.mean(value_rows * value_rows, axis=-1, keepdims=True) + norm_epsilon
    )
    unit_values = value_rows * root_factor
    return (unit_values * gain, unit_values, root_factor)


def norm_back(grad_out, unit_values, root_factor, gain):
    scaled = grad_out * gain
    return root_factor * (
        scaled - unit_values * jnp.mean(scaled * unit_values, axis=-1, keepdims=True)
    )


def place():
    return tuple(lax.axis_index(name) for name in EVERY)


def plane_neighbours():
    far, row, core, seq, ctx = place()
    return {
        "c": (far, row, 1 - core, seq, ctx),
        "x": (far, row, core, 1 - seq, ctx),
        "y": (far, 1 - row, core, seq, ctx),
    }


def plane_slots():
    _, row, core, seq, _ = place()

    def slot(r, c, s):
        return (r * 2 + c) * 2 + s

    return slot, row, core, seq


def greet(devices):
    barrier = pltpu.get_barrier_semaphore()
    for device in devices:
        pl.semaphore_signal(barrier, inc=1, device_id=device, device_id_type=MESH)
    pl.semaphore_wait(barrier, len(devices))


def gather_kernel(x_ref, o_ref, local_sem, send_sem, recv_sem):
    near = plane_neighbours()
    slot, row, core, seq = plane_slots()
    own = slot(row, core, seq)
    side = slot(row, core, 1 - seq)
    back = slot(1 - row, core, seq)
    diag = slot(1 - row, core, 1 - seq)
    half = o_ref.shape[0] // 2
    greet([near["c"], near["x"], near["y"]])

    def send(index, source, target, to):
        copy = pltpu.make_async_remote_copy(
            src_ref=source,
            dst_ref=target,
            send_sem=send_sem.at[index],
            recv_sem=recv_sem.at[index],
            device_id=near[to],
            device_id_type=MESH,
        )
        copy.start()
        return copy

    first = pl.ds(0, half)
    second = pl.ds(half, o_ref.shape[0] - half)
    mine = pltpu.make_async_copy(x_ref, o_ref.at[:, own], local_sem)
    to_x = send(0, x_ref, o_ref.at[:, own], "x")
    to_y = send(1, x_ref, o_ref.at[:, own], "y")
    to_c = send(2, x_ref, o_ref.at[:, own], "c")
    mine.start()
    to_x.wait_recv()
    on_y = send(3, o_ref.at[first, side], o_ref.at[first, side], "y")
    side_c = send(4, o_ref.at[:, side], o_ref.at[:, side], "c")
    to_y.wait_recv()
    on_x = send(5, o_ref.at[second, back], o_ref.at[second, back], "x")
    back_c = send(6, o_ref.at[:, back], o_ref.at[:, back], "c")
    on_y.wait_recv()
    diag_first = send(7, o_ref.at[first, diag], o_ref.at[first, diag], "c")
    on_x.wait_recv()
    diag_second = send(8, o_ref.at[second, diag], o_ref.at[second, diag], "c")
    mine.wait()
    for copy in (to_c, side_c, back_c, diag_first, diag_second):
        copy.wait_recv()
    for copy in (to_x, to_y, to_c, on_y, side_c, on_x, back_c, diag_first, diag_second):
        copy.wait_send()


def plane_gather(block):
    groups, rows, width = block.shape
    return pl.pallas_call(
        gather_kernel,
        out_shape=jax.ShapeDtypeStruct((groups, 8, rows, width), block.dtype),
        in_specs=[pl.BlockSpec(memory_space=pl.ANY)],
        out_specs=pl.BlockSpec(memory_space=pl.ANY),
        scratch_shapes=[
            pltpu.SemaphoreType.DMA,
            pltpu.SemaphoreType.DMA((9,)),
            pltpu.SemaphoreType.DMA((9,)),
        ],
        compiler_params=pltpu.CompilerParams(
            collective_id=0, has_side_effects=True, vmem_limit_bytes=VMEM_LIMIT
        ),
        name="plane_gather",
    )(block)


def scatter_kernel(
    p_ref, o_ref, mine, other, relay, arrived, load_sem, core_sem, core_recv, send_sem, recv_sem
):
    near = plane_neighbours()
    slot, row, core, seq = plane_slots()
    groups = mine.shape[1]
    half = groups // 2
    first = pl.ds(0, half)
    second = pl.ds(half, groups - half)
    greet([near["c"], near["x"], near["y"]])

    chips = ((1 - row, 1 - seq), (row, 1 - seq), (1 - row, seq), (row, seq))
    loads, exchanges = [], []
    for index, (r, s) in enumerate(chips):
        exchange = pltpu.make_async_remote_copy(
            src_ref=p_ref.at[:, slot(r, 1 - core, s)],
            dst_ref=other.at[index],
            send_sem=core_sem.at[index],
            recv_sem=core_recv.at[index],
            device_id=near["c"],
            device_id_type=MESH,
        )
        exchange.start()
        load = pltpu.make_async_copy(
            p_ref.at[:, slot(r, core, s)], mine.at[index], load_sem.at[index]
        )
        load.start()
        loads.append(load)
        exchanges.append(exchange)

    def chip_sum(index):
        loads[index].wait()
        exchanges[index].wait_recv()

        def body(g, carry):
            total = mine[index, g].astype(jnp.float32) + other[index, g].astype(jnp.float32)
            mine[index, g] = total.astype(mine.dtype)
            return carry

        lax.fori_loop(0, groups, body, 0)

    def send(index, source, target, to):
        copy = pltpu.make_async_remote_copy(
            src_ref=source,
            dst_ref=target,
            send_sem=send_sem.at[index],
            recv_sem=recv_sem.at[index],
            device_id=near[to],
            device_id_type=MESH,
        )
        copy.start()
        return copy

    def relay_sum(index, which, start):
        def body(g, carry):
            total = mine[index, g + start].astype(jnp.float32) + relay[which, g].astype(jnp.float32)
            mine[index, g + start] = total.astype(mine.dtype)
            return carry

        lax.fori_loop(0, half, body, 0)

    chip_sum(0)
    diag_x = send(0, mine.at[0, first], relay.at[0], "x")
    diag_y = send(1, mine.at[0, second], relay.at[1], "y")
    chip_sum(1)
    plain_x = send(2, mine.at[1, first], arrived.at[0, first], "x")
    chip_sum(2)
    plain_y = send(3, mine.at[2, second], arrived.at[1, second], "y")
    diag_x.wait_recv()
    relay_sum(2, 0, 0)
    joint_y = send(4, mine.at[2, first], arrived.at[1, first], "y")
    diag_y.wait_recv()
    relay_sum(1, 1, half)
    joint_x = send(5, mine.at[1, second], arrived.at[0, second], "x")
    loads[3].wait()
    exchanges[3].wait_recv()
    plain_x.wait_recv()
    plain_y.wait_recv()
    joint_x.wait_recv()
    joint_y.wait_recv()

    def body(g, carry):
        o_ref[g] = (
            mine[3, g].astype(jnp.float32)
            + other[3, g].astype(jnp.float32)
            + arrived[0, g].astype(jnp.float32)
            + arrived[1, g].astype(jnp.float32)
        )
        return carry

    lax.fori_loop(0, groups, body, 0)
    for copy in exchanges:
        copy.wait_send()
    for copy in (diag_x, diag_y, plain_x, plain_y, joint_x, joint_y):
        copy.wait_send()


def plane_scatter(partial_sums):
    groups, _, rows, width = partial_sums.shape
    kind = partial_sums.dtype
    return pl.pallas_call(
        scatter_kernel,
        out_shape=jax.ShapeDtypeStruct((groups, rows, width), jnp.float32),
        in_specs=[pl.BlockSpec(memory_space=pl.ANY)],
        out_specs=pl.BlockSpec(memory_space=pltpu.VMEM),
        scratch_shapes=[
            pltpu.VMEM((4, groups, rows, width), kind),
            pltpu.VMEM((4, groups, rows, width), kind),
            pltpu.VMEM((2, groups // 2, rows, width), kind),
            pltpu.VMEM((2, groups, rows, width), kind),
            pltpu.SemaphoreType.DMA((4,)),
            pltpu.SemaphoreType.DMA((4,)),
            pltpu.SemaphoreType.DMA((4,)),
            pltpu.SemaphoreType.DMA((6,)),
            pltpu.SemaphoreType.DMA((6,)),
        ],
        compiler_params=pltpu.CompilerParams(
            collective_id=1, has_side_effects=True, vmem_limit_bytes=VMEM_LIMIT
        ),
        name="plane_scatter",
    )(partial_sums)


def per_device(
    tokens,
    cotangent,
    document_index,
    padding_token_mask,
    attention_gain,
    projection_weight,
    head_gain,
    out_weight,
    feedforward_gain,
    gate_weight,
    up_weight,
    down_weight,
):
    far, row, core, seq, ctx = place()
    token_rows, model_width = tokens.shape
    sequence_length = document_index.shape[0]
    planes = lax.axis_size("ctx")
    seqs = lax.axis_size("seq")
    plane_size = lax.axis_size(PLANE)
    plane_rank = (row * 2 + core) * seqs + seq
    held = plane_size // planes
    chunk = token_rows // plane_size
    groups = held * planes
    plane_tokens = held * sequence_length
    shard_rows = projection_weight.shape[0]
    ff_part = gate_weight.shape[1] // plane_size
    heads = QUERY_HEADS // plane_size
    query_part = heads * HEAD_SIZE
    query_total = QUERY_HEADS * HEAD_SIZE
    key_total = KEY_VALUE_HEADS * HEAD_SIZE
    score_scale = HEAD_SIZE ** (-0.5)
    f32 = jnp.float32
    bf16 = jnp.bfloat16

    def to_inner(values):
        return (
            values.reshape(values.shape[0], seqs, planes, shard_rows)
            .transpose(0, 2, 1, 3)
            .reshape(values.shape)
        )

    def to_outer(values):
        return (
            values.reshape(values.shape[0], planes, seqs, shard_rows)
            .transpose(0, 2, 1, 3)
            .reshape(values.shape)
        )

    def to_plane(values):
        parts = lax.all_to_all(
            values.reshape(plane_size, chunk, model_width), PLANE, 0, 0, tiled=True
        )
        parts = lax.all_to_all(parts, "ctx", 0, 0, tiled=True)
        return (
            parts.reshape(planes, held, chunk, model_width)
            .transpose(1, 0, 2, 3)
            .reshape(groups, chunk, model_width)
        )

    def from_plane(values):
        parts = values.reshape(held, planes, chunk, model_width).transpose(1, 0, 2, 3)
        parts = lax.all_to_all(
            parts.reshape(plane_size, chunk, model_width), "ctx", 0, 0, tiled=True
        )
        parts = lax.all_to_all(parts, PLANE, 0, 0, tiled=True)
        return parts.reshape(token_rows, model_width)

    def gathered(block):
        return plane_gather(block).reshape(plane_tokens, model_width)

    def scattered(partial_rows):
        return plane_scatter(
            partial_rows.astype(bf16).reshape(groups, plane_size, chunk, model_width)
        )

    def columns_of(rank, weight, width, start):
        return lax.dynamic_slice_in_dim(weight, start + rank * width, width, 1)

    def proj_columns(rank):
        return jnp.concatenate(
            [
                columns_of(rank, projection_weight, query_part, 0),
                columns_of(rank, projection_weight, query_part, query_total),
                columns_of(rank, projection_weight, HEAD_SIZE, 2 * query_total),
                columns_of(rank, projection_weight, HEAD_SIZE, 2 * query_total + key_total),
            ],
            axis=1,
        )

    def out_columns(rank):
        return columns_of(rank, out_weight, query_part, 0)

    def up_columns(rank):
        return jnp.concatenate(
            [
                columns_of(rank, gate_weight, ff_part, 0),
                columns_of(rank, up_weight, ff_part, 0),
            ],
            axis=1,
        )

    def down_columns(rank):
        return columns_of(rank, down_weight, ff_part, 0)

    def whole_columns(piece_of):
        base = (row * 2 + core) * seqs
        both = jnp.stack([piece_of(base + other) for other in range(2)])
        swapped = lax.all_to_all(both, "seq", 0, 0, tiled=True)
        piece = swapped.reshape(seqs * shard_rows, swapped.shape[-1])
        return lax.all_gather(piece, "ctx", axis=0, tiled=True)

    proj_w = whole_columns(proj_columns)
    out_w = whole_columns(out_columns)
    up_w = whole_columns(up_columns)
    down_w = whole_columns(down_columns)

    gain_attn = lax.all_gather(attention_gain, ("ctx", "seq"), axis=0, tiled=True).astype(f32)
    gain_mlp = lax.all_gather(feedforward_gain, ("ctx", "seq"), axis=0, tiled=True).astype(f32)
    layout = lax.all_gather(
        jnp.stack([document_index, padding_token_mask]), PLANE, axis=0, tiled=False
    )
    layout = lax.dynamic_slice_in_dim(layout, ctx * held, held, 0)
    document = layout[:, 0]
    real = layout[:, 1]

    tokens_wide = to_plane(to_inner(tokens)).astype(f32)
    seq_pos = ctx * token_rows
    pad_here = lax.dynamic_slice_in_dim(padding_token_mask, seq_pos, token_rows, 0)
    grad_here = (cotangent.astype(f32) * pad_here.astype(f32)[:, None]).astype(bf16)
    own_grad = to_plane(to_inner(grad_here))

    root_attn = lax.rsqrt(jnp.mean(tokens_wide * tokens_wide, axis=2, keepdims=True) + norm_epsilon)
    unit_attn = tokens_wide * root_attn
    normed_attn = gathered((unit_attn * gain_attn).astype(bf16))
    grad_low = gathered(own_grad)

    projected = jnp.dot(normed_attn, proj_w, preferred_element_type=f32)
    queries_raw = projected[:, :query_part].reshape(held, sequence_length, heads, HEAD_SIZE)
    gate_logits = projected[:, query_part : 2 * query_part]
    keys_raw = projected[:, 2 * query_part : 2 * query_part + HEAD_SIZE].reshape(
        held, sequence_length, HEAD_SIZE
    )
    values_low = (
        projected[:, 2 * query_part + HEAD_SIZE :]
        .astype(bf16)
        .reshape(held, sequence_length, HEAD_SIZE)
    )
    half_size = HEAD_SIZE // 2
    frequency = rope_base ** (-2.0 * jnp.arange(half_size, dtype=f32) / HEAD_SIZE)
    angles = jnp.arange(sequence_length, dtype=jnp.int32).astype(f32)[:, None] * frequency[None, :]
    cosine = jnp.cos(angles)
    sine = jnp.sin(angles)
    head_gain_wide = head_gain.astype(f32)
    query_normed, query_unit, query_root = head_norm(queries_raw, head_gain_wide[0])
    key_normed, key_unit, key_root = head_norm(keys_raw, head_gain_wide[1])
    query_low = rotate(query_normed, cosine[None, :, None], sine[None, :, None]).astype(bf16)
    key_low = rotate(key_normed, cosine[None], sine[None]).astype(bf16)

    places = jnp.arange(sequence_length, dtype=jnp.int32)
    allowed = (document[:, :, None] == document[:, None, :]) & (
        places[None, None, :] <= places[None, :, None]
    ) & (real[:, None, :] == 1) | (places[None, None, :] == places[None, :, None])
    allowed = allowed[:, None]

    raw_scores = (
        jnp.einsum("sqgd,skd->sgqk", query_low, key_low, preferred_element_type=f32) * score_scale
    )
    scores = jnp.where(allowed, raw_scores, masked_value)
    peak = jnp.max(scores, axis=3, keepdims=True)
    exp_scores = jnp.exp(scores - peak)
    denominator = jnp.sum(exp_scores, axis=3, keepdims=True)
    log_total = peak + jnp.log(denominator)
    probs_low = (exp_scores / denominator).astype(bf16)
    attended = jnp.einsum("sgqk,skd->sqgd", probs_low, values_low, preferred_element_type=f32)
    attended = attended.reshape(plane_tokens, query_part)
    gate_act = jax.nn.sigmoid(gate_logits)
    mixed = (attended * gate_act).astype(bf16)
    resid_mid = tokens_wide + scattered(
        lax.dot_general(mixed, out_w, contract_cols, preferred_element_type=f32)
    )
    root_mlp = lax.rsqrt(jnp.mean(resid_mid * resid_mid, axis=2, keepdims=True) + norm_epsilon)
    unit_mlp = resid_mid * root_mlp
    normed_mlp = gathered((unit_mlp * gain_mlp).astype(bf16))
    both_lin = jnp.dot(normed_mlp, up_w, preferred_element_type=f32)
    gate_lin = both_lin[:, :ff_part]
    up_lin = both_lin[:, ff_part:]
    gate_sig = jax.nn.sigmoid(gate_lin)
    silu_gate = gate_lin * gate_sig
    hidden = (silu_gate * up_lin).astype(bf16)
    layer_own = (
        resid_mid
        + scattered(lax.dot_general(hidden, down_w, contract_cols, preferred_element_type=f32))
    ).astype(bf16)
    layer_out = to_outer(from_plane(layer_own))

    def grads_to_rows(grads):
        rows = lax.psum_scatter(grads.astype(bf16), "ctx", scatter_dimension=0, tiled=True)
        if lax.axis_size("far") > 1:
            rows = lax.psum(rows, "far")
        rows = rows.reshape(seqs, shard_rows, grads.shape[1])
        rows = lax.all_to_all(rows, "seq", 0, 0, tiled=True)
        rows = lax.all_gather(rows, ("row", "core"), axis=0, tiled=True)
        return rows

    def row_major(parts):
        return parts.transpose(1, 0, 2).reshape(shard_rows, -1).astype(f32)

    d_hidden = jnp.dot(grad_low, down_w, preferred_element_type=f32)
    d_gate = (d_hidden * up_lin * gate_sig * (1.0 + gate_lin * (1.0 - gate_sig))).astype(bf16)
    d_up = (d_hidden * silu_gate).astype(bf16)
    d_both = jnp.concatenate([d_gate, d_up], axis=1)
    down_rows = grads_to_rows(
        lax.dot_general(grad_low, hidden, contract_rows, preferred_element_type=f32)
    )
    d_normed_mlp = scattered(
        lax.dot_general(d_both, up_w, contract_cols, preferred_element_type=f32)
    )
    up_rows = grads_to_rows(
        lax.dot_general(normed_mlp, d_both, contract_rows, preferred_element_type=f32)
    )
    gain_mlp_term = jnp.sum(d_normed_mlp * unit_mlp, axis=(0, 1))
    d_resid = own_grad.astype(f32) + norm_back(d_normed_mlp, unit_mlp, root_mlp, gain_mlp)
    d_attn_low = gathered(d_resid.astype(bf16))
    mixed_grad = jnp.dot(d_attn_low, out_w, preferred_element_type=f32)
    out_rows = grads_to_rows(
        lax.dot_general(d_attn_low, mixed, contract_rows, preferred_element_type=f32)
    )
    d_gate_logits = mixed_grad * attended * gate_act * (1.0 - gate_act)
    d_attended = (
        (mixed_grad * gate_act).astype(bf16).reshape(held, sequence_length, heads, HEAD_SIZE)
    )
    probs = jnp.exp(scores - log_total)
    d_probs = jnp.einsum("sqgd,skd->sgqk", d_attended, values_low, preferred_element_type=f32)
    d_values = jnp.einsum("sgqk,sqgd->skd", probs_low, d_attended, preferred_element_type=f32)
    delta = jnp.sum(probs * d_probs, axis=3, keepdims=True)
    d_scores = (probs * (d_probs - delta)).astype(bf16)
    d_queries = (
        jnp.einsum("sgqk,skd->sqgd", d_scores, key_low, preferred_element_type=f32) * score_scale
    )
    d_keys = (
        jnp.einsum("sgqk,sqgd->skd", d_scores, query_low, preferred_element_type=f32) * score_scale
    )
    d_query_normed = rotate(d_queries, cosine[None, :, None], -sine[None, :, None])
    d_key_normed = rotate(d_keys, cosine[None], -sine[None])
    head_term = jnp.stack(
        [
            jnp.sum(d_query_normed * query_unit, axis=(0, 1, 2)),
            jnp.sum(d_key_normed * key_unit, axis=(0, 1)),
        ]
    )
    d_query_raw = norm_back(d_query_normed, query_unit, query_root, head_gain_wide[0])
    d_key_raw = norm_back(d_key_normed, key_unit, key_root, head_gain_wide[1])
    d_proj = jnp.concatenate(
        [
            d_query_raw.reshape(plane_tokens, query_part),
            d_gate_logits,
            d_key_raw.reshape(plane_tokens, HEAD_SIZE),
            d_values.reshape(plane_tokens, HEAD_SIZE),
        ],
        axis=1,
    ).astype(bf16)
    proj_rows = grads_to_rows(
        lax.dot_general(normed_attn, d_proj, contract_rows, preferred_element_type=f32)
    )
    d_normed_attn = scattered(
        lax.dot_general(d_proj, proj_w, contract_cols, preferred_element_type=f32)
    )
    gain_attn_term = jnp.sum(d_normed_attn * unit_attn, axis=(0, 1))
    tokens_grad = to_outer(
        from_plane(
            (d_resid + norm_back(d_normed_attn, unit_attn, root_attn, gain_attn)).astype(bf16)
        )
    )
    sum_attn, sum_mlp, sum_head = lax.psum((gain_attn_term, gain_mlp_term, head_term), EVERY)
    own_rows = (ctx * seqs + seq) * shard_rows
    attention_gain_grad = lax.dynamic_slice_in_dim(sum_attn, own_rows, shard_rows, 0)
    feedforward_gain_grad = lax.dynamic_slice_in_dim(sum_mlp, own_rows, shard_rows, 0)
    cuts = (0, query_part, 2 * query_part, 2 * query_part + HEAD_SIZE, 2 * (query_part + HEAD_SIZE))
    proj_weight_grad = jnp.concatenate(
        [row_major(proj_rows[:, :, a:b]) for a, b in zip(cuts[:-1], cuts[1:])], axis=1
    )
    return (
        layer_out,
        tokens_grad,
        attention_gain_grad,
        proj_weight_grad,
        sum_head,
        row_major(out_rows),
        feedforward_gain_grad,
        row_major(up_rows[:, :, :ff_part]),
        row_major(up_rows[:, :, ff_part:]),
        row_major(down_rows),
    )


def solution(mesh):
    rep, seqs, ctxs = (mesh.shape[name] for name in ("rep", "seq", "ctx"))
    inner = Mesh(mesh.devices.reshape(rep // 4, 2, 2, seqs, ctxs), EVERY)
    token_axes = ("far", "row", "core", "seq", "ctx")
    sequence_axes = ("far", "row", "core", "seq")
    in_specs = (
        P(token_axes, None),
        P(token_axes, None),
        P(sequence_axes),
        P(sequence_axes),
        P(("seq", "ctx")),
        P(("seq", "ctx"), None),
        P(),
        P(("seq", "ctx"), None),
        P(("seq", "ctx")),
        P(("seq", "ctx"), None),
        P(("seq", "ctx"), None),
        P(("seq", "ctx"), None),
    )
    out_specs = (
        P(token_axes, None),
        P(token_axes, None),
        P(("seq", "ctx")),
        P(("seq", "ctx"), None),
        P(),
        P(("seq", "ctx"), None),
        P(("seq", "ctx")),
        P(("seq", "ctx"), None),
        P(("seq", "ctx"), None),
        P(("seq", "ctx"), None),
    )
    return jax.shard_map(
        per_device, mesh=inner, in_specs=in_specs, out_specs=out_specs, check_vma=False
    )
```

time: 4390 us -> 1280 us (0.29)
  waiting for transfers between devices: 3850 us -> 198 us
  Pallas kernels: 0 us -> 360 us
  blocking collectives: 84 us -> 282 us
  matrix products: 243 us -> 185 us
  local copies, waits for them, and re-layouts: 57.2 us -> 110 us
  other arithmetic: 130 us -> 84.7 us
    all_gather x7 -> x8, waiting for transfers between devices: 2020 us -> 0.05 us  [the longest x4 0.05 us: whole_columns(): return lax.all_gather(piece, 'ctx', axis=0, tiled=True)]
    reduce_scatter x4, waiting for transfers between devices: 1670 us -> 114 us  [grads_to_rows(): lax.psum_scatter(grads.astype(bf16), 'ctx', scatter_dimension=0, tiled=True)]
    pallas_call x0 -> x8, Pallas kernels: none -> 360 us  [the longest x4 198 us: plane_scatter(): pl.pallas_call(scatter_kernel, out_shape=jax.ShapeDtypeStruct((groups, ro...]
    psum x1 -> x0, waiting for transfers between devices: 165 us -> none  [over_replicas(): lax.psum(grad_parts[1].astype(jnp.bfloat16), 'rep').astype(jnp.float32)]
    all_to_all x0 -> x8, blocking collectives: none -> 142 us  [the longest x3 40.6 us: grads_to_rows(): rows = lax.all_to_all(rows, 'seq', 0, 0, tiled=True)]
    all_to_all x0 -> x8, waiting for transfers between devices: none -> 84.6 us  [the longest x2 37.8 us: to_plane(): parts = lax.all_to_all(parts, 'ctx', 0, 0, tiled=True)]
    concatenate x3 -> x1, other arithmetic: 73.9 us -> 9.26 us  [per_device(): jnp.concatenate([row_major(proj_rows[:, :, a:b]) for a, b in zip(cuts[:-1...]
    dot_general x21 -> x18, matrix products: 243 us -> 185 us  [the longest x1 19.2 us: per_device(): lax.dot_general(d_both, up_w, contract_cols, preferred_element_type=f32)]
  transfers between devices with their start and end apart: 12 -> 20, of which waited for: 12 -> 7; matrix products, arithmetic and copies ran while one was open for 6% -> 22% of each run, Pallas kernels for 0% -> 22%
where the time goes in v1:
time: 1280 us; the launch traced here: 1270 us
  Pallas kernels  360 us (28%)
  blocking collectives  282 us (22%)
  waiting for transfers between devices  198 us (15%)
  matrix products  185 us (14%)
  local copies, waits for them, and re-layouts  110 us (9%)
  other arithmetic  84.7 us (7%)
  starting transfers between devices  37.2 us (3%)
  between operations  16.1 us (1%)
    pallas_call x4, Pallas kernels, plane_scatter(): pl.pallas_call(scatter_kernel, out_shape=jax.ShapeDtypeStruct((groups, ro...  198 us
    pallas_call x4, Pallas kernels, plane_gather(): pl.pallas_call(gather_kernel, out_shape=jax.ShapeDtypeStruct((groups, 8,...  163 us
    reduce_scatter x4, waiting for transfers between devices, grads_to_rows(): lax.psum_scatter(grads.astype(bf16), 'ctx', scatter_dimension=0, tiled=True)  114 us
    unnamed x164, local copies, waits for them, and re-layouts  54 us
    psum x1, blocking collectives, per_device(): lax.psum((gain_attn_term, gain_mlp_term, head_term), EVERY)  47 us
    all_to_all x3, blocking collectives, grads_to_rows(): rows = lax.all_to_all(rows, 'seq', 0, 0, tiled=True)  40.6 us
    all_gather x1, blocking collectives, per_device(): lax.all_gather(attention_gain, ('ctx', 'seq'), axis=0, tiled=True)  40.3 us
    all_to_all x2, waiting for transfers between devices, to_plane(): parts = lax.all_to_all(parts, 'ctx', 0, 0, tiled=True)  37.8 us
  transfers between devices with their start and end apart: 20, of which 7 were waited for; matrix products, arithmetic and copies ran while one was open for 22% of the time, Pallas kernels for 22%

profile of v1, /device:TPU:0, one launch (start us, length us, event | category | flops | bytes accessed | tf_op | source)
XLA Modules:
  0.0 1273.4 jit_solution(17159409582779834796)
XLA Ops:
  9.5 15.5 %all_to_all.80 = bf16[2,256,768]{2,1,0:T(8,128)(2,1)} all-to-all(bf16[2,256,768]{2,1,0:T(8,128)(2,1)S(1)} %pad_maximum_fusion.8), channel_id=1, replica_groups=mesh['far'=1,'row'=2,'core'=2,'seq'=2,'ctx'=4] {'seq'}, dimensions={0} | all-to-all | bytes 1572864 | tf_op jit(solution)/shard_map/all_to_all | solution.py:381
  37.9 21.3 %all_to_all.81 = bf16[2,256,1536]{2,1,0:T(8,128)(2,1)} all-to-all(bf16[2,256,1536]{2,1,0:T(8,128)(2,1)S(1)} %pad_maximum_fusion.5), channel_id=1, replica_groups=mesh['far'=1,'row'=2,'core'=2,'seq'=2,'ctx'=4] {'seq'}, dimensions={0} | all-to-all | bytes 3145728 | tf_op jit(solution)/shard_map/all_to_all | solution.py:381
  92.7 18.0 %all_to_all.82 = bf16[8,32,2048]{2,1,0:T(8,128)(2,1)} all-to-all(bf16[8,32,2048]{2,1,0:T(8,128)(2,1)S(1)} %reshape_reshape.12), channel_id=1, replica_groups=mesh['far'=1,'row'=2,'core'=2,'seq'=2,'ctx'=4] {'row','core','seq'}, dimensions={0} | all-to-all | bytes 2097152 | tf_op jit(solution)/shard_map/all_to_all | solution.py:323
  115.1 37.0 %all-gather.3 = bf16[8,1,256]{2,1,0:T(2,128)(2,1)S(1)} all-gather(bf16[1,1,256]{2,1,0:T(2,128)(2,1)S(1)} %reshape.516), channel_id=1, replica_groups=mesh['far'=1,'row'=2,'core'=2,'seq'=2,'ctx'=4] {'ctx','seq'}, dimensions={0}, use_global_device_ids=true | all-gather | bytes 4608 | tf_op jit(solution)/shard_map/all_gather | solution.py:391
  152.1 40.3 %all-gather.1 = bf16[8,1,256]{2,1,0:T(2,128)(2,1)S(1)} all-gather(bf16[1,1,256]{2,1,0:T(2,128)(2,1)S(1)} %reshape.512), channel_id=1, replica_groups=mesh['far'=1,'row'=2,'core'=2,'seq'=2,'ctx'=4] {'ctx','seq'}, dimensions={0}, use_global_device_ids=true | all-gather | bytes 4608 | tf_op jit(solution)/shard_map/all_gather | solution.py:390
  192.5 15.7 %all-gather.2 = s32[8,2,1024]{2,1,0:T(2,128)S(1)} all-gather(s32[1,2,1024]{2,1,0:T(2,128)S(1)} %add_bitcast_fusion), channel_id=2, replica_groups=mesh['far'=1,'row'=2,'core'=2,'seq'=2,'ctx'=4] {'row','core','seq'}, dimensions={0}, use_global_device_ids=true | all-gather | bytes 73728 | tf_op jit(solution)/shard_map/all_gather | solution.py:392
  225.8 37.8 %all-to-all-done.1 = bf16[8,32,2048]{2,1,0:T(8,128)(2,1)} async-done(((bf16[8,32,2048]{2,1,0:T(8,128)(2,1)}), bf16[8,32,2048]{2,1,0:T(8,128)(2,1)}, u32[]{:S(2)}, u32[]{:S(2)}) %all-to-all-start.1) | async-done | bytes 1048608 | tf_op jit(solution)/shard_map/all_to_all | solution.py:326
  268.6 40.8 %plane_gather.4 = bf16[8,8,32,2048]{3,2,1,0:T(8,128)(2,1)} custom-call(bf16[8,32,2048]{2,1,0:T(8,128)(2,1)S(1)} %get-tuple-element.81.x_ref), custom_call_target="tpu_custom_call" | custom-call | tf_op jit(solution)/shard_map/plane_gather/pallas_call | solution.py:133
  309.4 41.5 %plane_gather.6 = bf16[8,8,32,2048]{3,2,1,0:T(8,128)(2,1)} custom-call(bf16[8,32,2048]{2,1,0:T(8,128)(2,1)S(1)} %bitcast.240), custom_call_target="tpu_custom_call" | custom-call | tf_op jit(solution)/shard_map/plane_gather/pallas_call | solution.py:133
  417.7 40.5 %plane_scatter.4 = f32[8,32,2048]{2,1,0:T(8,128)S(1)} custom-call(bf16[8,8,32,2048]{3,2,1,0:T(8,128)(2,1)} %bitcast.241), custom_call_target="tpu_custom_call" | custom-call | tf_op jit(solution)/shard_map/plane_scatter/pallas_call | solution.py:250
  459.0 40.3 %plane_gather.5 = bf16[8,8,32,2048]{3,2,1,0:T(8,128)(2,1)} custom-call(bf16[8,32,2048]{2,1,0:T(8,128)(2,1)S(1)} %multiply_convert_fusion.5.x_ref), custom_call_target="tpu_custom_call" | custom-call | tf_op jit(solution)/shard_map/plane_gather/pallas_call | solution.py:133
  499.3 19.0 %fusion.37 = f32[2048,1536]{0,1:T(8,128)} fusion(bf16[2048,2048]{1,0:T(8,128)(2,1)} %bitcast.263, bf16[2048,1536]{1,0:T(8,128)(2,1)} %all-gather.17.cloned.1.call-done), kind=kOutput, calls=%fused_computation.158 | convolution fusion | flops 12884901888 | bytes 27262976 | tf_op jit(solution)/shard_map/dot_general | solution.py:457
  518.3 18.1 %multiply_convert_fusion.1 = (bf16[2048,768]{0,1:T(8,128)(2,1)}, bf16[2048,768]{0,1:T(8,128)(2,1)}, bf16[2048,768]{0,1:T(8,128)(2,1)}) fusion(f32[2048,1536]{0,1:T(8,128)} %fusion.37, bf16[2048,2048]{1,0:T(8,128)(2,1)} %bitcast.265, bf16[2048,768]{1,0:T(8,128)(2,1)} %all-gather.19.cloned.1.call-done), kind=kOutput, calls=%fused_computation.19 | convolution fusion | flops 6466043904 | bytes 33554432 | tf_op jit(solution)/shard_map/dot_general | solution.py:481
  536.4 19.2 %convolution_convert_fusion.1 = bf16[2048,2048]{1,0:T(8,128)(2,1)} fusion(bf16[2048,1536]{1,0:T(8,128)(2,1)} %all-gather.17.cloned.1.call-done, bf16[2048,768]{0,1:T(8,128)(2,1)} %get-tuple-element.84, bf16[2048,768]{0,1:T(8,128)(2,1)} %get-tuple-element.83), kind=kOutput, calls=%fused_computation.13 | convolution fusion | flops 12901679104 | bytes 20971520 | tf_op jit(solution)/shard_map/dot_general | solution.py:489
  555.6 40.7 %plane_scatter.6 = f32[8,32,2048]{2,1,0:T(8,128)S(1)} custom-call(bf16[8,8,32,2048]{3,2,1,0:T(8,128)(2,1)} %bitcast.255), custom_call_target="tpu_custom_call" | custom-call | tf_op jit(solution)/shard_map/plane_scatter/pallas_call | solution.py:250
  598.3 40.3 %plane_gather.7 = bf16[8,8,32,2048]{3,2,1,0:T(8,128)(2,1)} custom-call(bf16[8,32,2048]{2,1,0:T(8,128)(2,1)S(1)} %fusion.32.x_ref), custom_call_target="tpu_custom_call" | custom-call | tf_op jit(solution)/shard_map/plane_gather/pallas_call | solution.py:133
  655.1 11.4 convolution_convert_fusion.5
  668.2 13.0 %fusion = (f32[2,2,1024]{2,1,0:T(2,128)S(1)}, f32[2,1024,1024,2]{2,1,3,0:T(8,128)}) fusion(f32[2,1024,1024,2]{2,1,3,0:T(8,128)} %copy-done.4, f32[2,2,1024]{2,1,0:T(2,128)S(1)} %log_add_fusion, pred[2,1024,1024]{1,2,0:T(8,128)(4,1)S(1)} %copy-done.9, bf16[2,1024,128,1]{2,1,3,0:T(8,128)(2,1)S(1)} %bitcast.275, bf16[2,1024,2,128]{3,2,1,0:T(2,128)(2,1)} %reshape.490), kind=kOutput, calls=%fused_computation.2 | convolution fusion | flops 1094709248 | bytes 37257216 | tf_op jit(solution)/shard_map/sqgd,skd->sgqk/dot_general | solution.py:506
  681.3 12.6 fusion.2
  734.3 19.2 %convolution_convert_fusion.4 = bf16[2048,1536]{1,0:T(8,128)(2,1)} fusion(bf16[2048,2048]{1,0:T(8,128)(2,1)} %bitcast.264, bf16[2048,768]{0,1:T(8,128)(2,1)} %get-tuple-element.84, bf16[2048,768]{0,1:T(8,128)(2,1)} %get-tuple-element.83), kind=kOutput, calls=%fused_computation.16 | convolution fusion | flops 12900630528 | bytes 20971520 | tf_op jit(solution)/shard_map/dot_general | solution.py:492
  763.8 15.2 %all_to_all.84 = bf16[2,256,768]{2,1,0:T(8,128)(2,1)} all-to-all(bf16[2,256,768]{2,1,0:T(8,128)(2,1)} %bitcast.295), channel_id=1, replica_groups=mesh['far'=1,'row'=2,'core'=2,'seq'=2,'ctx'=4] {'seq'}, dimensions={0} | all-to-all | bytes 1572864 | tf_op jit(solution)/shard_map/all_to_all | solution.py:474
  779.0 15.1 %reduce-scatter.5.cloned.1.call-done = bf16[512,768]{1,0:T(8,128)(2,1)} async-done(((bf16[2048,768]{1,0:T(8,128)(2,1)}), bf16[512,768]{1,0:T(8,128)(2,1)}) %reduce-scatter.5.cloned.1.call-update) | async-done | bytes 786448 | tf_op jit(solution)/shard_map/reduce_scatter | solution.py:470
  794.2 15.3 %all_to_all.85 = bf16[2,256,768]{2,1,0:T(8,128)(2,1)} all-to-all(bf16[2,256,768]{2,1,0:T(8,128)(2,1)} %bitcast.296), channel_id=1, replica_groups=mesh['far'=1,'row'=2,'core'=2,'seq'=2,'ctx'=4] {'seq'}, dimensions={0} | all-to-all | bytes 1572864 | tf_op jit(solution)/shard_map/all_to_all | solution.py:474
  809.5 98.5 %reduce-scatter.9.cloned.1.call-done = bf16[512,1536]{1,0:T(8,128)(2,1)} async-done(((bf16[2048,1536]{1,0:T(8,128)(2,1)}), bf16[512,1536]{1,0:T(8,128)(2,1)}) %reduce-scatter.9.cloned.1.call-update) | async-done | bytes 1572880 | tf_op jit(solution)/shard_map/reduce_scatter | solution.py:470
  912.7 11.7 convolution_convert_fusion.2
  924.4 57.8 %plane_scatter.5 = f32[8,32,2048]{2,1,0:T(8,128)S(1)} custom-call(bf16[8,8,32,2048]{3,2,1,0:T(8,128)(2,1)} %bitcast.254), custom_call_target="tpu_custom_call" | custom-call | tf_op jit(solution)/shard_map/plane_scatter/pallas_call | solution.py:250
  982.2 11.4 convolution_convert_fusion
  993.7 58.6 %plane_scatter.7 = f32[8,32,2048]{2,1,0:T(8,128)S(1)} custom-call(bf16[8,8,32,2048]{3,2,1,0:T(8,128)(2,1)} %bitcast.253), custom_call_target="tpu_custom_call" | custom-call | tf_op jit(solution)/shard_map/plane_scatter/pallas_call | solution.py:250
  1061.1 25.9 %all-to-all-done.6 = bf16[8,32,2048]{2,1,0:T(8,128)(2,1)S(1)} async-done(((bf16[8,32,2048]{2,1,0:T(8,128)(2,1)}), bf16[8,32,2048]{2,1,0:T(8,128)(2,1)S(1)}, u32[]{:S(2)}, u32[]{:S(2)}) %all-to-all-start.6) | async-done | bytes 1048608 | tf_op jit(solution)/shard_map/all_to_all | solution.py:335
  1087.0 28.5 %all_to_all.86 = bf16[8,32,2048]{2,1,0:T(8,128)(2,1)} all-to-all(bf16[8,32,2048]{2,1,0:T(8,128)(2,1)S(1)} %bitcast.280), channel_id=1, replica_groups=mesh['far'=1,'row'=2,'core'=2,'seq'=2,'ctx'=4] {'ctx'}, dimensions={0} | all-to-all | bytes 2097152 | tf_op jit(solution)/shard_map/all_to_all | solution.py:335
  1115.5 18.0 %all_to_all.87 = bf16[8,32,2048]{2,1,0:T(8,128)(2,1)S(1)} all-to-all(bf16[8,32,2048]{2,1,0:T(8,128)(2,1)S(1)} %all-to-all-done.6), channel_id=1, replica_groups=mesh['far'=1,'row'=2,'core'=2,'seq'=2,'ctx'=4] {'row','core','seq'}, dimensions={0} | all-to-all | bytes 2097152 | tf_op jit(solution)/shard_map/all_to_all | solution.py:338
  1137.2 47.0 %all-reduce = (f32[2048]{0:T(1024)S(1)}, f32[2,128]{1,0:T(2,128)}, f32[2048]{0:T(1024)S(1)}) all-reduce(f32[2048]{0:T(1024)S(1)} %get-tuple-element.74, f32[2,128]{1,0:T(2,128)S(1)} %pad_maximum_fusion.15, f32[2048]{0:T(1024)S(1)} %copy-done.54), channel_id=1, replica_groups=mesh['far'=1,'row'=2,'core'=2,'seq'=2,'ctx'=4] {'far','row','core','seq'..., use_global_device_ids=true, to_apply=%region_12.13 | all-reduce | flops 4352 | bytes 34816 | tf_op jit(solution)/shard_map/psum | solution.py:547
  (327 shorter events, 312.3 us)
Async XLA Ops:
  7.2 343.8 %all-gather.13.cloned.1.call-start = ((), (), s32[]{:S(2)}) async-start(), calls=%async_computation.20 | async-start | bytes 3932160 | tf_op jit(solution)/shard_map/all_gather | solution.py:383
  26.7 8.6 all-to-all-start.3
  30.2 378.9 %all-gather.15.cloned.1.call-start = ((), (), s32[]{:S(2)}) async-start(), calls=%async_computation.21 | async-start | bytes 1310720 | tf_op jit(solution)/shard_map/all_gather | solution.py:383
  36.1 463.3 %all-gather.17.cloned.1.call-start = ((), (), s32[]{:S(2)}) async-start(), calls=%async_computation.22 | async-start | bytes 7864320 | tf_op jit(solution)/shard_map/all_gather | solution.py:383
  61.4 12.1 all-to-all-start.5
  73.5 19.2 %all-to-all-start.8 = ((bf16[8,32,2048]{2,1,0:T(8,128)(2,1)}), bf16[8,32,2048]{2,1,0:T(8,128)(2,1)}, u32[]{:S(2)}, u32[]{:S(2)}) async-start(bf16[8,32,2048]{2,1,0:T(8,128)(2,1)} %reshape_reshape.14), calls=%async_computation.8 | async-start | bytes 2097152 | tf_op jit(solution)/shard_map/all_to_all | solution.py:323
  80.7 111.7 %copy-start.60 = (s32[1024]{0:T(1024)S(1)}, s32[1024]{0:T(1024)}, u32[]{:S(2)}) copy-start(s32[1024]{0:T(1024)} %param.14) | copy-start | bytes 12292
  110.7 97.6 %all-to-all-start.9 = ((bf16[8,32,2048]{2,1,0:T(8,128)(2,1)}), bf16[8,32,2048]{2,1,0:T(8,128)(2,1)S(1)}, u32[]{:S(2)}, u32[]{:S(2)}) async-start(bf16[8,32,2048]{2,1,0:T(8,128)(2,1)} %all-to-all-done.8), calls=%async_computation.9 | async-start | bytes 2097152 | tf_op jit(solution)/shard_map/all_to_all | solution.py:326
  152.1 445.4 %copy-start.42 = (f32[8,1,256]{2,1,0:T(1,128)}, f32[8,1,256]{2,1,0:T(1,128)S(1)}, u32[]{:S(2)}) copy-start(f32[8,1,256]{2,1,0:T(1,128)S(1)} %convert_element_type.268) | copy-start | bytes 24580
  192.4 74.4 %copy-start.46 = (f32[8,1,256]{2,1,0:T(1,128)}, f32[8,1,256]{2,1,0:T(1,128)S(1)}, u32[]{:S(2)}) copy-start(f32[8,1,256]{2,1,0:T(1,128)S(1)} %convert_element_type.267) | copy-start | bytes 24580
  208.3 166.9 %copy-start.58 = (f32[128]{0:T(128)}, f32[128]{0:T(128)S(1)}, u32[]{:S(2)}) copy-start(f32[128]{0:T(128)S(1)} %get-tuple-element.128) | copy-start | bytes 1540
  208.3 169.2 %copy-start.55 = (f32[128]{0:T(128)}, f32[128]{0:T(128)S(1)}, u32[]{:S(2)}) copy-start(f32[128]{0:T(128)S(1)} %get-tuple-element.127) | copy-start | bytes 1540
  208.3 55.2 %all-to-all-start.1 = ((bf16[8,32,2048]{2,1,0:T(8,128)(2,1)}), bf16[8,32,2048]{2,1,0:T(8,128)(2,1)}, u32[]{:S(2)}, u32[]{:S(2)}) async-start(bf16[8,32,2048]{2,1,0:T(8,128)(2,1)} %all_to_all.82), calls=%async_computation.1 | async-start | bytes 2097152 | tf_op jit(solution)/shard_map/all_to_all | solution.py:326
  216.7 301.6 %all-gather.19.cloned.1.call-start = ((), (), s32[]{:S(2)}) async-start(), calls=%async_computation.23 | async-start | bytes 3932160 | tf_op jit(solution)/shard_map/all_gather | solution.py:383
  223.7 166.3 %copy-start.8 = (pred[2,1024,1024]{1,2,0:T(8,128)(4,1)}, pred[2,1024,1024]{1,2,0:T(8,128)(4,1)S(1)}, u32[]{:S(2)}) copy-start(pred[2,1024,1024]{1,2,0:T(8,128)(4,1)S(1)} %and_or_fusion) | copy-start | bytes 6291460
  223.7 529.8 %reduce-scatter.7.cloned.1.call-start = ((), (), s32[]{:S(2)}) async-start(), calls=%async_computation.26 | async-start | bytes 1310720 | tf_op jit(solution)/shard_map/reduce_scatter | solution.py:470
  225.8 371.8 %copy-start.2 = (bf16[2,4,32,2048]{3,2,1,0:T(8,128)(2,1)}, bf16[2,4,32,2048]{3,2,1,0:T(8,128)(2,1)S(1)}, u32[]{:S(2)}) copy-start(bf16[2,4,32,2048]{3,2,1,0:T(8,128)(2,1)S(1)} %copy.282) | copy-start | bytes 3145732
  458.5 139.0 %copy-start.5 = (f32[8,32,2048]{2,1,0:T(8,128)}, f32[8,32,2048]{2,1,0:T(8,128)S(1)}, u32[]{:S(2)}) copy-start(f32[8,32,2048]{2,1,0:T(8,128)S(1)} %bitcast_add_fusion) | copy-start | bytes 6291460
  458.7 138.8 %copy-start.48 = (f32[8,32]{1,0:T(8,128)}, f32[8,32]{1,0:T(8,128)S(1)}, u32[]{:S(2)}) copy-start(f32[8,32]{1,0:T(8,128)S(1)} %add_rsqrt_fusion.3) | copy-start | bytes 3076
  645.7 118.1 %reduce-scatter.11.cloned.1.call-start = ((), (), s32[]{:S(2)}) async-start(), calls=%async_computation.30 | async-start | bytes 3932160 | tf_op jit(solution)/shard_map/reduce_scatter | solution.py:470
  666.5 127.6 %reduce-scatter.5.cloned.1.call-start = ((), (), s32[]{:S(2)}) async-start(), calls=%async_computation.24 | async-start | bytes 3932160 | tf_op jit(solution)/shard_map/reduce_scatter | solution.py:470
  734.2 173.8 %reduce-scatter.9.cloned.1.call-start = ((), (), s32[]{:S(2)}) async-start(), calls=%async_computation.28 | async-start | bytes 7864320 | tf_op jit(solution)/shard_map/reduce_scatter | solution.py:470
  753.5 438.5 %all-gather.23.cloned.1.call-start = ((), (), s32[]{:S(2)}) async-start(), calls=%async_computation.27 | async-start | bytes 1310720 | tf_op jit(solution)/shard_map/all_gather | solution.py:475
  763.7 431.8 %all-gather.27.cloned.1.call-start = ((), (), s32[]{:S(2)}) async-start(), calls=%async_computation.31 | async-start | bytes 3932160 | tf_op jit(solution)/shard_map/all_gather | solution.py:475
  779.0 429.5 %all-gather.21.cloned.1.call-start = ((), (), s32[]{:S(2)}) async-start(), calls=%async_computation.25 | async-start | bytes 3932160 | tf_op jit(solution)/shard_map/all_gather | solution.py:475
  908.0 74.2 %all-to-all-start.14 = ((bf16[2,256,1536]{2,1,0:T(8,128)(2,1)}), bf16[2,256,1536]{2,1,0:T(8,128)(2,1)}, u32[]{:S(2)}, u32[]{:S(2)}) async-start(bf16[2,256,1536]{2,1,0:T(8,128)(2,1)} %bitcast.293), calls=%async_computation.17 | async-start | bytes 3145728 | tf_op jit(solution)/shard_map/all_to_all | solution.py:474
  912.6 317.8 %all-gather.25.cloned.1.call-start = ((), (), s32[]{:S(2)}) async-start(), calls=%async_computation.29 | async-start | bytes 7864320 | tf_op jit(solution)/shard_map/all_gather | solution.py:475
  993.7 58.7 %copy-start.14 = (f32[8,32,2048]{2,1,0:T(8,128)S(1)}, f32[8,32,2048]{2,1,0:T(8,128)}, u32[]{:S(2)}) copy-start(f32[8,32,2048]{2,1,0:T(8,128)} %get-tuple-element.82) | copy-start | bytes 6291460
  993.7 58.7 %copy-start.47 = (f32[8,1,256]{2,1,0:T(1,128)S(1)}, f32[8,1,256]{2,1,0:T(1,128)}, u32[]{:S(2)}) copy-start(f32[8,1,256]{2,1,0:T(1,128)} %copy-done.46) | copy-start | bytes 24580
  993.7 59.2 %copy-start.6 = (f32[8,32,2048]{2,1,0:T(8,128)S(1)}, f32[8,32,2048]{2,1,0:T(8,128)}, u32[]{:S(2)}) copy-start(f32[8,32,2048]{2,1,0:T(8,128)} %copy-done.5) | copy-start | bytes 6291460
  1056.4 30.6 %all-to-all-start.6 = ((bf16[8,32,2048]{2,1,0:T(8,128)(2,1)}), bf16[8,32,2048]{2,1,0:T(8,128)(2,1)S(1)}, u32[]{:S(2)}, u32[]{:S(2)}) async-start(bf16[8,32,2048]{2,1,0:T(8,128)(2,1)} %bitcast.39), calls=%async_computation.6 | async-start | bytes 2097152 | tf_op jit(solution)/shard_map/all_to_all | solution.py:335
  1133.5 55.2 %all-to-all-start.11 = ((bf16[8,32,2048]{2,1,0:T(8,128)(2,1)}), bf16[8,32,2048]{2,1,0:T(8,128)(2,1)S(1)}, u32[]{:S(2)}, u32[]{:S(2)}) async-start(bf16[8,32,2048]{2,1,0:T(8,128)(2,1)} %all_to_all.86), calls=%async_computation.11 | async-start | bytes 2097152 | tf_op jit(solution)/shard_map/all_to_all | solution.py:338
  (61 other events, 543.7 us)
Sparse Core Ops, SparseCore 0:
  25.1 64.0 all-gather.12
  90.8 26.5 all-gather.14
  119.0 146.5 all-gather.16
  267.6 61.3 all-gather.18
  645.8 24.4 reduce-scatter.6
  672.5 58.8 reduce-scatter.10
  734.3 59.7 reduce-scatter.4
  797.2 110.7 reduce-scatter.8
  909.6 17.2 all-gather.22
  928.4 46.7 all-gather.26
  976.9 32.7 all-gather.20
  1011.2 61.7 all-gather.24

commit v2 on v1

v2 whole, which is shorter than its diff:
```python
import functools

import jax
import jax.numpy as jnp
from jax import lax
from jax.experimental import pallas as pl
from jax.experimental.pallas import tpu as pltpu
from jax.sharding import Mesh
from jax.sharding import PartitionSpec as P

QUERY_HEADS = 16
KEY_VALUE_HEADS = 8
HEAD_SIZE = 128

norm_epsilon = 1e-06
rope_base = 1000000.0
masked_value = -1e30
contract_rows = (((0,), (0,)), ((), ()))
contract_cols = (((1,), (1,)), ((), ()))

MESH = pl.DeviceIdType.MESH
VMEM_LIMIT = 48 * 1024 * 1024

PLANE = ("row", "core", "seq")
EVERY = ("far", "row", "core", "seq", "ctx")


def norm_back(grad_out, unit_values, root_factor, gain):
    scaled = grad_out * gain
    return root_factor * (
        scaled - unit_values * jnp.mean(scaled * unit_values, axis=-1, keepdims=True)
    )


def place():
    return tuple(lax.axis_index(name) for name in EVERY)


def plane_neighbours():
    far, row, core, seq, ctx = place()
    return {
        "c": (far, row, 1 - core, seq, ctx),
        "x": (far, row, core, 1 - seq, ctx),
        "y": (far, 1 - row, core, seq, ctx),
    }


def plane_slots():
    _, row, core, seq, _ = place()

    def slot(r, c, s):
        return (r * 2 + c) * 2 + s

    return slot, row, core, seq


def greet(devices):
    barrier = pltpu.get_barrier_semaphore()
    for device in devices:
        pl.semaphore_signal(barrier, inc=1, device_id=device, device_id_type=MESH)
    pl.semaphore_wait(barrier, len(devices))


def sender(near, send_sem, recv_sem):
    def send(index, source, target, to):
        copy = pltpu.make_async_remote_copy(
            src_ref=source,
            dst_ref=target,
            send_sem=send_sem.at[index],
            recv_sem=recv_sem.at[index],
            device_id=near[to] if isinstance(to, str) else to,
            device_id_type=MESH,
        )
        copy.start()
        return copy

    return send


class Gather:
    def __init__(self, x_ref, o_ref, local_sem, send_sem, recv_sem):
        slot, row, core, seq = plane_slots()
        self.own = slot(row, core, seq)
        self.side = slot(row, core, 1 - seq)
        self.back = slot(1 - row, core, seq)
        self.diag = slot(1 - row, core, 1 - seq)
        self.send = sender(plane_neighbours(), send_sem, recv_sem)
        self.x_ref, self.o_ref = x_ref, o_ref
        self.local = pltpu.make_async_copy(x_ref, o_ref.at[:, self.own], local_sem)
        half = o_ref.shape[0] // 2
        self.first = pl.ds(0, half)
        self.second = pl.ds(half, o_ref.shape[0] - half)

    def pass_on(self, index, rows, slot, to):
        part = self.o_ref.at[:, slot] if rows is None else self.o_ref.at[rows, slot]
        return self.send(index, part, part, to)

    def start(self):
        target = self.o_ref.at[:, self.own]
        self.to_x = self.send(0, self.x_ref, target, "x")
        self.to_y = self.send(1, self.x_ref, target, "y")
        self.to_c = self.send(2, self.x_ref, target, "c")
        self.local.start()

    def middle(self):
        self.to_x.wait_recv()
        self.on_y = self.pass_on(3, self.first, self.side, "y")
        self.side_c = self.pass_on(4, None, self.side, "c")
        self.to_y.wait_recv()
        self.on_x = self.pass_on(5, self.second, self.back, "x")
        self.back_c = self.pass_on(6, None, self.back, "c")

    def finish(self):
        self.on_y.wait_recv()
        diag_first = self.pass_on(7, self.first, self.diag, "c")
        self.on_x.wait_recv()
        diag_second = self.pass_on(8, self.second, self.diag, "c")
        self.local.wait()
        late = (self.to_c, self.side_c, self.back_c, diag_first, diag_second)
        for copy in late:
            copy.wait_recv()
        for copy in (self.to_x, self.to_y, self.on_y, self.on_x) + late:
            copy.wait_send()


def gather_kernel(x_ref, o_ref, local_sem, send_sem, recv_sem):
    near = plane_neighbours()
    greet([near["c"], near["x"], near["y"]])
    gather = Gather(x_ref, o_ref, local_sem, send_sem, recv_sem)
    gather.start()
    gather.middle()
    gather.finish()


def plane_gather(block):
    groups, rows, width = block.shape
    return pl.pallas_call(
        gather_kernel,
        out_shape=jax.ShapeDtypeStruct((groups, 8, rows, width), block.dtype),
        in_specs=[pl.BlockSpec(memory_space=pl.ANY)],
        out_specs=pl.BlockSpec(memory_space=pl.ANY),
        scratch_shapes=[
            pltpu.SemaphoreType.DMA,
            pltpu.SemaphoreType.DMA((9,)),
            pltpu.SemaphoreType.DMA((9,)),
        ],
        compiler_params=pltpu.CompilerParams(
            collective_id=0, has_side_effects=True, vmem_limit_bytes=VMEM_LIMIT
        ),
        name="plane_gather",
    )(block)


def scatter_kernel(
    p_ref, o_ref, mine, other, relay, arrived, load_sem, core_sem, core_recv, send_sem, recv_sem
):
    near = plane_neighbours()
    slot, row, core, seq = plane_slots()
    groups = mine.shape[1]
    half = groups // 2
    first = pl.ds(0, half)
    second = pl.ds(half, groups - half)
    greet([near["c"], near["x"], near["y"]])

    chips = ((1 - row, 1 - seq), (row, 1 - seq), (1 - row, seq), (row, seq))
    loads, exchanges = [], []
    for index, (r, s) in enumerate(chips):
        exchange = pltpu.make_async_remote_copy(
            src_ref=p_ref.at[:, slot(r, 1 - core, s)],
            dst_ref=other.at[index],
            send_sem=core_sem.at[index],
            recv_sem=core_recv.at[index],
            device_id=near["c"],
            device_id_type=MESH,
        )
        exchange.start()
        load = pltpu.make_async_copy(
            p_ref.at[:, slot(r, core, s)], mine.at[index], load_sem.at[index]
        )
        load.start()
        loads.append(load)
        exchanges.append(exchange)

    def chip_sum(index):
        loads[index].wait()
        exchanges[index].wait_recv()

        def body(g, carry):
            total = mine[index, g].astype(jnp.float32) + other[index, g].astype(jnp.float32)
            mine[index, g] = total.astype(mine.dtype)
            return carry

        lax.fori_loop(0, groups, body, 0)

    def send(index, source, target, to):
        copy = pltpu.make_async_remote_copy(
            src_ref=source,
            dst_ref=target,
            send_sem=send_sem.at[index],
            recv_sem=recv_sem.at[index],
            device_id=near[to],
            device_id_type=MESH,
        )
        copy.start()
        return copy

    def relay_sum(index, which, start):
        def body(g, carry):
            total = mine[index, g + start].astype(jnp.float32) + relay[which, g].astype(jnp.float32)
            mine[index, g + start] = total.astype(mine.dtype)
            return carry

        lax.fori_loop(0, half, body, 0)

    chip_sum(0)
    diag_x = send(0, mine.at[0, first], relay.at[0], "x")
    diag_y = send(1, mine.at[0, second], relay.at[1], "y")
    chip_sum(1)
    plain_x = send(2, mine.at[1, first], arrived.at[0, first], "x")
    chip_sum(2)
    plain_y = send(3, mine.at[2, second], arrived.at[1, second], "y")
    diag_x.wait_recv()
    relay_sum(2, 0, 0)
    joint_y = send(4, mine.at[2, first], arrived.at[1, first], "y")
    diag_y.wait_recv()
    relay_sum(1, 1, half)
    joint_x = send(5, mine.at[1, second], arrived.at[0, second], "x")
    loads[3].wait()
    exchanges[3].wait_recv()
    plain_x.wait_recv()
    plain_y.wait_recv()
    joint_x.wait_recv()
    joint_y.wait_recv()

    def body(g, carry):
        o_ref[g] = (
            mine[3, g].astype(jnp.float32)
            + other[3, g].astype(jnp.float32)
            + arrived[0, g].astype(jnp.float32)
            + arrived[1, g].astype(jnp.float32)
        )
        return carry

    lax.fori_loop(0, groups, body, 0)
    for copy in exchanges:
        copy.wait_send()
    for copy in (diag_x, diag_y, plain_x, plain_y, joint_x, joint_y):
        copy.wait_send()


def plane_scatter(partial_sums):
    groups, _, rows, width = partial_sums.shape
    kind = partial_sums.dtype
    return pl.pallas_call(
        scatter_kernel,
        out_shape=jax.ShapeDtypeStruct((groups, rows, width), jnp.float32),
        in_specs=[pl.BlockSpec(memory_space=pl.ANY)],
        out_specs=pl.BlockSpec(memory_space=pltpu.VMEM),
        scratch_shapes=[
            pltpu.VMEM((4, groups, rows, width), kind),
            pltpu.VMEM((4, groups, rows, width), kind),
            pltpu.VMEM((2, groups // 2, rows, width), kind),
            pltpu.VMEM((2, groups, rows, width), kind),
            pltpu.SemaphoreType.DMA((4,)),
            pltpu.SemaphoreType.DMA((4,)),
            pltpu.SemaphoreType.DMA((4,)),
            pltpu.SemaphoreType.DMA((6,)),
            pltpu.SemaphoreType.DMA((6,)),
        ],
        compiler_params=pltpu.CompilerParams(
            collective_id=1, has_side_effects=True, vmem_limit_bytes=VMEM_LIMIT
        ),
        name="plane_scatter",
    )(partial_sums)


class Exchange:
    def __init__(self, outward, v_ref, o_ref, stage, send_sem, recv_sem):
        self.far, self.row, self.core, self.seq, self.ctx = place()
        self.planes = lax.axis_size("ctx")
        self.held = 8 // self.planes
        self.own = (self.row * 2 + self.core) * 2 + self.seq
        self.outward, self.v_ref, self.o_ref, self.stage = outward, v_ref, o_ref, stage
        self.send_sem, self.recv_sem = send_sem, recv_sem
        self.copies = []

    def move(self, index, source, target, arrival, rank, plane):
        same = (rank == self.own) & (plane == self.ctx)
        remote = pltpu.make_async_remote_copy(
            src_ref=source,
            dst_ref=target,
            send_sem=self.send_sem.at[index],
            recv_sem=self.recv_sem.at[arrival],
            device_id=(self.far, rank // 4, (rank // 2) % 2, rank % 2, plane),
            device_id_type=MESH,
        )
        local = pltpu.make_async_copy(source, target, self.recv_sem.at[arrival])
        pl.when(same)(local.start)
        pl.when(jnp.logical_not(same))(remote.start)
        self.copies.append((same, remote))

    def arrived(self, target, index):
        pltpu.make_async_copy(target, target, self.recv_sem.at[index]).wait()

    def start(self):
        own, ctx, held = self.own, self.ctx, self.held
        for k in range(8):
            if self.outward:
                rank = (own + k) % 8
                self.move(k, self.v_ref.at[rank], self.stage.at[own], 8 + own, rank, ctx)
            else:
                s, z = k // self.planes, (ctx + k) % self.planes
                rank = ctx * held + s
                self.move(k, self.v_ref.at[s, z], self.stage.at[rank], 8 + rank, own, z)

    def middle(self):
        own, ctx, held = self.own, self.ctx, self.held
        for k in range(8):
            rank = (own + 8 - k) % 8 if self.outward else (own + k) % 8
            self.arrived(self.stage.at[rank], 8 + rank)
            if self.outward:
                target = self.o_ref.at[rank % held, ctx]
                arrival = (rank % held) * self.planes + ctx
                self.move(8 + k, self.stage.at[rank], target, arrival, own, rank // held)
            else:
                self.move(8 + k, self.stage.at[rank], self.o_ref.at[own], own, rank, ctx)

    def received(self, k):
        if self.outward:
            self.arrived(self.o_ref.at[k // self.planes, k % self.planes], k)
        else:
            self.arrived(self.o_ref.at[k], k)

    def finish(self):
        for same, remote in self.copies:
            pl.when(jnp.logical_not(same))(remote.wait_send)


class Rows:
    def __init__(self, segments, r_ref, o_ref, local_sem, send_sem, recv_sem):
        slot, row, core, seq = plane_slots()
        self.seq = seq
        self.own = slot(row, core, seq)
        self.side = slot(row, core, 1 - seq)
        self.back = slot(1 - row, core, seq)
        self.diag = slot(1 - row, core, 1 - seq)
        self.segments, self.r_ref, self.o_ref = segments, r_ref, o_ref
        self.local_sem = local_sem
        self.send = sender(plane_neighbours(), send_sem, recv_sem)
        self.sent = []

    def part(self, rank, segment):
        _, width, base = self.segments[segment]
        return self.o_ref.at[:, pl.ds(pl.multiple_of(base + rank * width, 128), width)]

    def put(self, index, segment, source, target, to):
        copy = self.send(index * len(self.segments) + segment, source, target, to)
        self.sent.append(copy)
        return copy

    def start(self):
        self.to_x, self.to_y, self.to_c, self.local = [], [], [], []
        for i, (start, width, _) in enumerate(self.segments):
            target = self.part(self.own, i)
            mine = self.r_ref.at[self.seq, :, pl.ds(start, width)]
            theirs = self.r_ref.at[1 - self.seq, :, pl.ds(start, width)]
            self.to_x.append(self.put(0, i, theirs, target, "x"))
            self.to_y.append(self.put(1, i, mine, target, "y"))
            self.to_c.append(self.put(2, i, mine, target, "c"))
            copy = pltpu.make_async_copy(mine, target, self.local_sem.at[i])
            copy.start()
            self.local.append(copy)

    def middle(self):
        self.x_y, self.x_c, self.y_c = [], [], []
        for i in range(len(self.segments)):
            self.to_x[i].wait_recv()
            side = self.part(self.side, i)
            self.x_y.append(self.put(3, i, side, side, "y"))
            self.x_c.append(self.put(4, i, side, side, "c"))
        for i in range(len(self.segments)):
            self.to_y[i].wait_recv()
            back = self.part(self.back, i)
            self.y_c.append(self.put(5, i, back, back, "c"))

    def finish(self):
        d_c = []
        for i in range(len(self.segments)):
            self.x_y[i].wait_recv()
            diag = self.part(self.diag, i)
            d_c.append(self.put(6, i, diag, diag, "c"))
        for copy in self.to_c + self.x_c + self.y_c + d_c:
            copy.wait_recv()
        for copy in self.sent:
            copy.wait_send()
        for copy in self.local:
            copy.wait()


def mates_of(own, far, ctx):
    return [
        (far, (own + k) % 8 // 4, ((own + k) % 8 // 2) % 2, (own + k) % 2, ctx) for k in range(1, 8)
    ]


def prologue_kernel(
    tokens_ref, cot_ref, layout_ref, gain_ref,
    own_tokens, own_cot, normed_all, cot_all, lay_out, gain_out,
    normed, stage, small_send, small_recv, ex_send, ex_recv, local_sem, g_send, g_recv,
):
    far, row, core, seq, ctx = place()
    planes = lax.axis_size("ctx")
    own = (row * 2 + core) * 2 + seq
    mates = mates_of(own, far, ctx)
    line = ctx * 2 + seq
    total = planes * 2
    owners = [
        (far, row, core, (line + k) % 2, ((line + k) % total) // 2) for k in range(1, total)
    ]
    greet(mates + owners)
    lay_out[own] = layout_ref[...]
    gain_out[line] = gain_ref[...]
    send = sender({}, small_send, small_recv)
    small = [
        send(k, gain_ref, gain_out.at[line], device) for k, device in enumerate(owners)
    ] + [
        send(len(owners) + k, layout_ref, lay_out.at[own], device)
        for k, device in enumerate(mates)
    ]
    tokens = Exchange(True, tokens_ref, own_tokens, stage.at[0], ex_send.at[0], ex_recv.at[0])
    cots = Exchange(True, cot_ref, own_cot, stage.at[1], ex_send.at[1], ex_recv.at[1])
    tokens.start()
    tokens.middle()
    cots.start()
    for copy in small[: len(owners)]:
        copy.wait_recv()
    gain_rows = own_tokens.shape[-1] // total // 128
    pieces = [
        gain_out[owner, r : r + 1, :] for owner in range(total) for r in range(gain_rows)
    ]
    gain_row = jnp.concatenate(pieces, axis=1)
    for k in range(8):
        tokens.received(k)
        s, z = k // planes, k % planes
        wide = own_tokens[s, z].astype(jnp.float32)
        root = lax.rsqrt(jnp.mean(wide * wide, axis=1, keepdims=True) + norm_epsilon)
        normed[k] = (wide * root * gain_row).astype(normed.dtype)
    first = Gather(normed, normed_all, local_sem.at[0], g_send.at[0], g_recv.at[0])
    second = Gather(
        own_cot.reshape(normed.shape), cot_all, local_sem.at[1], g_send.at[1], g_recv.at[1]
    )
    first.start()
    cots.middle()
    first.middle()
    for k in range(8):
        cots.received(k)
    second.start()
    first.finish()
    second.middle()
    second.finish()
    for copy in small[len(owners) :]:
        copy.wait_recv()
    for copy in small:
        copy.wait_send()
    tokens.finish()
    cots.finish()


def prologue(tokens, cotangents, layout, gains):
    planes = lax.axis_size("ctx")
    rows, width = tokens.shape[-2:]
    kind = tokens.dtype
    count = 7 + 2 * planes - 1
    vmem = pl.BlockSpec(memory_space=pltpu.VMEM)
    anywhere = pl.BlockSpec(memory_space=pl.ANY)
    return pl.pallas_call(
        prologue_kernel,
        out_shape=(
            jax.ShapeDtypeStruct((8 // planes, planes, rows, width), kind),
            jax.ShapeDtypeStruct((8 // planes, planes, rows, width), kind),
            jax.ShapeDtypeStruct((8, 8, rows, width), kind),
            jax.ShapeDtypeStruct((8, 8, rows, width), kind),
            jax.ShapeDtypeStruct((8,) + layout.shape, layout.dtype),
            jax.ShapeDtypeStruct((2 * planes,) + gains.shape, gains.dtype),
        ),
        in_specs=[anywhere, anywhere, vmem, vmem],
        out_specs=(vmem, vmem, anywhere, anywhere, vmem, vmem),
        scratch_shapes=[
            pltpu.VMEM((8, rows, width), kind),
            pltpu.VMEM((2, 8, rows, width), kind),
            pltpu.SemaphoreType.DMA((count,)),
            pltpu.SemaphoreType.DMA((count,)),
            pltpu.SemaphoreType.DMA((2, 16)),
            pltpu.SemaphoreType.DMA((2, 16)),
            pltpu.SemaphoreType.DMA((2,)),
            pltpu.SemaphoreType.DMA((2, 9)),
            pltpu.SemaphoreType.DMA((2, 9)),
        ],
        compiler_params=pltpu.CompilerParams(
            collective_id=2, has_side_effects=True, vmem_limit_bytes=VMEM_LIMIT
        ),
        name="prologue",
    )(tokens, cotangents, layout, gains)


def return_kernel(
    plans, with_sum, *refs,
):
    count = len(plans)
    v_ref, *refs = refs
    r_refs, refs = refs[:count], refs[count:]
    if with_sum:
        small_ref, *refs = refs
    o_ref, *refs = refs
    g_refs, refs = refs[:count], refs[count:]
    if with_sum:
        sum_ref, *refs = refs
    stage, ex_send, ex_recv, *refs = refs
    row_sems, refs = refs[: 3 * count], refs[3 * count :]
    far, row, core, seq, ctx = place()
    planes = lax.axis_size("ctx")
    own = (row * 2 + core) * 2 + seq
    mates = mates_of(own, far, ctx)
    levels = [(far, row, core, seq, (ctx + k) % planes) for k in range(1, planes)]
    greet(mates + levels)
    exchange = Exchange(False, v_ref, o_ref, stage, ex_send, ex_recv)
    rows = [
        Rows(plan, r_refs[i], g_refs[i], *row_sems[3 * i : 3 * i + 3])
        for i, plan in enumerate(plans)
    ]
    for part in rows:
        part.start()
    exchange.start()
    if with_sum:
        line, got, sum_send, sum_recv = refs
        send = sender({}, sum_send, sum_recv)
        copies = [
            send(k - 1, small_ref.at[(ctx + k) % planes], line.at[k], levels[k - 1])
            for k in range(1, planes)
        ]
        for copy in copies:
            copy.wait_recv()
        total = small_ref[ctx]
        for k in range(1, planes):
            total += line[k]
        line[0] = total
        more = [
            send(planes - 2 + k, line.at[0, (own + k) % 2], got.at[k], mates[k - 1])
            for k in range(1, 8)
        ]
    for part in rows:
        part.middle()
    exchange.middle()
    for part in rows:
        part.finish()
    for k in range(8):
        exchange.received(k)
    exchange.finish()
    if with_sum:
        for copy in more:
            copy.wait_recv()
        total = line[0, seq]
        for k in range(1, 8):
            total += got[k]
        sum_ref[...] = total
        for copy in copies + more:
            copy.wait_send()


def send_back(values, parts, plans, widths, small, identity):
    planes = lax.axis_size("ctx")
    rows, width = values.shape[-2:]
    kind = values.dtype
    vmem = pl.BlockSpec(memory_space=pltpu.VMEM)
    anywhere = pl.BlockSpec(memory_space=pl.ANY)
    dma = pltpu.SemaphoreType.DMA
    outs = [jax.ShapeDtypeStruct((8, rows, width), kind)] + [
        jax.ShapeDtypeStruct((part.shape[1], total), part.dtype)
        for part, total in zip(parts, widths)
    ]
    scratch = [pltpu.VMEM((8, rows, width), kind), dma((16,)), dma((16,))]
    for plan in plans:
        scratch += [dma((len(plan),)), dma((7 * len(plan),)), dma((7 * len(plan),))]
    ins = [values, *parts]
    in_specs = [anywhere] * len(ins)
    out_specs = [anywhere] * len(outs)
    if small is not None:
        ins.append(small)
        in_specs.append(vmem)
        outs.append(jax.ShapeDtypeStruct(small.shape[2:], small.dtype))
        out_specs.append(vmem)
        scratch += [
            pltpu.VMEM(small.shape, small.dtype),
            pltpu.VMEM((8,) + small.shape[2:], small.dtype),
            dma((planes + 6,)),
            dma((planes + 6,)),
        ]
    return pl.pallas_call(
        functools.partial(return_kernel, plans, small is not None),
        out_shape=tuple(outs),
        in_specs=in_specs,
        out_specs=tuple(out_specs),
        scratch_shapes=scratch,
        compiler_params=pltpu.CompilerParams(
            collective_id=identity, has_side_effects=True, vmem_limit_bytes=VMEM_LIMIT
        ),
        name="send_back",
    )(*ins)


def head_rotation(values, gain, cosine, sine):
    root = lax.rsqrt(jnp.mean(values * values, axis=1, keepdims=True) + norm_epsilon)
    unit = values * root
    normed = unit * gain
    return normed * cosine + pltpu.roll(normed, HEAD_SIZE // 2, 1) * sine


def head_back(grads, values, gain, cosine, sine):
    back = grads * cosine - pltpu.roll(grads, HEAD_SIZE // 2, 1) * sine
    root = lax.rsqrt(jnp.mean(values * values, axis=1, keepdims=True) + norm_epsilon)
    unit = values * root
    scaled = back * gain
    raw = root * (scaled - unit * jnp.mean(scaled * unit, axis=1, keepdims=True))
    return raw, jnp.sum(back * unit, axis=0, keepdims=True)


def allowed_keys(query_code_ref, key_code_ref, start, size):
    stop = start + size
    same = query_code_ref[0, start:stop, :1] == key_code_ref[0, :1, :stop]
    queries = start + lax.broadcasted_iota(jnp.int32, (size, stop), 0)
    keys = lax.broadcasted_iota(jnp.int32, (size, stop), 1)
    return (same & (keys <= queries)) | (keys == queries)


def attend_kernel(
    heads, block, p_ref, gain_ref, cos_ref, sin_ref, qcode_ref, kcode_ref,
    mixed_ref, o_ref, q_ref, k_ref, lse_ref,
):
    length = p_ref.shape[1]
    width = heads * HEAD_SIZE
    scale = HEAD_SIZE ** (-0.5)
    f32, bf16 = jnp.float32, jnp.bfloat16
    cosine, sine = cos_ref[...], sin_ref[...]
    for h in range(heads):
        cols = slice(h * HEAD_SIZE, (h + 1) * HEAD_SIZE)
        q_ref[0, :, cols] = head_rotation(p_ref[0, :, cols], gain_ref[0:1], cosine, sine).astype(
            bf16
        )
    k_ref[0] = head_rotation(
        p_ref[0, :, 2 * width : 2 * width + HEAD_SIZE], gain_ref[1:2], cosine, sine
    ).astype(bf16)
    for start in range(0, length, block):
        stop = start + block
        allowed = allowed_keys(qcode_ref, kcode_ref, start, block)
        keys = k_ref[0, :stop]
        values = p_ref[0, :stop, 2 * width + HEAD_SIZE :].astype(bf16)
        for h in range(heads):
            cols = slice(h * HEAD_SIZE, (h + 1) * HEAD_SIZE)
            gates = slice(width + h * HEAD_SIZE, width + (h + 1) * HEAD_SIZE)
            scores = lax.dot_general(
                q_ref[0, start:stop, cols], keys, contract_cols, preferred_element_type=f32
            )
            scores = jnp.where(allowed, scores * scale, masked_value)
            peak = jnp.max(scores, axis=1, keepdims=True)
            exps = jnp.exp(scores - peak)
            total = jnp.sum(exps, axis=1, keepdims=True)
            probs = (exps * (1.0 / total)).astype(bf16)
            attended = jnp.dot(probs, values, preferred_element_type=f32)
            o_ref[0, start:stop, cols] = attended
            gate = jax.nn.sigmoid(p_ref[0, start:stop, gates])
            mixed_ref[0, start:stop, cols] = (attended * gate).astype(bf16)
            lse_ref[0, h, start:stop] = jnp.broadcast_to(peak + jnp.log(total), (block, HEAD_SIZE))


def attend_back_kernel(
    heads, block, da_ref, p_ref, gain_ref, cos_ref, sin_ref, qcode_ref, kcode_ref,
    o_ref, q_ref, k_ref, lse_ref, dp_ref, hg_ref, dq_acc, dk_acc, dv_acc,
):
    length = p_ref.shape[1]
    width = heads * HEAD_SIZE
    scale = HEAD_SIZE ** (-0.5)
    f32, bf16 = jnp.float32, jnp.bfloat16
    dk_acc[...] = jnp.zeros_like(dk_acc)
    dv_acc[...] = jnp.zeros_like(dv_acc)

    @pl.when(pl.program_id(0) == 0)
    def _():
        hg_ref[...] = jnp.zeros_like(hg_ref)

    for start in range(0, length, block):
        stop = start + block
        allowed = allowed_keys(qcode_ref, kcode_ref, start, block)
        keys = k_ref[0, :stop]
        values = p_ref[0, :stop, 2 * width + HEAD_SIZE :].astype(bf16)
        for h in range(heads):
            cols = slice(h * HEAD_SIZE, (h + 1) * HEAD_SIZE)
            gates = slice(width + h * HEAD_SIZE, width + (h + 1) * HEAD_SIZE)
            queries = q_ref[0, start:stop, cols]
            scores = lax.dot_general(queries, keys, contract_cols, preferred_element_type=f32)
            scores = jnp.where(allowed, scores * scale, masked_value)
            probs = jnp.exp(scores - lse_ref[0, h, start:stop, :1])
            gate = jax.nn.sigmoid(p_ref[0, start:stop, gates])
            grads = da_ref[0, start:stop, cols]
            dp_ref[0, start:stop, gates] = (
                grads * o_ref[0, start:stop, cols] * gate * (1.0 - gate)
            ).astype(bf16)
            d_out = (grads * gate).astype(bf16)
            d_probs = lax.dot_general(d_out, values, contract_cols, preferred_element_type=f32)
            delta = jnp.sum(probs * d_probs, axis=1, keepdims=True)
            d_scores = (probs * (d_probs - delta)).astype(bf16)
            dv_acc[:stop] += lax.dot_general(
                probs.astype(bf16), d_out, contract_rows, preferred_element_type=f32
            )
            dk_acc[:stop] += lax.dot_general(
                d_scores, queries, contract_rows, preferred_element_type=f32
            )
            dq_acc[h, start:stop] = jnp.dot(d_scores, keys, preferred_element_type=f32)
    cosine, sine = cos_ref[...], sin_ref[...]
    for h in range(heads):
        cols = slice(h * HEAD_SIZE, (h + 1) * HEAD_SIZE)
        raw, term = head_back(dq_acc[h] * scale, p_ref[0, :, cols], gain_ref[0:1], cosine, sine)
        dp_ref[0, :, cols] = raw.astype(bf16)
        hg_ref[0:1] += term
    at = 2 * width
    raw, term = head_back(
        dk_acc[...] * scale, p_ref[0, :, at : at + HEAD_SIZE], gain_ref[1:2], cosine, sine
    )
    dp_ref[0, :, at : at + HEAD_SIZE] = raw.astype(bf16)
    hg_ref[1:2] += term
    dp_ref[0, :, at + HEAD_SIZE :] = dv_acc[...].astype(bf16)


def whole_spec(shape):
    zeros = (0,) * len(shape)
    return pl.BlockSpec(tuple(shape), lambda i: zeros)


def first_spec(shape):
    zeros = (0,) * (len(shape) - 1)
    return pl.BlockSpec((1,) + tuple(shape[1:]), lambda i: (i,) + zeros)


def attend(projected, gain, cosine, sine, query_code, key_code, heads):
    held, length, _ = projected.shape
    width = heads * HEAD_SIZE
    f32, bf16 = jnp.float32, jnp.bfloat16
    outs = (
        jax.ShapeDtypeStruct((held, length, width), bf16),
        jax.ShapeDtypeStruct((held, length, width), f32),
        jax.ShapeDtypeStruct((held, length, width), bf16),
        jax.ShapeDtypeStruct((held, length, HEAD_SIZE), bf16),
        jax.ShapeDtypeStruct((held, heads, length, HEAD_SIZE), f32),
    )
    return pl.pallas_call(
        functools.partial(attend_kernel, heads, min(256, length)),
        grid=(held,),
        out_shape=outs,
        in_specs=[
            first_spec(projected.shape),
            whole_spec(gain.shape),
            whole_spec(cosine.shape),
            whole_spec(sine.shape),
            first_spec(query_code.shape),
            first_spec(key_code.shape),
        ],
        out_specs=tuple(first_spec(out.shape) for out in outs),
        compiler_params=pltpu.CompilerParams(vmem_limit_bytes=VMEM_LIMIT),
        cost_estimate=pl.CostEstimate(
            flops=4 * held * heads * length * length * HEAD_SIZE,
            bytes_accessed=held * length * 8192,
            transcendentals=held * heads * length * length,
        ),
        name="attend",
    )(projected, gain, cosine, sine, query_code, key_code)


def attend_back(da, projected, gain, cosine, sine, query_code, key_code, saved, heads):
    held, length, columns = projected.shape
    _, attended, queries, keys, lse = saved
    outs = (
        jax.ShapeDtypeStruct((held, length, columns), jnp.bfloat16),
        jax.ShapeDtypeStruct((8, HEAD_SIZE), jnp.float32),
    )
    ins = (query_code, key_code, attended, queries, keys, lse)
    return pl.pallas_call(
        functools.partial(attend_back_kernel, heads, min(256, length)),
        grid=(held,),
        out_shape=outs,
        in_specs=[
            first_spec(da.shape),
            first_spec(projected.shape),
            whole_spec(gain.shape),
            whole_spec(cosine.shape),
            whole_spec(sine.shape),
        ]
        + [first_spec(value.shape) for value in ins],
        out_specs=(first_spec(outs[0].shape), whole_spec(outs[1].shape)),
        scratch_shapes=[
            pltpu.VMEM((heads, length, HEAD_SIZE), jnp.float32),
            pltpu.VMEM((length, HEAD_SIZE), jnp.float32),
            pltpu.VMEM((length, HEAD_SIZE), jnp.float32),
        ],
        compiler_params=pltpu.CompilerParams(vmem_limit_bytes=VMEM_LIMIT),
        cost_estimate=pl.CostEstimate(
            flops=10 * held * heads * length * length * HEAD_SIZE,
            bytes_accessed=held * length * 8192,
            transcendentals=held * heads * length * length,
        ),
        name="attend_back",
    )(da, projected, gain, cosine, sine, *ins)


def per_device(
    tokens,
    cotangent,
    document_index,
    padding_token_mask,
    attention_gain,
    projection_weight,
    head_gain,
    out_weight,
    feedforward_gain,
    gate_weight,
    up_weight,
    down_weight,
):
    far, row, core, seq, ctx = place()
    token_rows, model_width = tokens.shape
    sequence_length = document_index.shape[0]
    planes = lax.axis_size("ctx")
    seqs = lax.axis_size("seq")
    plane_size = lax.axis_size(PLANE)
    plane_rank = (row * 2 + core) * seqs + seq
    held = plane_size // planes
    chunk = token_rows // plane_size
    groups = held * planes
    plane_tokens = held * sequence_length
    shard_rows = projection_weight.shape[0]
    ff_part = gate_weight.shape[1] // plane_size
    heads = QUERY_HEADS // plane_size
    query_part = heads * HEAD_SIZE
    query_total = QUERY_HEADS * HEAD_SIZE
    key_total = KEY_VALUE_HEADS * HEAD_SIZE
    score_scale = HEAD_SIZE ** (-0.5)
    f32 = jnp.float32
    bf16 = jnp.bfloat16

    def to_inner(values):
        return (
            values.reshape(values.shape[0], seqs, planes, shard_rows)
            .transpose(0, 2, 1, 3)
            .reshape(values.shape)
        )

    def to_outer(values):
        return (
            values.reshape(values.shape[0], planes, seqs, shard_rows)
            .transpose(0, 2, 1, 3)
            .reshape(values.shape)
        )

    def gathered(block):
        return plane_gather(block).reshape(plane_tokens, model_width)

    def scattered(partial_rows):
        return plane_scatter(
            partial_rows.astype(bf16).reshape(groups, plane_size, chunk, model_width)
        )

    def columns_of(rank, weight, width, start):
        return lax.dynamic_slice_in_dim(weight, start + rank * width, width, 1)

    def proj_columns(rank):
        return jnp.concatenate(
            [
                columns_of(rank, projection_weight, query_part, 0),
                columns_of(rank, projection_weight, query_part, query_total),
                columns_of(rank, projection_weight, HEAD_SIZE, 2 * query_total),
                columns_of(rank, projection_weight, HEAD_SIZE, 2 * query_total + key_total),
            ],
            axis=1,
        )

    def out_columns(rank):
        return columns_of(rank, out_weight, query_part, 0)

    def up_columns(rank):
        return jnp.concatenate(
            [
                columns_of(rank, gate_weight, ff_part, 0),
                columns_of(rank, up_weight, ff_part, 0),
            ],
            axis=1,
        )

    def down_columns(rank):
        return columns_of(rank, down_weight, ff_part, 0)

    def swapped(piece_of):
        base = (row * 2 + core) * seqs
        other = lax.ppermute(piece_of(base + 1 - seq), "seq", [(0, 1), (1, 0)])
        own = piece_of(base + seq)
        return jnp.where(seq == 0, jnp.stack([own, other]), jnp.stack([other, own]))

    def whole_columns(piece):
        piece = piece.reshape(seqs * shard_rows, piece.shape[-1])
        return lax.all_gather(piece, "ctx", axis=0, tiled=True)

    layout_pack = (document_index * 2 + padding_token_mask).astype(f32).reshape(-1, 128)
    gain_rows = 2 * shard_rows // 128
    gain_pack = (
        jnp.zeros((8, 128), f32)
        .at[:gain_rows]
        .set(jnp.concatenate([attention_gain, feedforward_gain]).astype(f32).reshape(-1, 128))
    )
    pad_here = lax.dynamic_slice_in_dim(padding_token_mask, ctx * token_rows, token_rows, 0)
    grad_here = (cotangent.astype(f32) * pad_here.astype(f32)[:, None]).astype(bf16)
    chunked = (plane_size, chunk, model_width)
    proj_piece = swapped(proj_columns)
    later = (swapped(out_columns), swapped(up_columns), swapped(down_columns))
    proj_w = whole_columns(proj_piece)
    tokens_own, own_grad, normed_attn, grad_low, layouts, gains = prologue(
        to_inner(tokens).reshape(chunked), to_inner(grad_here).reshape(chunked),
        layout_pack, gain_pack,
    )
    later, normed_attn = lax.optimization_barrier((later, normed_attn))
    out_w, up_w, down_w = (whole_columns(piece) for piece in later)
    tokens_wide = tokens_own.reshape(groups, chunk, model_width).astype(f32)
    own_grad = own_grad.reshape(groups, chunk, model_width)
    normed_attn = normed_attn.reshape(plane_tokens, model_width)
    grad_low = grad_low.reshape(plane_tokens, model_width)

    gains = gains[:, :gain_rows].reshape(planes * seqs, 2, shard_rows)
    gain_attn = gains[:, 0].reshape(model_width)
    gain_mlp = gains[:, 1].reshape(model_width)
    layouts = layouts.reshape(plane_size, sequence_length)
    layouts = lax.dynamic_slice_in_dim(layouts, ctx * held, held, 0).astype(jnp.int32)
    document = layouts // 2
    real = layouts % 2

    root_attn = lax.rsqrt(jnp.mean(tokens_wide * tokens_wide, axis=2, keepdims=True) + norm_epsilon)
    unit_attn = tokens_wide * root_attn

    half_size = HEAD_SIZE // 2
    frequency = rope_base ** (-2.0 * jnp.arange(half_size, dtype=f32) / HEAD_SIZE)
    angles = jnp.arange(sequence_length, dtype=jnp.int32).astype(f32)[:, None] * frequency[None, :]
    cosine = jnp.cos(angles)
    sine = jnp.sin(angles)
    cosine = jnp.concatenate([cosine, cosine], axis=1)
    sine = jnp.concatenate([-sine, sine], axis=1)
    head_gain_wide = head_gain.astype(f32)
    query_code = jnp.broadcast_to(
        document.astype(f32)[:, :, None], (held, sequence_length, HEAD_SIZE)
    )
    key_code = jnp.where(real == 1, document, -1).astype(f32)[:, None, :]
    key_code = jnp.broadcast_to(key_code, (held, 8, sequence_length))

    projected = jnp.dot(normed_attn, proj_w, preferred_element_type=f32).reshape(
        held, sequence_length, -1
    )
    tables = (head_gain_wide, cosine, sine, query_code, key_code)
    saved = attend(projected, *tables, heads)
    mixed = saved[0].reshape(plane_tokens, query_part)
    resid_mid = tokens_wide + scattered(
        lax.dot_general(mixed, out_w, contract_cols, preferred_element_type=f32)
    )
    root_mlp = lax.rsqrt(jnp.mean(resid_mid * resid_mid, axis=2, keepdims=True) + norm_epsilon)
    unit_mlp = resid_mid * root_mlp
    normed_mlp = gathered((unit_mlp * gain_mlp).astype(bf16))
    both_lin = jnp.dot(normed_mlp, up_w, preferred_element_type=f32)
    gate_lin = both_lin[:, :ff_part]
    up_lin = both_lin[:, ff_part:]
    gate_sig = jax.nn.sigmoid(gate_lin)
    silu_gate = gate_lin * gate_sig
    hidden = (silu_gate * up_lin).astype(bf16)
    def grads_to_rows(grads):
        rows = lax.psum_scatter(grads.astype(bf16), "ctx", scatter_dimension=0, tiled=True)
        if lax.axis_size("far") > 1:
            rows = lax.psum(rows, "far")
        return rows.reshape(seqs, shard_rows, grads.shape[1])

    def after(value, *earlier):
        return lax.optimization_barrier((value,) + earlier)[0]

    down_part = lax.dot_general(
        grad_low, hidden, contract_rows, preferred_element_type=f32
    ).astype(bf16)
    grad_low = after(grad_low, down_part)
    d_hidden = jnp.dot(grad_low, down_w, preferred_element_type=f32)
    d_gate = (d_hidden * up_lin * gate_sig * (1.0 + gate_lin * (1.0 - gate_sig))).astype(bf16)
    d_up = (d_hidden * silu_gate).astype(bf16)
    d_both = jnp.concatenate([d_gate, d_up], axis=1)
    down_rows = grads_to_rows(down_part)
    up_part = lax.dot_general(
        normed_mlp, d_both, contract_rows, preferred_element_type=f32
    ).astype(bf16)
    up_rows = grads_to_rows(up_part)
    d_both = after(d_both, up_part)
    d_normed_mlp = scattered(
        lax.dot_general(d_both, up_w, contract_cols, preferred_element_type=f32)
    )
    gain_mlp_term = jnp.sum(d_normed_mlp * unit_mlp, axis=(0, 1))
    d_resid = own_grad.astype(f32) + norm_back(d_normed_mlp, unit_mlp, root_mlp, gain_mlp)
    d_attn_low = gathered(d_resid.astype(bf16))
    mixed_grad = jnp.dot(d_attn_low, out_w, preferred_element_type=f32)
    out_part = lax.dot_general(
        d_attn_low, mixed, contract_rows, preferred_element_type=f32
    ).astype(bf16)
    out_rows = grads_to_rows(out_part)
    mixed_grad = after(mixed_grad, out_part)
    d_proj, head_term = attend_back(
        mixed_grad.reshape(held, sequence_length, query_part), projected, *tables, saved, heads
    )
    d_proj = d_proj.reshape(plane_tokens, -1)
    head_term = head_term[:2]
    proj_part = lax.dot_general(
        normed_attn, d_proj, contract_rows, preferred_element_type=f32
    ).astype(bf16)
    proj_rows = grads_to_rows(proj_part)
    d_proj = after(d_proj, proj_part)
    d_normed_attn = scattered(
        lax.dot_general(d_proj, proj_w, contract_cols, preferred_element_type=f32)
    )
    hidden = after(hidden, d_normed_attn)
    layer_own = (
        resid_mid
        + scattered(lax.dot_general(hidden, down_w, contract_cols, preferred_element_type=f32))
    ).astype(bf16)
    gain_attn_term = jnp.sum(d_normed_attn * unit_attn, axis=(0, 1))
    tokens_grad = (d_resid + norm_back(d_normed_attn, unit_attn, root_attn, gain_attn)).astype(bf16)
    small_rows = shard_rows // 128

    def gain_tiles(term):
        return term.reshape(planes, seqs, small_rows, 128)

    tiles = jnp.concatenate(
        [
            gain_tiles(gain_attn_term),
            gain_tiles(gain_mlp_term),
            jnp.broadcast_to(head_term[None, None], (planes, seqs, 2, HEAD_SIZE)),
            jnp.zeros((planes, seqs, 6 - 2 * small_rows, 128), f32),
        ],
        axis=2,
    )
    proj_segments = (
        (0, query_part, 0),
        (query_part, query_part, query_total),
        (2 * query_part, HEAD_SIZE, 2 * query_total),
        (2 * query_part + HEAD_SIZE, HEAD_SIZE, 2 * query_total + key_total),
    )
    ff_width = plane_size * ff_part
    up_segments = ((0, ff_part, 0), (ff_part, ff_part, ff_width))
    parted = (held, planes, chunk, model_width)
    layer_out, up_grad, down_grad = send_back(
        layer_own.reshape(parted),
        (up_rows, down_rows),
        (up_segments, ((0, ff_part, 0),)),
        (2 * ff_width, ff_width),
        None,
        3,
    )
    proj_rows = after(proj_rows, layer_out)
    tokens_grad, proj_grad, out_grad, small = send_back(
        tokens_grad.reshape(parted),
        (proj_rows, out_rows),
        (proj_segments, ((0, query_part, 0),)),
        (2 * (query_total + key_total), query_total),
        tiles,
        4,
    )
    layer_out = to_outer(layer_out.reshape(token_rows, model_width))
    tokens_grad = to_outer(tokens_grad.reshape(token_rows, model_width))
    if lax.axis_size("far") > 1:
        small = lax.psum(small, "far")
    attention_gain_grad = small[:small_rows].reshape(shard_rows)
    feedforward_gain_grad = small[small_rows : 2 * small_rows].reshape(shard_rows)
    sum_head = small[2 * small_rows : 2 * small_rows + 2]
    return (
        layer_out,
        tokens_grad,
        attention_gain_grad,
        proj_grad.astype(f32),
        sum_head,
        out_grad.astype(f32),
        feedforward_gain_grad,
        up_grad[:, :ff_width].astype(f32),
        up_grad[:, ff_width:].astype(f32),
        down_grad.astype(f32),
    )


def solution(mesh):
    rep, seqs, ctxs = (mesh.shape[name] for name in ("rep", "seq", "ctx"))
    inner = Mesh(mesh.devices.reshape(rep // 4, 2, 2, seqs, ctxs), EVERY)
    token_axes = ("far", "row", "core", "seq", "ctx")
    sequence_axes = ("far", "row", "core", "seq")
    in_specs = (
        P(token_axes, None),
        P(token_axes, None),
        P(sequence_axes),
        P(sequence_axes),
        P(("seq", "ctx")),
        P(("seq", "ctx"), None),
        P(),
        P(("seq", "ctx"), None),
        P(("seq", "ctx")),
        P(("seq", "ctx"), None),
        P(("seq", "ctx"), None),
        P(("seq", "ctx"), None),
    )
    out_specs = (
        P(token_axes, None),
        P(token_axes, None),
        P(("seq", "ctx")),
        P(("seq", "ctx"), None),
        P(),
        P(("seq", "ctx"), None),
        P(("seq", "ctx")),
        P(("seq", "ctx"), None),
        P(("seq", "ctx"), None),
        P(("seq", "ctx"), None),
    )
    return jax.shard_map(
        per_device, mesh=inner, in_specs=in_specs, out_specs=out_specs, check_vma=False
    )
```

time: 1280 us -> 875 us (0.68)
  blocking collectives: 282 us -> 0 us
  Pallas kernels: 360 us -> 546 us
  waiting for transfers between devices: 198 us -> 56.9 us
  local copies, waits for them, and re-layouts: 110 us -> 51.6 us
  other arithmetic: 84.7 us -> 41.5 us
  matrix products: 185 us -> 147 us
  starting transfers between devices: 37.2 us -> 7.39 us
    pallas_call x0 -> x5, Pallas kernels: none -> 299 us  [the longest x1 147 us: prologue(): pl.pallas_call(prologue_kernel, out_shape=(jax.ShapeDtypeStruct((8 // pla...]
    all_to_all x8 -> x0, blocking collectives: 142 us -> none  [the longest x3 40.6 us: grads_to_rows(): rows = lax.all_to_all(rows, 'seq', 0, 0, tiled=True)]
    reduce_scatter x4, waiting for transfers between devices: 114 us -> 0.01 us  [grads_to_rows(): lax.psum_scatter(grads.astype(bf16), 'ctx', scatter_dimension=0, tiled=True)]
    all_gather x3 -> x0, blocking collectives: 93 us -> none  [the longest x1 40.3 us: per_device(): lax.all_gather(attention_gain, ('ctx', 'seq'), axis=0, tiled=True)]
    all_to_all x8 -> x0, waiting for transfers between devices: 84.6 us -> none  [the longest x2 37.8 us: to_plane(): parts = lax.all_to_all(parts, 'ctx', 0, 0, tiled=True)]
    pallas_call x4 -> x2, Pallas kernels: 163 us -> 82 us  [plane_gather(): pl.pallas_call(gather_kernel, out_shape=jax.ShapeDtypeStruct((groups, 8,...]
    psum x1 -> x0, blocking collectives: 47 us -> none  [per_device(): lax.psum((gain_attn_term, gain_mlp_term, head_term), EVERY)]
    all_gather x4, waiting for transfers between devices: 0.05 us -> 47 us  [whole_columns(): return lax.all_gather(piece, 'ctx', axis=0, tiled=True)]
  transfers between devices with their start and end apart: 20 -> 12, of which waited for: 7 -> 3; matrix products, arithmetic and copies ran while one was open for 22% -> 22% of each run, Pallas kernels for 22% -> 57%
where the time goes in v2:
time: 875 us; the launch traced here: 865 us
  Pallas kernels  546 us (62%)
  matrix products  147 us (17%)
  waiting for transfers between devices  56.9 us (7%)
  local copies, waits for them, and re-layouts  51.6 us (6%)
  other arithmetic  41.5 us (5%)
  between operations  15.1 us (2%)
    pallas_call x4, Pallas kernels, plane_scatter(): pl.pallas_call(scatter_kernel, out_shape=jax.ShapeDtypeStruct((groups, ro...  164 us
    pallas_call x1, Pallas kernels, prologue(): pl.pallas_call(prologue_kernel, out_shape=(jax.ShapeDtypeStruct((8 // pla...  147 us
    pallas_call x2, Pallas kernels, send_back(): pl.pallas_call(functools.partial(return_kernel, plans, small is not None)...  117 us
    pallas_call x2, Pallas kernels, plane_gather(): pl.pallas_call(gather_kernel, out_shape=jax.ShapeDtypeStruct((groups, 8,...  82 us
    all_gather x4, waiting for transfers between devices, whole_columns(): return lax.all_gather(piece, 'ctx', axis=0, tiled=True)  47 us
    unnamed x103, local copies, waits for them, and re-layouts  27.8 us
    pallas_call x1, Pallas kernels, attend_back(): pl.pallas_call(functools.partial(attend_back_kernel, heads, min(256, leng...  19.9 us
    dot_general x1, matrix products, per_device(): lax.dot_general(normed_mlp, d_both, contract_rows, preferred_element_type...  19.2 us
  transfers between devices with their start and end apart: 12, of which 3 were waited for; matrix products, arithmetic and copies ran while one was open for 22% of the time, Pallas kernels for 57%

profile of v2, /device:TPU:0, one launch (start us, length us, event | category | flops | bytes accessed | tf_op | source)
XLA Modules:
  0.0 865.2 jit_solution(252646102084579661)
XLA Ops:
  9.4 3.0 collective-permute-start.3
  12.5 9.1 %collective-permute-done.3 = bf16[256,768]{1,0:T(8,128)(2,1)S(1)} collective-permute-done((bf16[256,768]{1,0:T(8,128)(2,1)S(1)}, bf16[256,768]{1,0:T(8,128)(2,1)S(1)}, u32[]{:S(2)}, u32[]{:S(2)}) %collective-permute-start.3) | collective-permute-done | bytes 393248 | tf_op jit(solution)/shard_map/ppermute | solution.py:901
  42.4 147.4 %prologue.1 = (bf16[2,4,32,2048]{3,2,1,0:T(8,128)(2,1)S(1)}, bf16[2,4,32,2048]{3,2,1,0:T(8,128)(2,1)S(1)}, bf16[8,8,32,2048]{3,2,1,0:T(8,128)(2,1)}, bf16[8,8,32...) custom-call(bf16[8,32,2048]{2,1,0:T(8,128)(2,1)S(1)} %copy-done.9, ...), custom_call_target="tpu_custom_call" | custom-call | tf_op jit(solution)/shard_map/prologue/pallas_call | solution.py:476
  202.0 11.7 %fusion.1.p_ref = f32[2,1024,768]{2,1,0:T(8,128)} fusion(bf16[2,1024,2048]{2,1,0:T(8,128)(2,1)} %bitcast.142, bf16[2048,768]{1,0:T(8,128)(2,1)} %all-gather.5.cloned.1.call-done), kind=kOutput, calls=%fused_computation.13 | convolution fusion | flops 6442450944 | bytes 17825792 | tf_op jit(solution)/shard_map/dot_general | solution.py:958
  214.0 15.5 %attend.1 = (bf16[2,1024,256]{2,1,0:T(8,128)(2,1)S(1)}, f32[2,1024,256]{2,1,0:T(8,128)}, bf16[2,1024,256]{2,1,0:T(8,128)(2,1)S(1)}, bf16[2,1024,128]{2,1,0:T(8,128)(2,1)S(1)}, f32[2,2,1024,128]{3,2,1,0:T(8,128)}) custom-call(f32[2,1024,768]{2,1,0:T(8,128)} %fusion.1.p_ref, f32[2,128]{1,0:T(2,128)S(1)} %convert_element_type.120.gain_ref, ...), custom_call_target="tpu_custom_call" | custom-call | flops 2147483648 | bytes 16777216 | tf_op jit(solution)/shard_map/attend/pallas_call | solution.py:754
  233.8 7.6 convolution_convert_fusion.3
  241.5 42.0 %plane_scatter.4 = f32[8,32,2048]{2,1,0:T(8,128)S(1)} custom-call(bf16[8,8,32,2048]{3,2,1,0:T(8,128)(2,1)} %bitcast.108), custom_call_target="tpu_custom_call" | custom-call | tf_op jit(solution)/shard_map/plane_scatter/pallas_call | solution.py:254
  286.8 41.1 %plane_gather.2 = bf16[8,8,32,2048]{3,2,1,0:T(8,128)(2,1)} custom-call(bf16[8,32,2048]{2,1,0:T(8,128)(2,1)S(1)} %multiply_convert_fusion.3.x_ref), custom_call_target="tpu_custom_call" | custom-call | tf_op jit(solution)/shard_map/plane_gather/pallas_call | solution.py:137
  327.9 20.3 %all-gather.9.cloned.1.call-done = bf16[2048,1536]{1,0:T(8,128)(2,1)} async-done(((bf16[512,1536]{1,0:T(8,128)(2,1)}), bf16[2048,1536]{1,0:T(8,128)(2,1)}) %all-gather.9.cloned.1.call-update) | async-done | bytes 6291472 | tf_op jit(solution)/shard_map/all_gather | solution.py:907
  348.2 18.2 %fusion.12 = f32[2048,1536]{0,1:T(8,128)S(1)} fusion(bf16[2048,2048]{1,0:T(8,128)(2,1)} %bitcast.112, bf16[2048,1536]{1,0:T(8,128)(2,1)} %all-gather.9.cloned.1.call-done), kind=kOutput, calls=%fused_computation.91 | convolution fusion | flops 12884901888 | bytes 27262976 | tf_op jit(solution)/shard_map/dot_general | solution.py:970
  366.5 4.6 copy-done.32
  374.7 10.5 %convolution_convert_fusion.6 = bf16[2048,768]{1,0:T(8,128)(2,1)} fusion(bf16[2048,2048]{1,0:T(8,128)(2,1)} %bitcast.144, bf16[2048,768]{0,1:T(8,128)(2,1)S(1)} %multiply_convert_fusion.2), kind=kOutput, calls=%fused_computation.12 | convolution fusion | flops 6444023808 | bytes 14680064 | tf_op jit(solution)/shard_map/dot_general | solution.py:985
  385.3 26.7 %all-gather.11.cloned.1.call-done = bf16[2048,768]{1,0:T(8,128)(2,1)} async-done(((bf16[512,768]{1,0:T(8,128)(2,1)}), bf16[2048,768]{1,0:T(8,128)(2,1)}) %all-gather.11.cloned.1.call-update) | async-done | bytes 3145744 | tf_op jit(solution)/shard_map/all_gather | solution.py:907
  412.0 16.9 %multiply_convert_fusion.1 = (bf16[2048,768]{0,1:T(8,128)(2,1)}, bf16[2048,768]{0,1:T(8,128)(2,1)}) fusion(f32[2048,1536]{0,1:T(8,128)} %copy-done.32, bf16[2048,2048]{1,0:T(8,128)(2,1)} %bitcast.145, bf16[2048,768]{1,0:T(8,128)(2,1)} %all-gather.11.cloned.1.call-done), kind=kOutput, calls=%fused_computation.7 | convolution fusion | flops 6462898176 | bytes 30408704 | tf_op jit(solution)/shard_map/dot_general | solution.py:989
  428.9 19.2 %convolution_convert_fusion.4 = bf16[2048,1536]{1,0:T(8,128)(2,1)} fusion(bf16[2048,2048]{1,0:T(8,128)(2,1)} %bitcast.113, bf16[2048,768]{0,1:T(8,128)(2,1)} %get-tuple-element.89, bf16[2048,768]{0,1:T(8,128)(2,1)} %get-tuple-element.88), kind=kOutput, calls=%fused_computation.4 | convolution fusion | flops 12900630528 | bytes 20971520 | tf_op jit(solution)/shard_map/dot_general | solution.py:994
  448.2 4.0 pad_maximum_fusion
  452.2 17.8 %convolution_convert_fusion.2 = bf16[2048,2048]{1,0:T(8,128)(2,1)} fusion(bf16[2048,1536]{0,1:T(8,128)(2,1)S(1)} %pad_maximum_fusion, bf16[2048,1536]{1,0:T(8,128)(2,1)} %all-gather.9.cloned.1.call-done), kind=kOutput, calls=%fused_computation.2 | convolution fusion | flops 12889096192 | bytes 20971520 | tf_op jit(solution)/shard_map/dot_general | solution.py:1000
  470.0 40.8 %plane_scatter.5 = f32[8,32,2048]{2,1,0:T(8,128)S(1)} custom-call(bf16[8,8,32,2048]{3,2,1,0:T(8,128)(2,1)} %bitcast.110), custom_call_target="tpu_custom_call" | custom-call | tf_op jit(solution)/shard_map/plane_scatter/pallas_call | solution.py:254
  512.1 40.9 %plane_gather.3 = bf16[8,8,32,2048]{3,2,1,0:T(8,128)(2,1)} custom-call(bf16[8,32,2048]{2,1,0:T(8,128)(2,1)S(1)} %fusion.10.x_ref), custom_call_target="tpu_custom_call" | custom-call | tf_op jit(solution)/shard_map/plane_gather/pallas_call | solution.py:137
  553.0 7.2 fusion.13
  560.2 3.6 convolution_convert_fusion.7
  569.8 19.9 %attend_back.1 = (bf16[2,1024,768]{2,1,0:T(8,128)(2,1)}, f32[8,128]{1,0:T(8,128)S(1)}) custom-call(f32[2,1024,256]{2,1,0:T(8,128)S(1)} %bitcast.107, f32[2,1024,768]{2,1,0:T(8,128)} %fusion.1.p_ref, f32[2,128]{1,0:T(2,128)S(1)} %copy-done.23, f32[1024,128]{1,0:T(8,128)S(1)} %copy-done.11, f32[1024,128]{1,0:T(8,128)S(1)} %copy-done.13, ...), custom_call_target="tpu_custom_call" | custom-call | flops 5368709120 | bytes 16777216 | tf_op jit(solution)/shard_map/attend_back/pallas_call | solution.py:785
  589.7 11.4 %convolution_convert_fusion.5 = bf16[2048,768]{1,0:T(8,128)(2,1)} fusion(bf16[2048,2048]{1,0:T(8,128)(2,1)} %bitcast.143, bf16[2048,768]{1,0:T(8,128)(2,1)} %bitcast.146), kind=kOutput, calls=%fused_computation.11 | convolution fusion | flops 6444023808 | bytes 14680064 | tf_op jit(solution)/shard_map/dot_general | solution.py:1016
  601.2 11.5 %convolution_convert_fusion.1 = bf16[2048,2048]{1,0:T(8,128)(2,1)} fusion(bf16[2048,768]{1,0:T(8,128)(2,1)} %bitcast.147, bf16[2048,768]{1,0:T(8,128)(2,1)} %all-gather.5.cloned.1.call-done), kind=kOutput, calls=%fused_computation.1 | convolution fusion | flops 6446645248 | bytes 14680064 | tf_op jit(solution)/shard_map/dot_general | solution.py:1022
  612.8 40.7 %plane_scatter.6 = f32[8,32,2048]{2,1,0:T(8,128)S(1)} custom-call(bf16[8,8,32,2048]{3,2,1,0:T(8,128)(2,1)} %bitcast.111), custom_call_target="tpu_custom_call" | custom-call | tf_op jit(solution)/shard_map/plane_scatter/pallas_call | solution.py:254
  654.8 11.5 %convolution_convert_fusion = bf16[2048,2048]{1,0:T(8,128)(2,1)} fusion(bf16[2048,768]{0,1:T(8,128)(2,1)} %copy-done.37, bf16[2048,768]{1,0:T(8,128)(2,1)} %all-gather.11.cloned.1.call-done), kind=kOutput, calls=%fused_computation | convolution fusion | flops 6446645248 | bytes 14680064 | tf_op jit(solution)/shard_map/dot_general | solution.py:1027
  666.3 40.5 %plane_scatter.7 = f32[8,32,2048]{2,1,0:T(8,128)S(1)} custom-call(bf16[8,8,32,2048]{3,2,1,0:T(8,128)(2,1)} %bitcast.109), custom_call_target="tpu_custom_call" | custom-call | tf_op jit(solution)/shard_map/plane_scatter/pallas_call | solution.py:254
  714.7 64.5 %send_back.2 = (bf16[8,32,2048]{2,1,0:T(8,128)(2,1)S(1)}, bf16[256,12288]{1,0:T(8,128)(2,1)}, bf16[256,6144]{1,0:T(8,128)(2,1)}) custom-call(bf16[2,4,32,2048]{3,2,1,0:T(8,128)(2,1)S(1)} %bitcast.99, bf16[2,256,1536]{2,1,0:T(8,128)(2,1)S(1)} %bitcast.102, bf16[2,256,768]{2,1,0:T(8,128)(2,1)S(1)} %bitcast.104), custom_call_target="tpu_custom_call" | custom-call | tf_op jit(solution)/shard_map/send_back/pallas_call | solution.py:598
  782.9 52.2 %send_back.3 = (bf16[8,32,2048]{2,1,0:T(8,128)(2,1)S(1)}, bf16[256,6144]{1,0:T(8,128)(2,1)}, bf16[256,2048]{1,0:T(8,128)(2,1)S(1)}, f32[8,128]{1,0:T(8,128)S(1)}) custom-call(bf16[2,4,32,2048]{3,2,1,0:T(8,128)(2,1)S(1)} %bitcast.98, bf16[2,256,768]{2,1,0:T(8,128)(2,1)S(1)} %bitcast.103, bf16[2,256,256]{2,1,0:T(8,128)(2,1)S(1)} %bitcast.105, ...), custom_call_target="tpu_custom_call" | custom-call | tf_op jit(solution)/shard_map/send_back/pallas_call | solution.py:598
  835.1 5.5 convert_element_type.143
  840.6 6.4 slice_convert_fusion
  852.6 3.4 convert_element_type.147
  (192 shorter events, 74.4 us)
Async XLA Ops:
  7.2 194.8 %all-gather.5.cloned.1.call-start = ((), (), s32[]{:S(2)}) async-start(), calls=%async_computation.4 | async-start | bytes 3932160 | tf_op jit(solution)/shard_map/all_gather | solution.py:907
  9.4 12.1 %collective-permute-start.3 = (bf16[256,768]{1,0:T(8,128)(2,1)S(1)}, bf16[256,768]{1,0:T(8,128)(2,1)S(1)}, u32[]{:S(2)}, u32[]{:S(2)}) collective-permute-start(bf16[256,768]{1,0:T(8,128)(2,1)S(1)} %pad_maximum_fusion.4), channel_id=1, source_target_pairs={{0,4},{4,0},{1,5},{5,1},{2,6},{6,2},{3,7},{7,3},{8,12},{12,8},{9,1... | collective-permute-start | bytes 1179656 | tf_op jit(solution)/shard_map/ppermute | solution.py:901
  22.6 211.3 %all-gather.7.cloned.1.call-start = ((), (), s32[]{:S(2)}) async-start(), calls=%async_computation.5 | async-start | bytes 1310720 | tf_op jit(solution)/shard_map/all_gather | solution.py:907
  22.6 10.9 %copy-start.44 = (s32[1024]{0:T(1024)S(1)}, s32[1024]{0:T(1024)}, u32[]{:S(2)}) copy-start(s32[1024]{0:T(1024)} %param.17) | copy-start | bytes 12292
  22.6 11.0 %copy-start.39 = (bf16[256,2048]{1,0:T(8,128)(2,1)S(1)}, bf16[256,2048]{1,0:T(8,128)(2,1)}, u32[]{:S(2)}) copy-start(bf16[256,2048]{1,0:T(8,128)(2,1)} %param.15) | copy-start | bytes 3145732
  25.1 8.8 %copy-start.45 = (s32[1024]{0:T(1024)S(1)}, s32[1024]{0:T(1024)}, u32[]{:S(2)}) copy-start(s32[1024]{0:T(1024)} %param.16) | copy-start | bytes 12292
  25.1 8.8 %copy-start.46 = (bf16[256]{0:T(256)(128)(2,1)S(1)}, bf16[256]{0:T(256)(128)(2,1)}, u32[]{:S(2)}) copy-start(bf16[256]{0:T(256)(128)(2,1)} %param.22) | copy-start | bytes 1540
  25.1 8.8 %copy-start.47 = (bf16[256]{0:T(256)(128)(2,1)S(1)}, bf16[256]{0:T(256)(128)(2,1)}, u32[]{:S(2)}) copy-start(bf16[256]{0:T(256)(128)(2,1)} %param.18) | copy-start | bytes 1540
  26.0 168.5 %collective-permute-start.1 = (bf16[256,1536]{1,0:T(8,128)(2,1)}, bf16[256,1536]{1,0:T(8,128)(2,1)}, u32[]{:S(2)}, u32[]{:S(2)}) collective-permute-start(bf16[256,1536]{1,0:T(8,128)(2,1)} %pad_maximum_fusion.1), channel_id=1, source_target_pairs={{0,4},{4,0},{1,5},{5,1},{2,6},{6,2},{3,7},{7,3},{8,12},{12,8},{9,1... | collective-permute-start | bytes 2359304 | tf_op jit(solution)/shard_map/ppermute | solution.py:901
  29.4 162.2 %collective-permute-start = (bf16[256,256]{1,0:T(8,128)(2,1)}, bf16[256,256]{1,0:T(8,128)(2,1)S(1)}, u32[]{:S(2)}, u32[]{:S(2)}) collective-permute-start(bf16[256,256]{1,0:T(8,128)(2,1)} %get-tuple-element.111), channel_id=1, source_target_pairs={{0,4},{4,0},{1,5},{5,1},{2,6},{6,2},{3,7},{7,3},{8,12},{12,8},{9,1... | collective-permute-start | bytes 393224 | tf_op jit(solution)/shard_map/ppermute | solution.py:901
  31.8 160.6 %collective-permute-start.2 = (bf16[256,768]{1,0:T(8,128)(2,1)}, bf16[256,768]{1,0:T(8,128)(2,1)}, u32[]{:S(2)}, u32[]{:S(2)}) collective-permute-start(bf16[256,768]{1,0:T(8,128)(2,1)} %get-tuple-element.101), channel_id=1, source_target_pairs={{0,4},{4,0},{1,5},{5,1},{2,6},{6,2},{3,7},{7,3},{8,12},{12,8},{9,1... | collective-permute-start | bytes 1179656 | tf_op jit(solution)/shard_map/ppermute | solution.py:901
  42.4 150.0 %copy-start.38 = (bf16[1,256,768]{2,1,0:T(8,128)(2,1)S(1)}, bf16[1,256,768]{2,1,0:T(8,128)(2,1)}, u32[]{:S(2)}) copy-start(bf16[1,256,768]{2,1,0:T(8,128)(2,1)} %get-tuple-element.100) | copy-start | bytes 1179652
  189.8 93.7 %copy-start.2 = (bf16[2,4,32,2048]{3,2,1,0:T(8,128)(2,1)}, bf16[2,4,32,2048]{3,2,1,0:T(8,128)(2,1)S(1)}, u32[]{:S(2)}) copy-start(bf16[2,4,32,2048]{3,2,1,0:T(8,128)(2,1)S(1)} %get-tuple-element.52) | copy-start | bytes 3145732
  189.8 321.6 %copy-start.7 = (bf16[2,4,32,2048]{3,2,1,0:T(8,128)(2,1)}, bf16[2,4,32,2048]{3,2,1,0:T(8,128)(2,1)S(1)}, u32[]{:S(2)}) copy-start(bf16[2,4,32,2048]{3,2,1,0:T(8,128)(2,1)S(1)} %get-tuple-element.60) | copy-start | bytes 3145732
  197.3 150.9 %all-gather.9.cloned.1.call-start = ((), (), s32[]{:S(2)}) async-start(), calls=%async_computation.6 | async-start | bytes 7864320 | tf_op jit(solution)/shard_map/all_gather | solution.py:907
  198.1 213.9 %all-gather.11.cloned.1.call-start = ((), (), s32[]{:S(2)}) async-start(), calls=%async_computation.7 | async-start | bytes 3932160 | tf_op jit(solution)/shard_map/all_gather | solution.py:907
  198.2 15.7 %copy-start.22 = (f32[2,128]{1,0:T(2,128)}, f32[2,128]{1,0:T(2,128)S(1)}, u32[]{:S(2)}) copy-start(f32[2,128]{1,0:T(2,128)S(1)} %convert_element_type.120.gain_ref) | copy-start | bytes 3076
  200.6 13.4 %copy-start.10 = (f32[1024,128]{1,0:T(8,128)}, f32[1024,128]{1,0:T(8,128)S(1)}, u32[]{:S(2)}) copy-start(f32[1024,128]{1,0:T(8,128)S(1)} %get-tuple-element.122.cos_ref) | copy-start | bytes 1572868
  200.6 13.4 %copy-start.12 = (f32[1024,128]{1,0:T(8,128)}, f32[1024,128]{1,0:T(8,128)S(1)}, u32[]{:S(2)}) copy-start(f32[1024,128]{1,0:T(8,128)S(1)} %get-tuple-element.123.sin_ref) | copy-start | bytes 1572868
  200.9 82.6 %copy-start.42 = (f32[2,4,32]{2,1,0:T(4,128)}, f32[2,4,32]{2,1,0:T(4,128)S(1)}, u32[]{:S(2)}) copy-start(f32[2,4,32]{2,1,0:T(4,128)S(1)} %add_rsqrt_fusion) | copy-start | bytes 3076
  201.6 509.4 %reduce-scatter.7.cloned.1.call-start = ((), (), s32[]{:S(2)}) async-start(), calls=%async_computation.9 | async-start | bytes 3932160 | tf_op jit(solution)/shard_map/reduce_scatter | solution.py:977
  385.2 325.7 %reduce-scatter.5.cloned.1.call-start = ((), (), s32[]{:S(2)}) async-start(), calls=%async_computation.8 | async-start | bytes 7864320 | tf_op jit(solution)/shard_map/reduce_scatter | solution.py:977
  448.1 332.7 %reduce-scatter.9.cloned.1.call-start = ((), (), s32[]{:S(2)}) async-start(), calls=%async_computation.10 | async-start | bytes 3932160 | tf_op jit(solution)/shard_map/reduce_scatter | solution.py:977
  470.0 40.8 %copy-start.30 = (f32[8,32,2048]{2,1,0:T(8,128)S(1)}, f32[8,32,2048]{2,1,0:T(8,128)}, u32[]{:S(2)}) copy-start(f32[8,32,2048]{2,1,0:T(8,128)} %copy-done.29) | copy-start | bytes 6291460
  512.0 40.9 %copy-start.40 = (bf16[2048,256]{1,0:T(8,128)(2,1)S(1)}, bf16[2048,256]{1,0:T(8,128)(2,1)}, u32[]{:S(2)}) copy-start(bf16[2048,256]{1,0:T(8,128)(2,1)} %all-gather.7.cloned.1.call-done) | copy-start | bytes 3145732
  601.1 179.7 %reduce-scatter.11.cloned.1.call-start = ((), (), s32[]{:S(2)}) async-start(), calls=%async_computation.11 | async-start | bytes 1310720 | tf_op jit(solution)/shard_map/reduce_scatter | solution.py:977
  666.3 40.6 %copy-start.1 = (f32[8,32,2048]{2,1,0:T(8,128)S(1)}, f32[8,32,2048]{2,1,0:T(8,128)}, u32[]{:S(2)}) copy-start(f32[8,32,2048]{2,1,0:T(8,128)} %copy-done) | copy-start | bytes 6291460
  666.3 40.6 %copy-start.3 = (bf16[2,4,32,2048]{3,2,1,0:T(8,128)(2,1)S(1)}, bf16[2,4,32,2048]{3,2,1,0:T(8,128)(2,1)}, u32[]{:S(2)}) copy-start(bf16[2,4,32,2048]{3,2,1,0:T(8,128)(2,1)} %copy-done.2) | copy-start | bytes 3145732
  666.3 40.6 %copy-start.33 = (f32[8,32,2048]{2,1,0:T(8,128)S(1)}, f32[8,32,2048]{2,1,0:T(8,128)}, u32[]{:S(2)}) copy-start(f32[8,32,2048]{2,1,0:T(8,128)} %get-tuple-element.108) | copy-start | bytes 6291460
  666.3 40.6 %copy-start.41 = (f32[8,1,256]{2,1,0:T(1,128)S(1)}, f32[8,1,256]{2,1,0:T(1,128)}, u32[]{:S(2)}) copy-start(f32[8,1,256]{2,1,0:T(1,128)} %get-tuple-element.112) | copy-start | bytes 24580
  666.3 40.6 %copy-start.43 = (f32[2,4,32]{2,1,0:T(4,128)S(1)}, f32[2,4,32]{2,1,0:T(4,128)}, u32[]{:S(2)}) copy-start(f32[2,4,32]{2,1,0:T(4,128)} %copy-done.42) | copy-start | bytes 3076
  782.9 57.7 %slice-start = ((s8[6291456]{0:T(1024)(128)(4,1)}), s8[2097152]{0:T(1024)(128)(4,1)S(1)}, s32[]{:S(2)}) async-start(s8[6291456]{0:T(1024)(128)(4,1)} %bitcast.117), calls=%async_computation.12 | async-start | bytes 4194304
  (31 other events, 72.2 us)
Sparse Core Ops, SparseCore 0:
  22.7 95.7 all-gather.4
  197.5 33.6 all-gather.6
  233.4 114.8 all-gather.8
  350.2 61.7 all-gather.10
  414.1 58.8 reduce-scatter.6
  475.8 110.7 reduce-scatter.4
  601.2 58.3 reduce-scatter.8
  662.5 27.1 reduce-scatter.10

commit v3 on v2

--- a/solution.py
+++ b/solution.py
@@ -123,7 +123,25 @@
             copy.wait_send()
 
 
-def gather_kernel(x_ref, o_ref, local_sem, send_sem, recv_sem):
+def gather_kernel(x_ref, v_ref, o_ref, moved_ref, local_sem, send_sem, recv_sem, *refs):
+    near = plane_neighbours()
+    far, row, core, seq, ctx = place()
+    planes = lax.axis_size("ctx")
+    levels = [(far, row, core, seq, (ctx + k) % planes) for k in range(1, planes)]
+    greet(mates_of((row * 2 + core) * 2 + seq, far, ctx) + levels)
+    gather = Gather(x_ref, o_ref, local_sem, send_sem, recv_sem)
+    mover = Exchange(True, v_ref, moved_ref, *refs)
+    mover.start()
+    gather.start()
+    mover.middle()
+    gather.middle()
+    gather.finish()
+    for k in range(8):
+        mover.received(k)
+    mover.finish()
+
+
+def plain_gather_kernel(x_ref, o_ref, local_sem, send_sem, recv_sem):
     near = plane_neighbours()
     greet([near["c"], near["x"], near["y"]])
     gather = Gather(x_ref, o_ref, local_sem, send_sem, recv_sem)
@@ -132,146 +150,505 @@
     gather.finish()
 
 
-def plane_gather(block):
+def plane_gather(block, values=None):
     groups, rows, width = block.shape
-    return pl.pallas_call(
-        gather_kernel,
-        out_shape=jax.ShapeDtypeStruct((groups, 8, rows, width), block.dtype),
-        in_specs=[pl.BlockSpec(memory_space=pl.ANY)],
-        out_specs=pl.BlockSpec(memory_space=pl.ANY),
-        scratch_shapes=[
-            pltpu.SemaphoreType.DMA,
-            pltpu.SemaphoreType.DMA((9,)),
-            pltpu.SemaphoreType.DMA((9,)),
-        ],
+    dma = pltpu.SemaphoreType.DMA
+    anywhere = pl.BlockSpec(memory_space=pl.ANY)
+    ins = [block]
+    outs = [jax.ShapeDtypeStruct((groups, 8, rows, width), block.dtype)]
+    scratch = [dma, dma((9,)), dma((9,))]
+    if values is not None:
+        ins.append(values)
+        outs.append(exchanged(values, True))
+        scratch += exchange_scratch(values)
+    result = pl.pallas_call(
+        plain_gather_kernel if values is None else gather_kernel,
+        out_shape=tuple(outs),
+        in_specs=[anywhere] * len(ins),
+        out_specs=(anywhere,) * len(outs),
+        scratch_shapes=scratch,
         compiler_params=pltpu.CompilerParams(
-            collective_id=0, has_side_effects=True, vmem_limit_bytes=VMEM_LIMIT
+            collective_id=0 if values is None else 9,
+            has_side_effects=True,
+            vmem_limit_bytes=VMEM_LIMIT,
         ),
         name="plane_gather",
-    )(block)
-
-
-def scatter_kernel(
-    p_ref, o_ref, mine, other, relay, arrived, load_sem, core_sem, core_recv, send_sem, recv_sem
-):
-    near = plane_neighbours()
-    slot, row, core, seq = plane_slots()
-    groups = mine.shape[1]
-    half = groups // 2
-    first = pl.ds(0, half)
-    second = pl.ds(half, groups - half)
-    greet([near["c"], near["x"], near["y"]])
-
-    chips = ((1 - row, 1 - seq), (row, 1 - seq), (1 - row, seq), (row, seq))
-    loads, exchanges = [], []
-    for index, (r, s) in enumerate(chips):
-        exchange = pltpu.make_async_remote_copy(
-            src_ref=p_ref.at[:, slot(r, 1 - core, s)],
-            dst_ref=other.at[index],
-            send_sem=core_sem.at[index],
-            recv_sem=core_recv.at[index],
-            device_id=near["c"],
+    )(*ins)
+    return result[0] if values is None else result
+
+
+class Swap:
+    def __init__(self, plan, weights, pieces, local_sem, send_sem, recv_sem):
+        _, row, core, seq, _ = place()
+        self.own = (row * 2 + core) * 2 + seq
+        self.side = (row * 2 + core) * 2 + 1 - seq
+        self.seq, self.plan, self.weights, self.pieces = seq, plan, weights, pieces
+        self.local_sem = local_sem
+        self.send = sender(plane_neighbours(), send_sem, recv_sem)
+        self.local, self.sent = {}, {}
+
+    def start(self, index):
+        weight, base, width, piece, offset = self.plan[index]
+        target = self.pieces[piece].at[self.seq, :, pl.ds(offset, width)]
+
+        def source(rank):
+            start = pl.multiple_of(base + rank * width, 128)
+            return self.weights[weight].at[:, pl.ds(start, width)]
+
+        self.sent[index] = self.send(index, source(self.side), target, "x")
+        self.local[index] = pltpu.make_async_copy(
+            source(self.own), target, self.local_sem.at[index]
+        )
+        self.local[index].start()
+
+    def finish(self, index):
+        self.local[index].wait()
+        self.sent[index].wait_recv()
+        self.sent[index].wait_send()
+
+
+class Scatter:
+    def __init__(self, mine, theirs, other, relay, arrived, core_sem, core_recv, send_sem, recv_sem):
+        self.near = plane_neighbours()
+        slot, row, core, seq = plane_slots()
+        chips = ((1 - row, 1 - seq), (row, 1 - seq), (1 - row, seq), (row, seq))
+        self.order = [slot(r, c, s) for r, s in chips for c in (1 - core, core)]
+        self.mine, self.theirs, self.other = mine, theirs, other
+        self.relay, self.arrived = relay, arrived
+        self.core_sem, self.core_recv = core_sem, core_recv
+        self.send = sender(self.near, send_sem, recv_sem)
+        self.groups = mine.shape[1]
+        self.half = self.groups // 2
+        self.first = pl.ds(0, self.half)
+        self.second = pl.ds(self.half, self.groups - self.half)
+
+    def exchange(self, produce, index):
+        produce(2 * index, self.theirs.at[index])
+        copy = pltpu.make_async_remote_copy(
+            src_ref=self.theirs.at[index],
+            dst_ref=self.other.at[index],
+            send_sem=self.core_sem.at[index],
+            recv_sem=self.core_recv.at[index],
+            device_id=self.near["c"],
             device_id_type=MESH,
         )
-        exchange.start()
-        load = pltpu.make_async_copy(
-            p_ref.at[:, slot(r, core, s)], mine.at[index], load_sem.at[index]
-        )
-        load.start()
-        loads.append(load)
-        exchanges.append(exchange)
-
-    def chip_sum(index):
-        loads[index].wait()
-        exchanges[index].wait_recv()
+        copy.start()
+        self.exchanges.append(copy)
+        produce(2 * index + 1, self.mine.at[index])
+
+    def chip_sum(self, index):
+        self.exchanges[index].wait_recv()
+        mine, other = self.mine, self.other
 
         def body(g, carry):
             total = mine[index, g].astype(jnp.float32) + other[index, g].astype(jnp.float32)
             mine[index, g] = total.astype(mine.dtype)
             return carry
 
-        lax.fori_loop(0, groups, body, 0)
-
-    def send(index, source, target, to):
-        copy = pltpu.make_async_remote_copy(
-            src_ref=source,
-            dst_ref=target,
-            send_sem=send_sem.at[index],
-            recv_sem=recv_sem.at[index],
-            device_id=near[to],
-            device_id_type=MESH,
-        )
-        copy.start()
-        return copy
-
-    def relay_sum(index, which, start):
+        lax.fori_loop(0, self.groups, body, 0)
+
+    def relay_sum(self, index, which, start):
+        mine, relay = self.mine, self.relay
+
         def body(g, carry):
             total = mine[index, g + start].astype(jnp.float32) + relay[which, g].astype(jnp.float32)
             mine[index, g + start] = total.astype(mine.dtype)
             return carry
 
-        lax.fori_loop(0, half, body, 0)
-
-    chip_sum(0)
-    diag_x = send(0, mine.at[0, first], relay.at[0], "x")
-    diag_y = send(1, mine.at[0, second], relay.at[1], "y")
-    chip_sum(1)
-    plain_x = send(2, mine.at[1, first], arrived.at[0, first], "x")
-    chip_sum(2)
-    plain_y = send(3, mine.at[2, second], arrived.at[1, second], "y")
-    diag_x.wait_recv()
-    relay_sum(2, 0, 0)
-    joint_y = send(4, mine.at[2, first], arrived.at[1, first], "y")
-    diag_y.wait_recv()
-    relay_sum(1, 1, half)
-    joint_x = send(5, mine.at[1, second], arrived.at[0, second], "x")
-    loads[3].wait()
-    exchanges[3].wait_recv()
-    plain_x.wait_recv()
-    plain_y.wait_recv()
-    joint_x.wait_recv()
-    joint_y.wait_recv()
-
-    def body(g, carry):
-        o_ref[g] = (
-            mine[3, g].astype(jnp.float32)
-            + other[3, g].astype(jnp.float32)
-            + arrived[0, g].astype(jnp.float32)
-            + arrived[1, g].astype(jnp.float32)
+        lax.fori_loop(0, self.half, body, 0)
+
+    def start(self, produce):
+        mine, relay, arrived, send = self.mine, self.relay, self.arrived, self.send
+        first, second = self.first, self.second
+        self.exchanges = []
+        self.exchange(produce, 0)
+        self.chip_sum(0)
+        self.diag_x = send(0, mine.at[0, first], relay.at[0], "x")
+        self.diag_y = send(1, mine.at[0, second], relay.at[1], "y")
+        self.exchange(produce, 1)
+        self.chip_sum(1)
+        self.plain_x = send(2, mine.at[1, first], arrived.at[0, first], "x")
+        self.exchange(produce, 2)
+        self.chip_sum(2)
+        self.plain_y = send(3, mine.at[2, second], arrived.at[1, second], "y")
+        self.exchange(produce, 3)
+
+    def middle(self):
+        mine, arrived, send = self.mine, self.arrived, self.send
+        first, second = self.first, self.second
+        self.diag_x.wait_recv()
+        self.relay_sum(2, 0, 0)
+        self.joint_y = send(4, mine.at[2, first], arrived.at[1, first], "y")
+        self.diag_y.wait_recv()
+        self.relay_sum(1, 1, self.half)
+        self.joint_x = send(5, mine.at[1, second], arrived.at[0, second], "x")
+
+    def finish(self, o_ref):
+        mine, other, arrived = self.mine, self.other, self.arrived
+        self.exchanges[3].wait_recv()
+        for copy in (self.plain_x, self.plain_y, self.joint_x, self.joint_y):
+            copy.wait_recv()
+
+        def body(g, carry):
+            o_ref[g] = (
+                mine[3, g].astype(jnp.float32)
+                + other[3, g].astype(jnp.float32)
+                + arrived[0, g].astype(jnp.float32)
+                + arrived[1, g].astype(jnp.float32)
+            )
+            return carry
+
+        lax.fori_loop(0, self.groups, body, 0)
+        for copy in self.exchanges:
+            copy.wait_send()
+        for copy in (
+            self.diag_x, self.diag_y, self.plain_x, self.plain_y, self.joint_x, self.joint_y
+        ):
+            copy.wait_send()
+
+
+def scatter_scratch(groups, rows, width, kind):
+    dma = pltpu.SemaphoreType.DMA
+    return [
+        pltpu.VMEM((4, groups, rows, width), kind),
+        pltpu.VMEM((4, groups, rows, width), kind),
+        pltpu.VMEM((4, groups, rows, width), kind),
+        pltpu.VMEM((2, groups // 2, rows, width), kind),
+        pltpu.VMEM((2, groups, rows, width), kind),
+        dma((4,)),
+        dma((4,)),
+        dma((6,)),
+        dma((6,)),
+    ]
+
+
+def multiply_into(block, w_buf, target):
+    groups, rows, width = target.shape
+    columns = min(512, width)
+
+    def body(n, carry):
+        start = pl.multiple_of(n * columns, columns)
+        out = lax.dot_general(
+            block,
+            w_buf[pl.ds(start, columns), :],
+            contract_cols,
+            preferred_element_type=jnp.float32,
+        )
+        target[:, :, pl.ds(start, columns)] = out.astype(target.dtype).reshape(
+            groups, rows, columns
         )
         return carry
 
-    lax.fori_loop(0, groups, body, 0)
-    for copy in exchanges:
-        copy.wait_send()
-    for copy in (diag_x, diag_y, plain_x, plain_y, joint_x, joint_y):
-        copy.wait_send()
-
-
-def plane_scatter(partial_sums):
-    groups, _, rows, width = partial_sums.shape
-    kind = partial_sums.dtype
+    lax.fori_loop(0, width // columns, body, 0)
+
+
+def scatter_kernel(outward, swap_plan, *refs):
+    if outward is None:
+        a_ref, w_ref, o_ref, *refs = refs
+    elif swap_plan is None:
+        a_ref, w_ref, v_ref, o_ref, moved_ref, *refs = refs
+    else:
+        a_ref, w_ref, v_ref, swap_ref, o_ref, moved_ref, piece_ref, *refs = refs
+    scatter = Scatter(*refs[:9])
+    a_buf, w_buf, a_sem, w_sem, *refs = refs[9:]
+    w_load = pltpu.make_async_copy(w_ref, w_buf, w_sem)
+    w_load.start()
+    loads = [
+        pltpu.make_async_copy(a_ref.at[:, slot], a_buf.at[k], a_sem.at[k])
+        for k, slot in enumerate(scatter.order)
+    ]
+    for load in loads:
+        load.start()
+    near = scatter.near
+    if outward is None:
+        greet([near["c"], near["x"], near["y"]])
+    else:
+        far, row, core, seq, ctx = place()
+        planes = lax.axis_size("ctx")
+        levels = [(far, row, core, seq, (ctx + k) % planes) for k in range(1, planes)]
+        greet(mates_of((row * 2 + core) * 2 + seq, far, ctx) + levels)
+        mover = Exchange(outward, v_ref, moved_ref, *refs[:3])
+        mover.start()
+        if swap_plan is not None:
+            swap = Swap(swap_plan, [swap_ref], [piece_ref], *refs[3:])
+            swap.start(0)
+
+    def produce(index, target):
+        loads[index].wait()
+        groups, rows, _ = target.shape
+        multiply_into(a_buf[index].reshape(groups * rows, a_buf.shape[-1]), w_buf, target)
+
+    w_load.wait()
+    scatter.start(produce)
+    if outward:
+        mover.middle()
+    scatter.middle()
+    if outward is False:
+        mover.middle()
+    scatter.finish(o_ref)
+    if outward is not None:
+        for k in range(8):
+            mover.received(k)
+        mover.finish()
+    if swap_plan is not None:
+        swap.finish(0)
+
+
+def exchanged(values, outward):
+    planes = lax.axis_size("ctx")
+    lead = (8 // planes, planes) if outward else (8,)
+    return jax.ShapeDtypeStruct(lead + values.shape[-2:], values.dtype)
+
+
+def exchange_scratch(values):
+    dma = pltpu.SemaphoreType.DMA
+    return [pltpu.VMEM((8,) + values.shape[-2:], values.dtype), dma((16,)), dma((16,))]
+
+
+def multiply_scatter(identity, a, weight, values=None, outward=None, swap=None, swap_plan=None):
+    groups, _, rows, depth = a.shape
+    width = weight.shape[0]
+    kind = a.dtype
+    dma = pltpu.SemaphoreType.DMA
+    anywhere = pl.BlockSpec(memory_space=pl.ANY)
+    outs = [jax.ShapeDtypeStruct((groups, rows, width), jnp.float32)]
+    out_specs = [pl.BlockSpec(memory_space=pltpu.VMEM)]
+    scratch = scatter_scratch(groups, rows, width, kind) + [
+        pltpu.VMEM((8, groups, rows, depth), kind),
+        pltpu.VMEM(weight.shape, kind),
+        dma((8,)),
+        dma,
+    ]
+    ins = [a, weight]
+    if outward is not None:
+        ins.append(values)
+        outs.append(exchanged(values, outward))
+        out_specs.append(anywhere)
+        scratch += exchange_scratch(values)
+    if swap is not None:
+        ins.append(swap)
+        outs.append(jax.ShapeDtypeStruct((2, swap.shape[0], swap_plan[0][2]), swap.dtype))
+        out_specs.append(anywhere)
+        scratch += [dma((1,)), dma((1,)), dma((1,))]
+    result = pl.pallas_call(
+        functools.partial(scatter_kernel, outward, swap_plan),
+        out_shape=tuple(outs),
+        in_specs=[anywhere] * len(ins),
+        out_specs=tuple(out_specs),
+        scratch_shapes=scratch,
+        compiler_params=pltpu.CompilerParams(
+            collective_id=identity, has_side_effects=True, vmem_limit_bytes=VMEM_LIMIT
+        ),
+        cost_estimate=pl.CostEstimate(
+            flops=16 * groups * rows * width * depth,
+            bytes_accessed=16 * groups * rows * (width + depth),
+            transcendentals=0,
+        ),
+        name="multiply_scatter",
+    )(*ins)
+    return result[0] if outward is None else result
+
+
+def silu_parts(linear):
+    part = linear.shape[-1] // 2
+    gate, up = linear[:, :part], linear[:, part:]
+    sig = jax.nn.sigmoid(gate)
+    return gate, up, sig, gate * sig
+
+
+def forward_kernel(
+    x_ref, h_ref, w_ref, x_all, lin_ref, hid_ref,
+    local_sem, send_sem, recv_sem, h_buf, w_buf, lin_buf, hid_buf, h_sem, w_sem, out_sem,
+):
+    near = plane_neighbours()
+    w_load = pltpu.make_async_copy(w_ref, w_buf, w_sem)
+    w_load.start()
+
+    def load(d, slot):
+        return pltpu.make_async_copy(h_ref.at[:, d], h_buf.at[slot], h_sem.at[slot])
+
+    def stores(d, slot):
+        return (
+            pltpu.make_async_copy(lin_buf.at[slot], lin_ref.at[:, d], out_sem.at[0, slot]),
+            pltpu.make_async_copy(hid_buf.at[slot], hid_ref.at[:, d], out_sem.at[1, slot]),
+        )
+
+    load(0, 0).start()
+    greet([near["c"], near["x"], near["y"]])
+    gather = Gather(x_ref, x_all, local_sem, send_sem, recv_sem)
+    gather.start()
+    w_load.wait()
+    groups, rows, depth = h_buf.shape[1:]
+    part = hid_buf.shape[-1]
+
+    def body(d, carry):
+        slot = lax.rem(d, 2)
+        load(d, slot).wait()
+
+        @pl.when(d < 7)
+        def _():
+            load(d + 1, 1 - slot).start()
+
+        @pl.when(d > 1)
+        def _():
+            for store in stores(d - 2, slot):
+                store.wait()
+
+        block = h_buf[slot].reshape(groups * rows, depth)
+        gate = jnp.dot(block, w_buf[:, :part], preferred_element_type=jnp.float32)
+        up = jnp.dot(block, w_buf[:, part:], preferred_element_type=jnp.float32)
+        lin_buf[slot, :, :, :part] = gate.reshape(groups, rows, part)
+        lin_buf[slot, :, :, part:] = up.reshape(groups, rows, part)
+        hidden = gate * jax.nn.sigmoid(gate) * up
+        hid_buf[slot] = hidden.astype(hid_buf.dtype).reshape(groups, rows, part)
+        for store in stores(d, slot):
+            store.start()
+        return carry
+
+    lax.fori_loop(0, 8, body, 0)
+    gather.middle()
+    for d in (6, 7):
+        for store in stores(d, d % 2):
+            store.wait()
+    gather.finish()
+
+
+def gather_and_feed(block, normed, weight):
+    groups, rows, width = block.shape
+    kind = block.dtype
+    both = weight.shape[1]
+    dma = pltpu.SemaphoreType.DMA
+    anywhere = pl.BlockSpec(memory_space=pl.ANY)
     return pl.pallas_call(
-        scatter_kernel,
-        out_shape=jax.ShapeDtypeStruct((groups, rows, width), jnp.float32),
-        in_specs=[pl.BlockSpec(memory_space=pl.ANY)],
-        out_specs=pl.BlockSpec(memory_space=pltpu.VMEM),
+        forward_kernel,
+        out_shape=(
+            jax.ShapeDtypeStruct((groups, 8, rows, width), kind),
+            jax.ShapeDtypeStruct((groups, 8, rows, both), jnp.float32),
+            jax.ShapeDtypeStruct((groups, 8, rows, both // 2), kind),
+        ),
+        in_specs=[anywhere] * 3,
+        out_specs=(anywhere,) * 3,
         scratch_shapes=[
-            pltpu.VMEM((4, groups, rows, width), kind),
-            pltpu.VMEM((4, groups, rows, width), kind),
-            pltpu.VMEM((2, groups // 2, rows, width), kind),
+            dma,
+            dma((9,)),
+            dma((9,)),
             pltpu.VMEM((2, groups, rows, width), kind),
-            pltpu.SemaphoreType.DMA((4,)),
-            pltpu.SemaphoreType.DMA((4,)),
-            pltpu.SemaphoreType.DMA((4,)),
-            pltpu.SemaphoreType.DMA((6,)),
-            pltpu.SemaphoreType.DMA((6,)),
+            pltpu.VMEM(weight.shape, kind),
+            pltpu.VMEM((2, groups, rows, both), jnp.float32),
+            pltpu.VMEM((2, groups, rows, both // 2), kind),
+            dma((2,)),
+            dma,
+            dma((2, 2)),
+        ],
+        compiler_params=pltpu.CompilerParams(
+            collective_id=8, has_side_effects=True, vmem_limit_bytes=VMEM_LIMIT
+        ),
+        cost_estimate=pl.CostEstimate(
+            flops=16 * groups * rows * width * both,
+            bytes_accessed=16 * groups * rows * (width + both),
+            transcendentals=4 * groups * rows * both,
+        ),
+        name="gather_and_feed",
+    )(block, normed, weight)
+
+
+def backward_kernel(
+    g_ref, lin_ref, down_ref, up_ref, o_ref, d_ref, *refs,
+):
+    scatter = Scatter(*refs[:9])
+    g_buf, lin_buf, d_buf, down_buf, up_buf, g_sem, lin_sem, d_sem, w_sem = refs[9:]
+    weights = (
+        pltpu.make_async_copy(down_ref, down_buf, w_sem.at[0]),
+        pltpu.make_async_copy(up_ref, up_buf, w_sem.at[1]),
+    )
+
+    def loads(index):
+        slot, d = index % 2, scatter.order[index]
+        return (
+            pltpu.make_async_copy(g_ref.at[:, d], g_buf.at[slot], g_sem.at[slot]),
+            pltpu.make_async_copy(lin_ref.at[:, d], lin_buf.at[slot], lin_sem.at[slot]),
+        )
+
+    def store(index):
+        slot, d = index % 2, scatter.order[index]
+        return pltpu.make_async_copy(d_buf.at[slot], d_ref.at[:, d], d_sem.at[slot])
+
+    weights[0].start()
+    for copy in loads(0):
+        copy.start()
+    weights[1].start()
+    near = scatter.near
+    greet([near["c"], near["x"], near["y"]])
+    for copy in weights:
+        copy.wait()
+    part = down_buf.shape[1]
+
+    def produce(index, target):
+        slot = index % 2
+        for copy in loads(index):
+            copy.wait()
+        if index < 7:
+            for copy in loads(index + 1):
+                copy.start()
+        if index > 1:
+            store(index - 2).wait()
+        groups, rows, width = target.shape
+        d_hidden = jnp.dot(
+            g_buf[slot].reshape(groups * rows, width),
+            down_buf[...],
+            preferred_element_type=jnp.float32,
+        )
+        gate, up, sig, silu = silu_parts(lin_buf[slot].reshape(groups * rows, 2 * part))
+        d_gate = d_hidden * up * sig * (1.0 + gate * (1.0 - sig))
+        d_up = d_hidden * silu
+        d_buf[slot, :, :, :part] = d_gate.astype(d_buf.dtype).reshape(groups, rows, part)
+        d_buf[slot, :, :, part:] = d_up.astype(d_buf.dtype).reshape(groups, rows, part)
+        store(index).start()
+        multiply_into(d_buf[slot].reshape(groups * rows, 2 * part), up_buf, target)
+
+    scatter.start(produce)
+    scatter.middle()
+    for index in (6, 7):
+        store(index).wait()
+    scatter.finish(o_ref)
+
+
+def feed_back(grads, linear, down, up):
+    groups, _, rows, width = grads.shape
+    kind = grads.dtype
+    both = up.shape[1]
+    dma = pltpu.SemaphoreType.DMA
+    anywhere = pl.BlockSpec(memory_space=pl.ANY)
+    return pl.pallas_call(
+        backward_kernel,
+        out_shape=(
+            jax.ShapeDtypeStruct((groups, rows, width), jnp.float32),
+            jax.ShapeDtypeStruct((groups, 8, rows, both), kind),
+        ),
+        in_specs=[anywhere] * 4,
+        out_specs=(pl.BlockSpec(memory_space=pltpu.VMEM), anywhere),
+        scratch_shapes=scatter_scratch(groups, rows, width, kind)
+        + [
+            pltpu.VMEM((2, groups, rows, width), kind),
+            pltpu.VMEM((2, groups, rows, both), jnp.float32),
+            pltpu.VMEM((2, groups, rows, both), kind),
+            pltpu.VMEM(down.shape, kind),
+            pltpu.VMEM(up.shape, kind),
+            dma((2,)),
+            dma((2,)),
+            dma((2,)),
+            dma((2,)),
         ],
         compiler_params=pltpu.CompilerParams(
             collective_id=1, has_side_effects=True, vmem_limit_bytes=VMEM_LIMIT
         ),
-        name="plane_scatter",
-    )(partial_sums)
+        cost_estimate=pl.CostEstimate(
+            flops=24 * groups * rows * width * both,
+            bytes_accessed=16 * groups * rows * (2 * width + 3 * both),
+            transcendentals=4 * groups * rows * both,
+        ),
+        name="feed_back",
+    )(grads, linear, down, up)
 
 
 class Exchange:
@@ -403,13 +780,59 @@
     ]
 
 
+class Line:
+    def __init__(self, full, up_send, down_send, recv_sem):
+        self.far, self.row, self.core, self.seq, self.ctx = place()
+        self.planes = lax.axis_size("ctx")
+        self.full, self.recv_sem = full, recv_sem
+        self.sems = {1: up_send, -1: down_send}
+        self.sent = []
+
+    def pass_on(self, plane, k, step, valid):
+        target = self.ctx + step
+        valid = valid & (target >= 0) & (target < self.planes)
+        index = jnp.clip(plane, 0, self.planes - 1)
+        part = self.full.at[index, k]
+        copy = pltpu.make_async_remote_copy(
+            src_ref=part,
+            dst_ref=part,
+            send_sem=self.sems[step].at[index, k],
+            recv_sem=self.recv_sem.at[index, k],
+            device_id=(
+                self.far, self.row, self.core, self.seq, jnp.clip(target, 0, self.planes - 1)
+            ),
+            device_id_type=MESH,
+        )
+        pl.when(valid)(copy.start)
+        self.sent.append((valid, copy))
+
+    def begin(self, k):
+        for step in (1, -1):
+            self.pass_on(self.ctx, k, step, self.ctx >= 0)
+
+    def hop(self, distance, k):
+        for step in (1, -1):
+            plane = self.ctx - step * distance
+            valid = (plane >= 0) & (plane < self.planes)
+            index = jnp.clip(plane, 0, self.planes - 1)
+            part = self.full.at[index, k]
+            wait = pltpu.make_async_copy(part, part, self.recv_sem.at[index, k]).wait
+            pl.when(valid)(wait)
+            self.pass_on(plane, k, step, valid)
+
+    def finish(self):
+        for valid, copy in self.sent:
+            pl.when(valid)(copy.wait_send)
+
+
 def prologue_kernel(
-    tokens_ref, cot_ref, layout_ref, gain_ref,
-    own_tokens, own_cot, normed_all, cot_all, lay_out, gain_out,
+    weight_plan, planes,
+    tokens_ref, layout_ref, gain_ref, proj_ref, out_ref, gate_ref, up_ref,
+    own_tokens, normed_all, lay_out, gain_out, proj_full, out_piece, up_piece,
     normed, stage, small_send, small_recv, ex_send, ex_recv, local_sem, g_send, g_recv,
+    w_local, w_send, w_recv, up_send, line_down, line_recv,
 ):
     far, row, core, seq, ctx = place()
-    planes = lax.axis_size("ctx")
     own = (row * 2 + core) * 2 + seq
     mates = mates_of(own, far, ctx)
     line = ctx * 2 + seq
@@ -418,6 +841,15 @@
         (far, row, core, (line + k) % 2, ((line + k) % total) // 2) for k in range(1, total)
     ]
     greet(mates + owners)
+    weights = {"proj": proj_ref, "out": out_ref, "gate": gate_ref, "up": up_ref}
+    pieces = {"proj": proj_full.at[ctx], "out": out_piece, "up": up_piece}
+    swap = Swap(weight_plan, weights, pieces, w_local, w_send, w_recv)
+    proj_parts = [i for i, plan in enumerate(weight_plan) if plan[0] == "proj"]
+    other_parts = [i for i, plan in enumerate(weight_plan) if plan[0] != "proj"]
+    for index in proj_parts:
+        swap.start(index)
+    tokens = Exchange(True, tokens_ref, own_tokens, stage, ex_send, ex_recv)
+    tokens.start()
     lay_out[own] = layout_ref[...]
     gain_out[line] = gain_ref[...]
     send = sender({}, small_send, small_recv)
@@ -427,95 +859,109 @@
         send(len(owners) + k, layout_ref, lay_out.at[own], device)
         for k, device in enumerate(mates)
     ]
-    tokens = Exchange(True, tokens_ref, own_tokens, stage.at[0], ex_send.at[0], ex_recv.at[0])
-    cots = Exchange(True, cot_ref, own_cot, stage.at[1], ex_send.at[1], ex_recv.at[1])
-    tokens.start()
+    relay = Line(proj_full, up_send, line_down, line_recv)
+    for index in proj_parts:
+        swap.local[index].wait()
+    relay.begin(seq)
     tokens.middle()
-    cots.start()
+    for index in other_parts:
+        swap.start(index)
+    for index in proj_parts:
+        swap.sent[index].wait_recv()
+    relay.begin(1 - seq)
     for copy in small[: len(owners)]:
         copy.wait_recv()
     gain_rows = own_tokens.shape[-1] // total // 128
-    pieces = [
-        gain_out[owner, r : r + 1, :] for owner in range(total) for r in range(gain_rows)
-    ]
-    gain_row = jnp.concatenate(pieces, axis=1)
+    gain_row = jnp.concatenate(
+        [gain_out[owner, r : r + 1, :] for owner in range(total) for r in range(gain_rows)],
+        axis=1,
+    )
     for k in range(8):
         tokens.received(k)
-        s, z = k // planes, k % planes
-        wide = own_tokens[s, z].astype(jnp.float32)
+        wide = own_tokens[k // planes, k % planes].astype(jnp.float32)
         root = lax.rsqrt(jnp.mean(wide * wide, axis=1, keepdims=True) + norm_epsilon)
         normed[k] = (wide * root * gain_row).astype(normed.dtype)
-    first = Gather(normed, normed_all, local_sem.at[0], g_send.at[0], g_recv.at[0])
-    second = Gather(
-        own_cot.reshape(normed.shape), cot_all, local_sem.at[1], g_send.at[1], g_recv.at[1]
-    )
-    first.start()
-    cots.middle()
-    first.middle()
-    for k in range(8):
-        cots.received(k)
-    second.start()
-    first.finish()
-    second.middle()
-    second.finish()
+    gather = Gather(normed, normed_all, local_sem, g_send, g_recv)
+    gather.start()
+    for k in range(2):
+        relay.hop(1, k)
+    gather.middle()
+    for distance in range(2, planes):
+        for k in range(2):
+            relay.hop(distance, k)
+    gather.finish()
+    relay.finish()
+    for index in other_parts:
+        swap.finish(index)
+    for index in proj_parts:
+        swap.sent[index].wait_send()
     for copy in small[len(owners) :]:
         copy.wait_recv()
     for copy in small:
         copy.wait_send()
     tokens.finish()
-    cots.finish()
-
-
-def prologue(tokens, cotangents, layout, gains):
+
+
+def prologue(tokens, layout, gains, weights, weight_plan, widths):
     planes = lax.axis_size("ctx")
     rows, width = tokens.shape[-2:]
     kind = tokens.dtype
+    shard_rows = weights[0].shape[0]
     count = 7 + 2 * planes - 1
+    plan_count = len(weight_plan)
     vmem = pl.BlockSpec(memory_space=pltpu.VMEM)
     anywhere = pl.BlockSpec(memory_space=pl.ANY)
+    dma = pltpu.SemaphoreType.DMA
+    pieces = [(planes, 2, shard_rows, widths[0])] + [(2, shard_rows, w) for w in widths[1:]]
     return pl.pallas_call(
-        prologue_kernel,
+        functools.partial(prologue_kernel, weight_plan, planes),
         out_shape=(
             jax.ShapeDtypeStruct((8 // planes, planes, rows, width), kind),
-            jax.ShapeDtypeStruct((8 // planes, planes, rows, width), kind),
-            jax.ShapeDtypeStruct((8, 8, rows, width), kind),
             jax.ShapeDtypeStruct((8, 8, rows, width), kind),
             jax.ShapeDtypeStruct((8,) + layout.shape, layout.dtype),
             jax.ShapeDtypeStruct((2 * planes,) + gains.shape, gains.dtype),
-        ),
-        in_specs=[anywhere, anywhere, vmem, vmem],
-        out_specs=(vmem, vmem, anywhere, anywhere, vmem, vmem),
+        )
+        + tuple(jax.ShapeDtypeStruct(piece, kind) for piece in pieces),
+        in_specs=[anywhere, vmem, vmem] + [anywhere] * 4,
+        out_specs=(vmem, anywhere, vmem, vmem) + (anywhere,) * 3,
         scratch_shapes=[
             pltpu.VMEM((8, rows, width), kind),
-            pltpu.VMEM((2, 8, rows, width), kind),
-            pltpu.SemaphoreType.DMA((count,)),
-            pltpu.SemaphoreType.DMA((count,)),
-            pltpu.SemaphoreType.DMA((2, 16)),
-            pltpu.SemaphoreType.DMA((2, 16)),
-            pltpu.SemaphoreType.DMA((2,)),
-            pltpu.SemaphoreType.DMA((2, 9)),
-            pltpu.SemaphoreType.DMA((2, 9)),
+            pltpu.VMEM((8, rows, width), kind),
+            dma((count,)),
+            dma((count,)),
+            dma((16,)),
+            dma((16,)),
+            dma,
+            dma((9,)),
+            dma((9,)),
+            dma((plan_count,)),
+            dma((plan_count,)),
+            dma((plan_count,)),
+            dma((planes, 2)),
+            dma((planes, 2)),
+            dma((planes, 2)),
         ],
         compiler_params=pltpu.CompilerParams(
             collective_id=2, has_side_effects=True, vmem_limit_bytes=VMEM_LIMIT
         ),
         name="prologue",
-    )(tokens, cotangents, layout, gains)
-
-
-def return_kernel(
-    plans, with_sum, *refs,
-):
+    )(tokens, layout, gains, *weights)
+
+
+def return_kernel(plans, with_values, with_sum, *refs):
     count = len(plans)
-    v_ref, *refs = refs
+    if with_values:
+        v_ref, *refs = refs
     r_refs, refs = refs[:count], refs[count:]
     if with_sum:
         small_ref, *refs = refs
-    o_ref, *refs = refs
+    if with_values:
+        o_ref, *refs = refs
     g_refs, refs = refs[:count], refs[count:]
     if with_sum:
         sum_ref, *refs = refs
-    stage, ex_send, ex_recv, *refs = refs
+    if with_values:
+        stage, ex_send, ex_recv, *refs = refs
     row_sems, refs = refs[: 3 * count], refs[3 * count :]
     far, row, core, seq, ctx = place()
     planes = lax.axis_size("ctx")
@@ -523,14 +969,16 @@
     mates = mates_of(own, far, ctx)
     levels = [(far, row, core, seq, (ctx + k) % planes) for k in range(1, planes)]
     greet(mates + levels)
-    exchange = Exchange(False, v_ref, o_ref, stage, ex_send, ex_recv)
+    if with_values:
+        exchange = Exchange(False, v_ref, o_ref, stage, ex_send, ex_recv)
     rows = [
         Rows(plan, r_refs[i], g_refs[i], *row_sems[3 * i : 3 * i + 3])
         for i, plan in enumerate(plans)
     ]
     for part in rows:
         part.start()
-    exchange.start()
+    if with_values:
+        exchange.start()
     if with_sum:
         line, got, sum_send, sum_recv = refs
         send = sender({}, sum_send, sum_recv)
@@ -550,12 +998,14 @@
         ]
     for part in rows:
         part.middle()
-    exchange.middle()
+    if with_values:
+        exchange.middle()
     for part in rows:
         part.finish()
-    for k in range(8):
-        exchange.received(k)
-    exchange.finish()
+    if with_values:
+        for k in range(8):
+            exchange.received(k)
+        exchange.finish()
     if with_sum:
         for copy in more:
             copy.wait_recv()
@@ -569,19 +1019,21 @@
 
 def send_back(values, parts, plans, widths, small, identity):
     planes = lax.axis_size("ctx")
-    rows, width = values.shape[-2:]
-    kind = values.dtype
     vmem = pl.BlockSpec(memory_space=pltpu.VMEM)
     anywhere = pl.BlockSpec(memory_space=pl.ANY)
     dma = pltpu.SemaphoreType.DMA
-    outs = [jax.ShapeDtypeStruct((8, rows, width), kind)] + [
+    outs = [
         jax.ShapeDtypeStruct((part.shape[1], total), part.dtype)
         for part, total in zip(parts, widths)
     ]
-    scratch = [pltpu.VMEM((8, rows, width), kind), dma((16,)), dma((16,))]
+    ins, scratch = list(parts), []
+    if values is not None:
+        moved = jax.ShapeDtypeStruct((8,) + values.shape[-2:], values.dtype)
+        outs.insert(0, moved)
+        ins.insert(0, values)
+        scratch += [pltpu.VMEM(moved.shape, moved.dtype), dma((16,)), dma((16,))]
     for plan in plans:
         scratch += [dma((len(plan),)), dma((7 * len(plan),)), dma((7 * len(plan),))]
-    ins = [values, *parts]
     in_specs = [anywhere] * len(ins)
     out_specs = [anywhere] * len(outs)
     if small is not None:
@@ -596,7 +1048,7 @@
             dma((planes + 6,)),
         ]
     return pl.pallas_call(
-        functools.partial(return_kernel, plans, small is not None),
+        functools.partial(return_kernel, plans, values is not None, small is not None),
         out_shape=tuple(outs),
         in_specs=in_specs,
         out_specs=tuple(out_specs),
@@ -845,62 +1297,27 @@
     f32 = jnp.float32
     bf16 = jnp.bfloat16
 
+    def reorder(values, order):
+        return jnp.concatenate(
+            [values[..., k * shard_rows : (k + 1) * shard_rows] for k in order], axis=-1
+        )
+
     def to_inner(values):
-        return (
-            values.reshape(values.shape[0], seqs, planes, shard_rows)
-            .transpose(0, 2, 1, 3)
-            .reshape(values.shape)
-        )
+        return reorder(values, [x * planes + z for z in range(planes) for x in range(seqs)])
 
     def to_outer(values):
-        return (
-            values.reshape(values.shape[0], planes, seqs, shard_rows)
-            .transpose(0, 2, 1, 3)
-            .reshape(values.shape)
-        )
-
-    def gathered(block):
-        return plane_gather(block).reshape(plane_tokens, model_width)
-
-    def scattered(partial_rows):
-        return plane_scatter(
-            partial_rows.astype(bf16).reshape(groups, plane_size, chunk, model_width)
-        )
-
-    def columns_of(rank, weight, width, start):
-        return lax.dynamic_slice_in_dim(weight, start + rank * width, width, 1)
-
-    def proj_columns(rank):
-        return jnp.concatenate(
-            [
-                columns_of(rank, projection_weight, query_part, 0),
-                columns_of(rank, projection_weight, query_part, query_total),
-                columns_of(rank, projection_weight, HEAD_SIZE, 2 * query_total),
-                columns_of(rank, projection_weight, HEAD_SIZE, 2 * query_total + key_total),
-            ],
-            axis=1,
-        )
-
-    def out_columns(rank):
-        return columns_of(rank, out_weight, query_part, 0)
-
-    def up_columns(rank):
-        return jnp.concatenate(
-            [
-                columns_of(rank, gate_weight, ff_part, 0),
-                columns_of(rank, up_weight, ff_part, 0),
-            ],
-            axis=1,
-        )
-
-    def down_columns(rank):
-        return columns_of(rank, down_weight, ff_part, 0)
-
-    def swapped(piece_of):
-        base = (row * 2 + core) * seqs
-        other = lax.ppermute(piece_of(base + 1 - seq), "seq", [(0, 1), (1, 0)])
-        own = piece_of(base + seq)
-        return jnp.where(seq == 0, jnp.stack([own, other]), jnp.stack([other, own]))
+        return reorder(values, [z * seqs + x for x in range(seqs) for z in range(planes)])
+
+    weight_plan = (
+        ("proj", 0, query_part, "proj", 0),
+        ("proj", query_total, query_part, "proj", query_part),
+        ("proj", 2 * query_total, HEAD_SIZE, "proj", 2 * query_part),
+        ("proj", 2 * query_total + key_total, HEAD_SIZE, "proj", 2 * query_part + HEAD_SIZE),
+        ("out", 0, query_part, "out", 0),
+        ("gate", 0, ff_part, "up", 0),
+        ("up", 0, ff_part, "up", ff_part),
+    )
+    piece_widths = (2 * (query_part + HEAD_SIZE), query_part, 2 * ff_part)
 
     def whole_columns(piece):
         piece = piece.reshape(seqs * shard_rows, piece.shape[-1])
@@ -916,19 +1333,19 @@
     pad_here = lax.dynamic_slice_in_dim(padding_token_mask, ctx * token_rows, token_rows, 0)
     grad_here = (cotangent.astype(f32) * pad_here.astype(f32)[:, None]).astype(bf16)
     chunked = (plane_size, chunk, model_width)
-    proj_piece = swapped(proj_columns)
-    later = (swapped(out_columns), swapped(up_columns), swapped(down_columns))
-    proj_w = whole_columns(proj_piece)
-    tokens_own, own_grad, normed_attn, grad_low, layouts, gains = prologue(
-        to_inner(tokens).reshape(chunked), to_inner(grad_here).reshape(chunked),
-        layout_pack, gain_pack,
-    )
-    later, normed_attn = lax.optimization_barrier((later, normed_attn))
-    out_w, up_w, down_w = (whole_columns(piece) for piece in later)
+    tokens_own, normed_attn, layouts, gains, proj_w, out_piece, up_piece = prologue(
+        to_inner(tokens).reshape(chunked),
+        layout_pack,
+        gain_pack,
+        (projection_weight, out_weight, gate_weight, up_weight),
+        weight_plan,
+        piece_widths,
+    )
+    proj_w = proj_w.reshape(model_width, piece_widths[0])
+    out_w = whole_columns(out_piece)
+    up_w = whole_columns(up_piece)
     tokens_wide = tokens_own.reshape(groups, chunk, model_width).astype(f32)
-    own_grad = own_grad.reshape(groups, chunk, model_width)
     normed_attn = normed_attn.reshape(plane_tokens, model_width)
-    grad_low = grad_low.reshape(plane_tokens, model_width)
 
     gains = gains[:, :gain_rows].reshape(planes * seqs, 2, shard_rows)
     gain_attn = gains[:, 0].reshape(model_width)
@@ -961,18 +1378,35 @@
     tables = (head_gain_wide, cosine, sine, query_code, key_code)
     saved = attend(projected, *tables, heads)
     mixed = saved[0].reshape(plane_tokens, query_part)
-    resid_mid = tokens_wide + scattered(
-        lax.dot_general(mixed, out_w, contract_cols, preferred_element_type=f32)
-    )
+    def parts_of(values):
+        return values.reshape(groups, plane_size, chunk, -1)
+
+    grad_chunks = to_inner(grad_here).reshape(chunked)
+    half = chunk // 2
+    attn_rows, grad_first, down_piece = multiply_scatter(
+        5,
+        parts_of(mixed),
+        out_w,
+        grad_chunks[:, :half],
+        True,
+        down_weight,
+        ((0, 0, ff_part, 0, 0),),
+    )
+    down_w = whole_columns(down_piece)
+    resid_mid = tokens_wide + attn_rows
     root_mlp = lax.rsqrt(jnp.mean(resid_mid * resid_mid, axis=2, keepdims=True) + norm_epsilon)
     unit_mlp = resid_mid * root_mlp
-    normed_mlp = gathered((unit_mlp * gain_mlp).astype(bf16))
-    both_lin = jnp.dot(normed_mlp, up_w, preferred_element_type=f32)
-    gate_lin = both_lin[:, :ff_part]
-    up_lin = both_lin[:, ff_part:]
-    gate_sig = jax.nn.sigmoid(gate_lin)
-    silu_gate = gate_lin * gate_sig
-    hidden = (silu_gate * up_lin).astype(bf16)
+    normed_all, grad_second = plane_gather(
+        (unit_mlp * gain_mlp).astype(bf16), grad_chunks[:, half:]
+    )
+    own_grad = jnp.concatenate([grad_first, grad_second], axis=2).reshape(
+        groups, chunk, model_width
+    )
+    grad_all, linear, hidden = gather_and_feed(own_grad, normed_all, up_w)
+    normed_mlp = normed_all.reshape(plane_tokens, model_width)
+    grad_low = grad_all.reshape(plane_tokens, model_width)
+    hidden = hidden.reshape(plane_tokens, ff_part)
+
     def grads_to_rows(grads):
         rows = lax.psum_scatter(grads.astype(bf16), "ctx", scatter_dimension=0, tiled=True)
         if lax.axis_size("far") > 1:
@@ -985,23 +1419,17 @@
     down_part = lax.dot_general(
         grad_low, hidden, contract_rows, preferred_element_type=f32
     ).astype(bf16)
-    grad_low = after(grad_low, down_part)
-    d_hidden = jnp.dot(grad_low, down_w, preferred_element_type=f32)
-    d_gate = (d_hidden * up_lin * gate_sig * (1.0 + gate_lin * (1.0 - gate_sig))).astype(bf16)
-    d_up = (d_hidden * silu_gate).astype(bf16)
-    d_both = jnp.concatenate([d_gate, d_up], axis=1)
     down_rows = grads_to_rows(down_part)
+    d_normed_mlp, d_both = feed_back(after(grad_all, down_part), linear, down_w, up_w)
+    d_both = d_both.reshape(plane_tokens, 2 * ff_part)
     up_part = lax.dot_general(
         normed_mlp, d_both, contract_rows, preferred_element_type=f32
     ).astype(bf16)
     up_rows = grads_to_rows(up_part)
-    d_both = after(d_both, up_part)
-    d_normed_mlp = scattered(
-        lax.dot_general(d_both, up_w, contract_cols, preferred_element_type=f32)
-    )
+    d_normed_mlp = after(d_normed_mlp, up_part)
     gain_mlp_term = jnp.sum(d_normed_mlp * unit_mlp, axis=(0, 1))
     d_resid = own_grad.astype(f32) + norm_back(d_normed_mlp, unit_mlp, root_mlp, gain_mlp)
-    d_attn_low = gathered(d_resid.astype(bf16))
+    d_attn_low = plane_gather(d_resid.astype(bf16)).reshape(plane_tokens, model_width)
     mixed_grad = jnp.dot(d_attn_low, out_w, preferred_element_type=f32)
     out_part = lax.dot_general(
         d_attn_low, mixed, contract_rows, preferred_element_type=f32
@@ -1018,14 +1446,12 @@
     ).astype(bf16)
     proj_rows = grads_to_rows(proj_part)
     d_proj = after(d_proj, proj_part)
-    d_normed_attn = scattered(
-        lax.dot_general(d_proj, proj_w, contract_cols, preferred_element_type=f32)
-    )
-    hidden = after(hidden, d_normed_attn)
-    layer_own = (
-        resid_mid
-        + scattered(lax.dot_general(hidden, down_w, contract_cols, preferred_element_type=f32))
-    ).astype(bf16)
+    hidden = after(hidden, proj_part)
+    parted = (held, planes, chunk, model_width)
+    layer_own = (resid_mid + multiply_scatter(7, parts_of(hidden), down_w)).astype(bf16)
+    d_normed_attn, layer_out = multiply_scatter(
+        6, parts_of(d_proj), proj_w, to_outer(layer_own).reshape(parted), False
+    )
     gain_attn_term = jnp.sum(d_normed_attn * unit_attn, axis=(0, 1))
     tokens_grad = (d_resid + norm_back(d_normed_attn, unit_attn, root_attn, gain_attn)).astype(bf16)
     small_rows = shard_rows // 128
@@ -1050,26 +1476,25 @@
     )
     ff_width = plane_size * ff_part
     up_segments = ((0, ff_part, 0), (ff_part, ff_part, ff_width))
-    parted = (held, planes, chunk, model_width)
-    layer_out, up_grad, down_grad = send_back(
-        layer_own.reshape(parted),
+    tokens_grad, up_grad, down_grad = send_back(
+        to_outer(tokens_grad).reshape(parted),
         (up_rows, down_rows),
         (up_segments, ((0, ff_part, 0),)),
         (2 * ff_width, ff_width),
         None,
         3,
     )
-    proj_rows = after(proj_rows, layer_out)
-    tokens_grad, proj_grad, out_grad, small = send_back(
-        tokens_grad.reshape(parted),
+    proj_rows = after(proj_rows, tokens_grad)
+    proj_grad, out_grad, small = send_back(
+        None,
         (proj_rows, out_rows),
         (proj_segments, ((0, query_part, 0),)),
         (2 * (query_total + key_total), query_total),
         tiles,
         4,
     )
-    layer_out = to_outer(layer_out.reshape(token_rows, model_width))
-    tokens_grad = to_outer(tokens_grad.reshape(token_rows, model_width))
+    layer_out = layer_out.reshape(token_rows, model_width)
+    tokens_grad = tokens_grad.reshape(token_rows, model_width)
     if lax.axis_size("far") > 1:
         small = lax.psum(small, "far")
     attention_gain_grad = small[:small_rows].reshape(shard_rows)

time: 875 us -> 750 us (0.86)
  matrix products: 147 us -> 60.2 us
  Pallas kernels: 546 us -> 569 us
  waiting for transfers between devices: 56.9 us -> 35.6 us
  local copies, waits for them, and re-layouts: 51.6 us -> 36.1 us
  other arithmetic: 41.5 us -> 28.4 us
    dot_general x6 -> x0, matrix products: 83.6 us -> none  [the longest x1 18.2 us: per_device(): both_lin = jnp.dot(normed_mlp, up_w, preferred_element_type=f32)]
    pallas_call x9 -> x10, Pallas kernels: 510 us -> 534 us  [the longest x3 159 us: multiply_scatter(): pl.pallas_call(functools.partial(scatter_kernel, outward, swap_plan), out...]
    all_gather x4 -> x3, waiting for transfers between devices: 47 us -> 34.7 us  [whole_columns(): return lax.all_gather(piece, 'ctx', axis=0, tiled=True)]
    ppermute x4 -> x0, waiting for transfers between devices: 9.09 us -> none  [swapped(): other = lax.ppermute(piece_of(base + 1 - seq), 'seq', [(0, 1), (1, 0)])]
    unnamed x103 -> x123, local copies, waits for them, and re-layouts: 27.8 us -> 32.4 us
  transfers between devices with their start and end apart: 12 -> 7, of which waited for: 3 -> 2; matrix products, arithmetic and copies ran while one was open for 22% -> 11% of each run, Pallas kernels for 57% -> 60%
where the time goes in v3:
time: 750 us; the launch traced here: 746 us
  Pallas kernels  569 us (76%)
  matrix products  60.2 us (8%)
  local copies, waits for them, and re-layouts  36.1 us (5%)
  waiting for transfers between devices  35.6 us (5%)
  other arithmetic  28.4 us (4%)
  between operations  15.5 us (2%)
    pallas_call x3, Pallas kernels, multiply_scatter(): pl.pallas_call(functools.partial(scatter_kernel, outward, swap_plan), out...  159 us
    pallas_call x2, Pallas kernels, send_back(): pl.pallas_call(functools.partial(return_kernel, plans, values is not None...  104 us
    pallas_call x1, Pallas kernels, prologue(): pl.pallas_call(functools.partial(prologue_kernel, weight_plan, planes), o...  91.9 us
    pallas_call x2, Pallas kernels, plane_gather(): pl.pallas_call(plain_gather_kernel if values is None else gather_kernel,...  87 us
    pallas_call x1, Pallas kernels, feed_back(): pl.pallas_call(backward_kernel, out_shape=(jax.ShapeDtypeStruct((groups,...  51.5 us
    pallas_call x1, Pallas kernels, gather_and_feed(): pl.pallas_call(forward_kernel, out_shape=(jax.ShapeDtypeStruct((groups, 8...  41.6 us
    all_gather x3, waiting for transfers between devices, whole_columns(): return lax.all_gather(piece, 'ctx', axis=0, tiled=True)  34.7 us
    unnamed x123, local copies, waits for them, and re-layouts  32.4 us
  transfers between devices with their start and end apart: 7, of which 2 were waited for; matrix products, arithmetic and copies ran while one was open for 11% of the time, Pallas kernels for 60%

profile of v3, /device:TPU:0, one launch (start us, length us, event | category | flops | bytes accessed | tf_op | source)
XLA Modules:
  0.0 746.2 jit_solution(18360862123517341113)
XLA Ops:
  14.8 91.9 %prologue.1 = (bf16[2,4,32,2048]{3,2,1,0:T(8,128)(2,1)S(1)}, bf16[8,8,32,2048]{3,2,1,0:T(8,128)(2,1)}, f32[8,8,128]{2,1,0:T(8,128)S(1)}, f32[8,8,128]{2,1,0:T(8,...) custom-call(bf16[8,32,2048]{2,1,0:T(8,128)(2,1)S(1)} %bitcast.78, ...), custom_call_target="tpu_custom_call" | custom-call | tf_op jit(solution)/shard_map/prologue/pallas_call | solution.py:916
  108.0 1.9 fusion.1
  110.6 1.6 copy-done.44
  112.2 10.7 %fusion.10.p_ref = f32[2,1024,768]{2,1,0:T(8,128)} fusion(bf16[2,1024,2048]{2,1,0:T(8,128)(2,1)} %bitcast.107, bf16[2048,768,1]{1,0,2:T(8,128)(2,1)S(1)} %bitcast.110), kind=kOutput, calls=%fused_computation.87 | convolution fusion | flops 6442450944 | bytes 17825792 | tf_op jit(solution)/shard_map/dot_general | solution.py:1375
  123.3 15.8 %attend.1 = (bf16[2,1024,256]{2,1,0:T(8,128)(2,1)S(1)}, f32[2,1024,256]{2,1,0:T(8,128)}, bf16[2,1024,256]{2,1,0:T(8,128)(2,1)S(1)}, bf16[2,1024,128]{2,1,0:T(8,128)(2,1)S(1)}, f32[2,2,1024,128]{3,2,1,0:T(8,128)}) custom-call(f32[2,1024,768]{2,1,0:T(8,128)} %fusion.10.p_ref, f32[2,128]{1,0:T(2,128)S(1)} %convert_element_type.91.gain_ref, ...), custom_call_target="tpu_custom_call" | custom-call | flops 2147483648 | bytes 16777216 | tf_op jit(solution)/shard_map/attend/pallas_call | solution.py:1206
  143.2 59.6 %multiply_scatter.3 = (f32[8,32,2048]{2,1,0:T(8,128)S(1)}, bf16[2,4,16,2048]{3,2,1,0:T(8,128)(2,1)S(1)}, bf16[2,256,768]{2,1,0:T(8,128)(2,1)}) custom-call(bf16[8,8,32,256]{3,2,1,0:T(8,128)(2,1)S(1)} %bitcast.87, bf16[2048,256]{1,0:T(8,128)(2,1)S(1)} %copy-done.16, bf16[8,16,2048]{2,1,0:T(8,128)(2,1)S(1)} %get-tuple-element.109.refs_2_, ...), custom_call_target="tpu_custom_call" | custom-call | flops 2147483648 | bytes 9437184 | tf_op jit(solution)/shard_map/multiply_scatter/pallas_call | solution.py:433
  202.8 1.7 bitcast_multiply_fusion
  205.8 47.3 %plane_gather.2 = (bf16[8,8,32,2048]{3,2,1,0:T(8,128)(2,1)}, bf16[2,4,16,2048]{3,2,1,0:T(8,128)(2,1)S(1)}) custom-call(bf16[8,32,2048]{2,1,0:T(8,128)(2,1)S(1)} %multiply_convert_fusion.x_ref, bf16[8,16,2048]{2,1,0:T(8,128)(2,1)S(1)} %get-tuple-element.108.v_ref), custom_call_target="tpu_custom_call" | custom-call | tf_op jit(solution)/shard_map/plane_gather/pallas_call | solution.py:164
  253.3 25.6 %all-gather.6.cloned.1.call-done.w_ref.up_ref = bf16[2048,1536]{1,0:T(8,128)(2,1)} async-done(((bf16[512,1536]{1,0:T(8,128)(2,1)}), bf16[2048,1536]{1,0:T(8,128)(2,1)}) %all-gather.6.cloned.1.call-update) | async-done | bytes 6291472 | tf_op jit(solution)/shard_map/all_gather | solution.py:1324
  278.9 41.6 %gather_and_feed.1 = (bf16[8,8,32,2048]{3,2,1,0:T(8,128)(2,1)}, f32[8,8,32,1536]{3,2,1,0:T(8,128)}, bf16[8,8,32,768]{3,2,1,0:T(8,128)(2,1)S(1)}) custom-call(bf16[8,32,2048]{2,1,0:T(8,128)(2,1)S(1)} %bitcast.76, bf16[8,8,32,2048]{3,2,1,0:T(8,128)(2,1)} %get-tuple-element.70.h_ref, bf16[2048,1536]{1,0:T(8,128)(2,1)} %all-gather.6.cloned.1.call-done.w_ref.up_ref), custom_call_target="tpu_custom_call" | custom-call | flops 12884901888 | bytes 14680064 | tf_op jit(solution)/shard_map/gather_and_feed/pallas_call | solution.py:522
  320.6 10.4 %bitcast_convert_fusion.1 = bf16[2048,768]{1,0:T(8,128)(2,1)} fusion(bf16[8,8,32,2048]{3,2,1,0:T(8,128)(2,1)} %get-tuple-element.74.g_ref, bf16[8,8,32,768]{3,2,1,0:T(8,128)(2,1)S(1)} %get-tuple-element.73), kind=kOutput, calls=%fused_computation.1 | convolution fusion | flops 6444023808 | bytes 14680064 | tf_op jit(solution)/shard_map/dot_general | solution.py:1419
  331.0 1.7 copy-done.25
  333.2 9.1 %all-gather.8.cloned.1.call-done.down_ref.refs_1_ = bf16[2048,768]{1,0:T(8,128)(2,1)} async-done(((bf16[512,768]{1,0:T(8,128)(2,1)}), bf16[2048,768]{1,0:T(8,128)(2,1)}) %all-gather.8.cloned.1.call-update) | async-done | bytes 3145744 | tf_op jit(solution)/shard_map/all_gather | solution.py:1324
  342.3 1.9 copy-done.15
  344.1 51.5 %feed_back.1 = (f32[8,32,2048]{2,1,0:T(8,128)S(1)}, bf16[8,8,32,1536]{3,2,1,0:T(8,128)(2,1)}) custom-call(bf16[8,8,32,2048]{3,2,1,0:T(8,128)(2,1)} %get-tuple-element.74.g_ref, f32[8,8,32,1536]{3,2,1,0:T(8,128)} %get-tuple-element.75.lin_ref, bf16[2048,768]{1,0:T(8,128)(2,1)S(1)} %copy-done.15, bf16[2048,1536]{1,0:T(8,128)(2,1)} %all-gather.6.cloned.1.call-done.w_ref.up_ref), custom_call_target="tpu_custom_call" | custom-call | flops 19327352832 | bytes 35651584 | tf_op jit(solution)/shard_map/feed_back/pallas_call | solution.py:622
  395.7 16.8 %bitcast_convert_fusion = bf16[2048,1536]{1,0:T(8,128)(2,1)} fusion(bf16[8,8,32,2048]{3,2,1,0:T(8,128)(2,1)S(1)} %copy-done.43, bf16[8,8,32,1536]{3,2,1,0:T(8,128)(2,1)} %get-tuple-element.78), kind=kOutput, calls=%fused_computation | convolution fusion | flops 12888047616 | bytes 20971520 | tf_op jit(solution)/shard_map/dot_general | solution.py:1425
  412.7 2.4 multiply_reduce_fusion
  415.8 39.7 %plane_gather.3 = bf16[8,8,32,2048]{3,2,1,0:T(8,128)(2,1)} custom-call(bf16[8,32,2048]{2,1,0:T(8,128)(2,1)S(1)} %fusion.7.x_ref), custom_call_target="tpu_custom_call" | custom-call | tf_op jit(solution)/shard_map/plane_gather/pallas_call | solution.py:164
  455.5 7.2 fusion.11
  462.7 3.7 convolution_convert_fusion.1
  472.0 1.6 copy-done.27
  473.6 19.4 %attend_back.1 = (bf16[2,1024,768]{2,1,0:T(8,128)(2,1)}, f32[8,128]{1,0:T(8,128)S(1)}) custom-call(f32[2,1024,256]{2,1,0:T(8,128)S(1)} %bitcast.89, f32[2,1024,768]{2,1,0:T(8,128)} %fusion.10.p_ref, f32[2,128]{1,0:T(2,128)S(1)} %convert_element_type.91.gain_ref, f32[1024,128]{1,0:T(8,128)S(1)} %copy-done.5, f32[1024,128]{1,0:T(8,128)S(1)} %copy-done.7, ...), custom_call_target="tpu_custom_call" | custom-call | flops 5368709120 | bytes 16777216 | tf_op jit(solution)/shard_map/attend_back/pallas_call | solution.py:1237
  493.0 11.4 %convolution_convert_fusion = bf16[2048,768]{1,0:T(8,128)(2,1)} fusion(bf16[2048,2048]{1,0:T(8,128)(2,1)} %bitcast.108, bf16[2048,768]{1,0:T(8,128)(2,1)} %bitcast.111), kind=kOutput, calls=%fused_computation.2 | convolution fusion | flops 6444023808 | bytes 14680064 | tf_op jit(solution)/shard_map/dot_general | solution.py:1444
  504.4 1.9 copy-done.26
  506.3 44.5 %multiply_scatter.4 = f32[8,32,2048]{2,1,0:T(8,128)S(1)} custom-call(bf16[8,8,32,768]{3,2,1,0:T(8,128)(2,1)S(1)} %copy-done.26, bf16[2048,768]{1,0:T(8,128)(2,1)} %all-gather.8.cloned.1.call-done.down_ref.refs_1_), custom_call_target="tpu_custom_call" | custom-call | flops 6442450944 | bytes 11534336 | tf_op jit(solution)/shard_map/multiply_scatter/pallas_call | solution.py:433
  551.4 54.6 %multiply_scatter.5 = (f32[8,32,2048]{2,1,0:T(8,128)S(1)}, bf16[8,32,2048]{2,1,0:T(8,128)(2,1)S(1)}) custom-call(bf16[8,8,32,768]{3,2,1,0:T(8,128)(2,1)} %bitcast.112, bf16[2048,768]{1,0:T(8,128)(2,1)} %bitcast.109, bf16[2,4,32,2048]{3,2,1,0:T(8,128)(2,1)S(1)} %bitcast.86), custom_call_target="tpu_custom_call" | custom-call | flops 6442450944 | bytes 11534336 | tf_op jit(solution)/shard_map/multiply_scatter/pallas_call | solution.py:433
  612.9 74.3 %send_back.2 = (bf16[8,32,2048]{2,1,0:T(8,128)(2,1)S(1)}, bf16[256,12288]{1,0:T(8,128)(2,1)}, bf16[256,6144]{1,0:T(8,128)(2,1)}) custom-call(bf16[2,4,32,2048]{3,2,1,0:T(8,128)(2,1)S(1)} %bitcast.79, bf16[2,256,1536]{2,1,0:T(8,128)(2,1)S(1)} %bitcast.77, bf16[2,256,768]{2,1,0:T(8,128)(2,1)S(1)} %bitcast.83), custom_call_target="tpu_custom_call" | custom-call | tf_op jit(solution)/shard_map/send_back/pallas_call | solution.py:1050
  687.2 9.3 %slice_convert_fusion = (f32[256,6144]{1,0:T(8,128)}, f32[256,6144]{1,0:T(8,128)}) fusion(bf16[256,12288]{1,0:T(8,128)(2,1)} %get-tuple-element.96), kind=kLoop, calls=%fused_computation.3 | loop fusion | flops 3145728 | bytes 18874368 | tf_op jit(solution)/shard_map/convert_element_type | solution.py:1512
  697.5 29.4 %send_back.3 = (bf16[256,6144]{1,0:T(8,128)(2,1)S(1)}, bf16[256,2048]{1,0:T(8,128)(2,1)S(1)}, f32[8,128]{1,0:T(8,128)S(1)}) custom-call(bf16[2,256,768]{2,1,0:T(8,128)(2,1)S(1)} %bitcast.82, bf16[2,256,256]{2,1,0:T(8,128)(2,1)S(1)} %bitcast.84, f32[4,2,8,128]{3,2,1,0:T(8,128)S(1)} %maximum_maximum_fusion.refs_2_), custom_call_target="tpu_custom_call" | custom-call | tf_op jit(solution)/shard_map/send_back/pallas_call | solution.py:1050
  726.8 3.5 convert_element_type.111
  730.3 1.6 convert_element_type.112
  732.9 3.5 convert_element_type.115
  (175 shorter events, 33.9 us)
Async XLA Ops:
  7.2 7.5 %copy-start.39 = (s32[1024]{0:T(1024)S(1)}, s32[1024]{0:T(1024)}, u32[]{:S(2)}) copy-start(s32[1024]{0:T(1024)} %param.17) | copy-start | bytes 12292
  7.2 7.5 %copy-start.40 = (s32[1024]{0:T(1024)S(1)}, s32[1024]{0:T(1024)}, u32[]{:S(2)}) copy-start(s32[1024]{0:T(1024)} %param.16) | copy-start | bytes 12292
  7.2 7.6 %copy-start.42 = (bf16[256]{0:T(256)(128)(2,1)S(1)}, bf16[256]{0:T(256)(128)(2,1)}, u32[]{:S(2)}) copy-start(bf16[256]{0:T(256)(128)(2,1)} %param.18) | copy-start | bytes 1540
  7.2 7.6 %copy-start.41 = (bf16[256]{0:T(256)(128)(2,1)S(1)}, bf16[256]{0:T(256)(128)(2,1)}, u32[]{:S(2)}) copy-start(bf16[256]{0:T(256)(128)(2,1)} %param.22) | copy-start | bytes 1540
  7.2 7.6 %copy-start.9 = (bf16[256,2048]{1,0:T(8,128)(2,1)S(1)}, bf16[256,2048]{1,0:T(8,128)(2,1)}, u32[]{:S(2)}) copy-start(bf16[256,2048]{1,0:T(8,128)(2,1)} %out_ref.1) | copy-start | bytes 3145732
  7.2 133.5 %all-gather.4.cloned.1.call-start = ((), (), s32[]{:S(2)}) async-start(), calls=%async_computation.4 | async-start | bytes 1310720 | tf_op jit(solution)/shard_map/all_gather | solution.py:1324
  14.8 93.0 %copy-start.45 = (bf16[2,128]{1,0:T(2,128)(2,1)S(1)}, bf16[2,128]{1,0:T(2,128)(2,1)}, u32[]{:S(2)}) copy-start(bf16[2,128]{1,0:T(2,128)(2,1)} %param.20) | copy-start | bytes 1540
  106.7 96.1 %copy-start = (bf16[2,4,32,2048]{3,2,1,0:T(8,128)(2,1)}, bf16[2,4,32,2048]{3,2,1,0:T(8,128)(2,1)S(1)}, u32[]{:S(2)}) copy-start(bf16[2,4,32,2048]{3,2,1,0:T(8,128)(2,1)S(1)} %get-tuple-element.66) | copy-start | bytes 3145732
  106.7 172.2 %all-gather.6.cloned.1.call-start = ((), (), s32[]{:S(2)}) async-start(), calls=%async_computation.5 | async-start | bytes 7864320 | tf_op jit(solution)/shard_map/all_gather | solution.py:1324
  107.5 234.8 %all-gather.8.cloned.1.call-start = ((), (), s32[]{:S(2)}) async-start(), calls=%async_computation.6 | async-start | bytes 3932160 | tf_op jit(solution)/shard_map/all_gather | solution.py:1324
  110.3 13.0 %copy-start.4 = (f32[1024,128]{1,0:T(8,128)}, f32[1024,128]{1,0:T(8,128)S(1)}, u32[]{:S(2)}) copy-start(f32[1024,128]{1,0:T(8,128)S(1)} %get-tuple-element.118.cos_ref) | copy-start | bytes 1572868
  110.3 13.0 %copy-start.6 = (f32[1024,128]{1,0:T(8,128)}, f32[1024,128]{1,0:T(8,128)S(1)}, u32[]{:S(2)}) copy-start(f32[1024,128]{1,0:T(8,128)S(1)} %get-tuple-element.119.sin_ref) | copy-start | bytes 1572868
  123.2 15.9 %copy-start.2 = (f32[2,1024,128]{2,1,0:T(8,128)}, f32[2,1024,128]{2,1,0:T(8,128)S(1)}, u32[]{:S(2)}) copy-start(f32[2,1024,128]{2,1,0:T(8,128)S(1)} %broadcast_in_dim.9.qcode_ref) | copy-start | bytes 3145732
  123.3 16.6 %copy-start.35 = (bf16[256,2048]{1,0:T(8,128)(2,1)S(1)}, bf16[256,2048]{1,0:T(8,128)(2,1)}, u32[]{:S(2)}) copy-start(bf16[256,2048]{1,0:T(8,128)(2,1)} %param.15) | copy-start | bytes 3145732
  139.2 63.7 %copy-start.37 = (f32[2,4,32]{2,1,0:T(4,128)}, f32[2,4,32]{2,1,0:T(4,128)S(1)}, u32[]{:S(2)}) copy-start(f32[2,4,32]{2,1,0:T(4,128)S(1)} %add_rsqrt_fusion) | copy-start | bytes 3076
  253.3 357.0 %reduce-scatter.7.cloned.1.call-start = ((), (), s32[]{:S(2)}) async-start(), calls=%async_computation.8 | async-start | bytes 3932160 | tf_op jit(solution)/shard_map/reduce_scatter | solution.py:1411
  332.7 277.6 %reduce-scatter.5.cloned.1.call-start = ((), (), s32[]{:S(2)}) async-start(), calls=%async_computation.7 | async-start | bytes 7864320 | tf_op jit(solution)/shard_map/reduce_scatter | solution.py:1411
  344.1 51.5 %copy-start.43 = (bf16[8,8,32,2048]{3,2,1,0:T(8,128)(2,1)S(1)}, bf16[8,8,32,2048]{3,2,1,0:T(8,128)(2,1)}, u32[]{:S(2)}) copy-start(bf16[8,8,32,2048]{3,2,1,0:T(8,128)(2,1)} %get-tuple-element.70.h_ref) | copy-start | bytes 25165828
  412.5 274.6 %reduce-scatter.9.cloned.1.call-start = ((), (), s32[]{:S(2)}) async-start(), calls=%async_computation.9 | async-start | bytes 3932160 | tf_op jit(solution)/shard_map/reduce_scatter | solution.py:1411
  412.7 2.4 copy-start.29
  415.8 39.7 %copy-start.17 = (bf16[2048,256]{1,0:T(8,128)(2,1)S(1)}, bf16[2048,256]{1,0:T(8,128)(2,1)}, u32[]{:S(2)}) copy-start(bf16[2048,256]{1,0:T(8,128)(2,1)} %all-gather.4.cloned.1.call-done.refs_1_) | copy-start | bytes 3145732
  455.5 7.2 copy-start.22
  455.5 7.2 copy-start.32
  504.3 192.2 %reduce-scatter.11.cloned.1.call-start = ((), (), s32[]{:S(2)}) async-start(), calls=%async_computation.10 | async-start | bytes 1310720 | tf_op jit(solution)/shard_map/reduce_scatter | solution.py:1411
  506.3 44.5 %copy-start.30 = (f32[8,32,2048]{2,1,0:T(8,128)S(1)}, f32[8,32,2048]{2,1,0:T(8,128)}, u32[]{:S(2)}) copy-start(f32[8,32,2048]{2,1,0:T(8,128)} %copy-done.28) | copy-start | bytes 6291460
  551.3 54.6 %copy-start.1 = (bf16[2,4,32,2048]{3,2,1,0:T(8,128)(2,1)S(1)}, bf16[2,4,32,2048]{3,2,1,0:T(8,128)(2,1)}, u32[]{:S(2)}) copy-start(bf16[2,4,32,2048]{3,2,1,0:T(8,128)(2,1)} %copy-done) | copy-start | bytes 3145732
  551.4 54.6 %copy-start.31 = (f32[8,32,2048]{2,1,0:T(8,128)S(1)}, f32[8,32,2048]{2,1,0:T(8,128)}, u32[]{:S(2)}) copy-start(f32[8,32,2048]{2,1,0:T(8,128)} %get-tuple-element.106) | copy-start | bytes 6291460
  551.4 54.6 %copy-start.36 = (f32[8,1,256]{2,1,0:T(1,128)S(1)}, f32[8,1,256]{2,1,0:T(1,128)}, u32[]{:S(2)}) copy-start(f32[8,1,256]{2,1,0:T(1,128)} %get-tuple-element.110) | copy-start | bytes 24580
  551.4 54.6 %copy-start.38 = (f32[2,4,32]{2,1,0:T(4,128)S(1)}, f32[2,4,32]{2,1,0:T(4,128)}, u32[]{:S(2)}) copy-start(f32[2,4,32]{2,1,0:T(4,128)} %copy-done.37) | copy-start | bytes 3076
  687.2 9.3 %copy-start.12 = (bf16[512,768]{1,0:T(8,128)(2,1)S(1)}, bf16[512,768]{1,0:T(8,128)(2,1)}, u32[]{:S(2)}) copy-start(bf16[512,768]{1,0:T(8,128)(2,1)} %reduce-scatter.9.cloned.1.call-done) | copy-start | bytes 2359300
  730.3 2.6 copy-start.34
  732.9 4.0 copy-start.11
  (21 other events, 28.1 us)
Sparse Core Ops, SparseCore 0:
  106.9 33.3 all-gather.3
  141.8 137.0 all-gather.5
  280.5 61.6 all-gather.7
  344.4 58.8 reduce-scatter.6
  412.7 108.6 reduce-scatter.4
  524.1 77.4 reduce-scatter.8
  609.4 52.6 reduce-scatter.10

commit v4 on v3

--- a/solution.py
+++ b/solution.py
@@ -828,9 +828,9 @@
 def prologue_kernel(
     weight_plan, planes,
     tokens_ref, layout_ref, gain_ref, proj_ref, out_ref, gate_ref, up_ref,
-    own_tokens, normed_all, lay_out, gain_out, proj_full, out_piece, up_piece,
+    own_tokens, normed_all, lay_out, gain_out, proj_full, out_full, up_piece,
     normed, stage, small_send, small_recv, ex_send, ex_recv, local_sem, g_send, g_recv,
-    w_local, w_send, w_recv, up_send, line_down, line_recv,
+    w_local, w_send, w_recv, up_send, line_down, line_recv, out_up, out_down, out_recv,
 ):
     far, row, core, seq, ctx = place()
     own = (row * 2 + core) * 2 + seq
@@ -842,10 +842,11 @@
     ]
     greet(mates + owners)
     weights = {"proj": proj_ref, "out": out_ref, "gate": gate_ref, "up": up_ref}
-    pieces = {"proj": proj_full.at[ctx], "out": out_piece, "up": up_piece}
+    pieces = {"proj": proj_full.at[ctx], "out": out_full.at[ctx], "up": up_piece}
     swap = Swap(weight_plan, weights, pieces, w_local, w_send, w_recv)
     proj_parts = [i for i, plan in enumerate(weight_plan) if plan[0] == "proj"]
-    other_parts = [i for i, plan in enumerate(weight_plan) if plan[0] != "proj"]
+    out_parts = [i for i, plan in enumerate(weight_plan) if plan[0] == "out"]
+    other_parts = [i for i, plan in enumerate(weight_plan) if plan[3] == "up"]
     for index in proj_parts:
         swap.start(index)
     tokens = Exchange(True, tokens_ref, own_tokens, stage, ex_send, ex_recv)
@@ -864,11 +865,12 @@
         swap.local[index].wait()
     relay.begin(seq)
     tokens.middle()
-    for index in other_parts:
+    for index in out_parts + other_parts:
         swap.start(index)
     for index in proj_parts:
         swap.sent[index].wait_recv()
     relay.begin(1 - seq)
+    out_relay = Line(out_full, out_up, out_down, out_recv)
     for copy in small[: len(owners)]:
         copy.wait_recv()
     gain_rows = own_tokens.shape[-1] // total // 128
@@ -885,15 +887,25 @@
     gather.start()
     for k in range(2):
         relay.hop(1, k)
+    for index in out_parts:
+        swap.local[index].wait()
+        swap.sent[index].wait_recv()
+    for k in range(2):
+        out_relay.begin(k)
     gather.middle()
     for distance in range(2, planes):
         for k in range(2):
             relay.hop(distance, k)
+        for k in range(2):
+            out_relay.hop(distance - 1, k)
     gather.finish()
+    for k in range(2):
+        out_relay.hop(planes - 1, k)
     relay.finish()
+    out_relay.finish()
     for index in other_parts:
         swap.finish(index)
-    for index in proj_parts:
+    for index in proj_parts + out_parts:
         swap.sent[index].wait_send()
     for copy in small[len(owners) :]:
         copy.wait_recv()
@@ -912,7 +924,7 @@
     vmem = pl.BlockSpec(memory_space=pltpu.VMEM)
     anywhere = pl.BlockSpec(memory_space=pl.ANY)
     dma = pltpu.SemaphoreType.DMA
-    pieces = [(planes, 2, shard_rows, widths[0])] + [(2, shard_rows, w) for w in widths[1:]]
+    pieces = [(planes, 2, shard_rows, w) for w in widths[:2]] + [(2, shard_rows, widths[2])]
     return pl.pallas_call(
         functools.partial(prologue_kernel, weight_plan, planes),
         out_shape=(
@@ -937,10 +949,8 @@
             dma((plan_count,)),
             dma((plan_count,)),
             dma((plan_count,)),
-            dma((planes, 2)),
-            dma((planes, 2)),
-            dma((planes, 2)),
-        ],
+        ]
+        + [dma((planes, 2)) for _ in range(6)],
         compiler_params=pltpu.CompilerParams(
             collective_id=2, has_side_effects=True, vmem_limit_bytes=VMEM_LIMIT
         ),
@@ -986,6 +996,9 @@
             send(k - 1, small_ref.at[(ctx + k) % planes], line.at[k], levels[k - 1])
             for k in range(1, planes)
         ]
+    for part in rows:
+        part.middle()
+    if with_sum:
         for copy in copies:
             copy.wait_recv()
         total = small_ref[ctx]
@@ -996,8 +1009,6 @@
             send(planes - 2 + k, line.at[0, (own + k) % 2], got.at[k], mates[k - 1])
             for k in range(1, 8)
         ]
-    for part in rows:
-        part.middle()
     if with_values:
         exchange.middle()
     for part in rows:
@@ -1125,61 +1136,106 @@
 
 
 def attend_back_kernel(
-    heads, block, da_ref, p_ref, gain_ref, cos_ref, sin_ref, qcode_ref, kcode_ref,
-    o_ref, q_ref, k_ref, lse_ref, dp_ref, hg_ref, dq_acc, dk_acc, dv_acc,
+    heads, block, held,
+    da_ref, p_ref, gain_ref, cos_ref, sin_ref, qcode_ref, kcode_ref,
+    saved_o_ref, q_ref, k_ref, lse_ref, a_ref, w_ref,
+    out_ref, hg_ref, sum_ref, *refs,
 ):
-    length = p_ref.shape[1]
+    scatter = Scatter(*refs[:9])
+    a_buf, w_buf, a_sem, w_sem, *refs = refs[9:]
+    dq_acc, dk_acc, dv_acc, *refs = refs
+    buffers, dp_buf, load_sem, store_sem = refs[:6], refs[6], refs[7], refs[8]
+    hbm = (p_ref, da_ref, saved_o_ref, q_ref, k_ref, lse_ref)
+    w_load = pltpu.make_async_copy(w_ref, w_buf, w_sem)
+    w_load.start()
+    a_loads = [
+        pltpu.make_async_copy(a_ref.at[:, slot], a_buf.at[k], a_sem.at[k])
+        for k, slot in enumerate(scatter.order)
+    ]
+    for load in a_loads:
+        load.start()
+    loads = [
+        [
+            pltpu.make_async_copy(source.at[s], buffer.at[s], load_sem.at[s, k])
+            for k, (source, buffer) in enumerate(zip(hbm, buffers))
+        ]
+        for s in range(held)
+    ]
+    for copies in loads:
+        for load in copies:
+            load.start()
+    near = scatter.near
+    greet([near["c"], near["x"], near["y"]])
+
+    def produce(index, target):
+        a_loads[index].wait()
+        groups, count, _ = target.shape
+        multiply_into(a_buf[index].reshape(groups * count, a_buf.shape[-1]), w_buf, target)
+
+    w_load.wait()
+    scatter.start(produce)
+
+    p_buf, da_buf, o_buf, q_buf, k_buf, lse_buf = buffers
+    length = p_buf.shape[1]
     width = heads * HEAD_SIZE
     scale = HEAD_SIZE ** (-0.5)
     f32, bf16 = jnp.float32, jnp.bfloat16
-    dk_acc[...] = jnp.zeros_like(dk_acc)
-    dv_acc[...] = jnp.zeros_like(dv_acc)
-
-    @pl.when(pl.program_id(0) == 0)
-    def _():
-        hg_ref[...] = jnp.zeros_like(hg_ref)
-
-    for start in range(0, length, block):
-        stop = start + block
-        allowed = allowed_keys(qcode_ref, kcode_ref, start, block)
-        keys = k_ref[0, :stop]
-        values = p_ref[0, :stop, 2 * width + HEAD_SIZE :].astype(bf16)
+    cosine, sine = cos_ref[...], sin_ref[...]
+    hg_ref[...] = jnp.zeros_like(hg_ref)
+    stores = []
+    for s in range(held):
+        for load in loads[s]:
+            load.wait()
+        dk_acc[...] = jnp.zeros_like(dk_acc)
+        dv_acc[...] = jnp.zeros_like(dv_acc)
+        for start in range(0, length, block):
+            stop = start + block
+            allowed = allowed_keys(qcode_ref.at[s : s + 1], kcode_ref.at[s : s + 1], start, block)
+            keys = k_buf[s, :stop]
+            values = p_buf[s, :stop, 2 * width + HEAD_SIZE :].astype(bf16)
+            for h in range(heads):
+                cols = slice(h * HEAD_SIZE, (h + 1) * HEAD_SIZE)
+                gates = slice(width + h * HEAD_SIZE, width + (h + 1) * HEAD_SIZE)
+                queries = q_buf[s, start:stop, cols]
+                scores = lax.dot_general(queries, keys, contract_cols, preferred_element_type=f32)
+                scores = jnp.where(allowed, scores * scale, masked_value)
+                probs = jnp.exp(scores - lse_buf[s, h, start:stop, :1])
+                gate = jax.nn.sigmoid(p_buf[s, start:stop, gates])
+                grads = da_buf[s, start:stop, cols]
+                dp_buf[s, start:stop, gates] = (
+                    grads * o_buf[s, start:stop, cols] * gate * (1.0 - gate)
+                ).astype(bf16)
+                d_out = (grads * gate).astype(bf16)
+                d_probs = lax.dot_general(d_out, values, contract_cols, preferred_element_type=f32)
+                delta = jnp.sum(probs * d_probs, axis=1, keepdims=True)
+                d_scores = (probs * (d_probs - delta)).astype(bf16)
+                dv_acc[:stop] += lax.dot_general(
+                    probs.astype(bf16), d_out, contract_rows, preferred_element_type=f32
+                )
+                dk_acc[:stop] += lax.dot_general(
+                    d_scores, queries, contract_rows, preferred_element_type=f32
+                )
+                dq_acc[h, start:stop] = jnp.dot(d_scores, keys, preferred_element_type=f32)
         for h in range(heads):
             cols = slice(h * HEAD_SIZE, (h + 1) * HEAD_SIZE)
-            gates = slice(width + h * HEAD_SIZE, width + (h + 1) * HEAD_SIZE)
-            queries = q_ref[0, start:stop, cols]
-            scores = lax.dot_general(queries, keys, contract_cols, preferred_element_type=f32)
-            scores = jnp.where(allowed, scores * scale, masked_value)
-            probs = jnp.exp(scores - lse_ref[0, h, start:stop, :1])
-            gate = jax.nn.sigmoid(p_ref[0, start:stop, gates])
-            grads = da_ref[0, start:stop, cols]
-            dp_ref[0, start:stop, gates] = (
-                grads * o_ref[0, start:stop, cols] * gate * (1.0 - gate)
-            ).astype(bf16)
-            d_out = (grads * gate).astype(bf16)
-            d_probs = lax.dot_general(d_out, values, contract_cols, preferred_element_type=f32)
-            delta = jnp.sum(probs * d_probs, axis=1, keepdims=True)
-            d_scores = (probs * (d_probs - delta)).astype(bf16)
-            dv_acc[:stop] += lax.dot_general(
-                probs.astype(bf16), d_out, contract_rows, preferred_element_type=f32
-            )
-            dk_acc[:stop] += lax.dot_general(
-                d_scores, queries, contract_rows, preferred_element_type=f32
-            )
-            dq_acc[h, start:stop] = jnp.dot(d_scores, keys, preferred_element_type=f32)
-    cosine, sine = cos_ref[...], sin_ref[...]
-    for h in range(heads):
-        cols = slice(h * HEAD_SIZE, (h + 1) * HEAD_SIZE)
-        raw, term = head_back(dq_acc[h] * scale, p_ref[0, :, cols], gain_ref[0:1], cosine, sine)
-        dp_ref[0, :, cols] = raw.astype(bf16)
-        hg_ref[0:1] += term
-    at = 2 * width
-    raw, term = head_back(
-        dk_acc[...] * scale, p_ref[0, :, at : at + HEAD_SIZE], gain_ref[1:2], cosine, sine
-    )
-    dp_ref[0, :, at : at + HEAD_SIZE] = raw.astype(bf16)
-    hg_ref[1:2] += term
-    dp_ref[0, :, at + HEAD_SIZE :] = dv_acc[...].astype(bf16)
+            raw, term = head_back(dq_acc[h] * scale, p_buf[s, :, cols], gain_ref[0:1], cosine, sine)
+            dp_buf[s, :, cols] = raw.astype(bf16)
+            hg_ref[0:1] += term
+        at = 2 * width
+        raw, term = head_back(
+            dk_acc[...] * scale, p_buf[s, :, at : at + HEAD_SIZE], gain_ref[1:2], cosine, sine
+        )
+        dp_buf[s, :, at : at + HEAD_SIZE] = raw.astype(bf16)
+        hg_ref[1:2] += term
+        dp_buf[s, :, at + HEAD_SIZE :] = dv_acc[...].astype(bf16)
+        store = pltpu.make_async_copy(dp_buf.at[s], out_ref.at[s], store_sem.at[s])
+        store.start()
+        stores.append(store)
+        if s == 0:
+            scatter.middle()
+    scatter.finish(sum_ref)
+    for store in stores:
+        store.wait()
 
 
 def whole_spec(shape):
@@ -1226,40 +1282,53 @@
     )(projected, gain, cosine, sine, query_code, key_code)
 
 
-def attend_back(da, projected, gain, cosine, sine, query_code, key_code, saved, heads):
+def attend_back(
+    da, projected, gain, cosine, sine, query_code, key_code, saved, heads, a, weight
+):
     held, length, columns = projected.shape
     _, attended, queries, keys, lse = saved
-    outs = (
-        jax.ShapeDtypeStruct((held, length, columns), jnp.bfloat16),
-        jax.ShapeDtypeStruct((8, HEAD_SIZE), jnp.float32),
-    )
-    ins = (query_code, key_code, attended, queries, keys, lse)
+    groups, _, rows, depth = a.shape
+    width = weight.shape[0]
+    kind = a.dtype
+    dma = pltpu.SemaphoreType.DMA
+    vmem = pl.BlockSpec(memory_space=pltpu.VMEM)
+    anywhere = pl.BlockSpec(memory_space=pl.ANY)
+    big = (projected, da, attended, queries, keys, lse)
     return pl.pallas_call(
-        functools.partial(attend_back_kernel, heads, min(256, length)),
-        grid=(held,),
-        out_shape=outs,
-        in_specs=[
-            first_spec(da.shape),
-            first_spec(projected.shape),
-            whole_spec(gain.shape),
-            whole_spec(cosine.shape),
-            whole_spec(sine.shape),
-        ]
-        + [first_spec(value.shape) for value in ins],
-        out_specs=(first_spec(outs[0].shape), whole_spec(outs[1].shape)),
-        scratch_shapes=[
+        functools.partial(attend_back_kernel, heads, min(256, length), held),
+        out_shape=(
+            jax.ShapeDtypeStruct((held, length, columns), kind),
+            jax.ShapeDtypeStruct((8, HEAD_SIZE), jnp.float32),
+            jax.ShapeDtypeStruct((groups, rows, width), jnp.float32),
+        ),
+        in_specs=[anywhere] * 2 + [vmem] * 5 + [anywhere] * 6,
+        out_specs=(anywhere, vmem, vmem),
+        scratch_shapes=scatter_scratch(groups, rows, width, kind)
+        + [
+            pltpu.VMEM((8, groups, rows, depth), kind),
+            pltpu.VMEM(weight.shape, kind),
+            dma((8,)),
+            dma,
             pltpu.VMEM((heads, length, HEAD_SIZE), jnp.float32),
             pltpu.VMEM((length, HEAD_SIZE), jnp.float32),
             pltpu.VMEM((length, HEAD_SIZE), jnp.float32),
-        ],
-        compiler_params=pltpu.CompilerParams(vmem_limit_bytes=VMEM_LIMIT),
+        ]
+        + [pltpu.VMEM(value.shape, value.dtype) for value in big]
+        + [pltpu.VMEM(projected.shape, kind), dma((held, 6)), dma((held,))],
+        compiler_params=pltpu.CompilerParams(
+            collective_id=7, has_side_effects=True, vmem_limit_bytes=58 * 1024 * 1024
+        ),
         cost_estimate=pl.CostEstimate(
-            flops=10 * held * heads * length * length * HEAD_SIZE,
-            bytes_accessed=held * length * 8192,
+            flops=10 * held * heads * length * length * HEAD_SIZE
+            + 16 * groups * rows * width * depth,
+            bytes_accessed=held * length * 16384,
             transcendentals=held * heads * length * length,
         ),
         name="attend_back",
-    )(da, projected, gain, cosine, sine, *ins)
+    )(
+        da, projected, gain, cosine, sine, query_code, key_code,
+        attended, queries, keys, lse, a, weight,
+    )
 
 
 def per_device(
@@ -1333,7 +1402,7 @@
     pad_here = lax.dynamic_slice_in_dim(padding_token_mask, ctx * token_rows, token_rows, 0)
     grad_here = (cotangent.astype(f32) * pad_here.astype(f32)[:, None]).astype(bf16)
     chunked = (plane_size, chunk, model_width)
-    tokens_own, normed_attn, layouts, gains, proj_w, out_piece, up_piece = prologue(
+    tokens_own, normed_attn, layouts, gains, proj_w, out_w, up_piece = prologue(
         to_inner(tokens).reshape(chunked),
         layout_pack,
         gain_pack,
@@ -1342,7 +1411,7 @@
         piece_widths,
     )
     proj_w = proj_w.reshape(model_width, piece_widths[0])
-    out_w = whole_columns(out_piece)
+    out_w = out_w.reshape(model_width, query_part)
     up_w = whole_columns(up_piece)
     tokens_wide = tokens_own.reshape(groups, chunk, model_width).astype(f32)
     normed_attn = normed_attn.reshape(plane_tokens, model_width)
@@ -1434,24 +1503,27 @@
     out_part = lax.dot_general(
         d_attn_low, mixed, contract_rows, preferred_element_type=f32
     ).astype(bf16)
-    out_rows = grads_to_rows(out_part)
-    mixed_grad = after(mixed_grad, out_part)
-    d_proj, head_term = attend_back(
-        mixed_grad.reshape(held, sequence_length, query_part), projected, *tables, saved, heads
+    mixed_grad = after(mixed_grad, out_part, down_rows)
+    d_proj, head_term, layer_rows = attend_back(
+        mixed_grad.reshape(held, sequence_length, query_part),
+        projected,
+        *tables,
+        saved,
+        heads,
+        parts_of(hidden),
+        down_w,
     )
     d_proj = d_proj.reshape(plane_tokens, -1)
     head_term = head_term[:2]
     proj_part = lax.dot_general(
         normed_attn, d_proj, contract_rows, preferred_element_type=f32
     ).astype(bf16)
-    proj_rows = grads_to_rows(proj_part)
-    d_proj = after(d_proj, proj_part)
-    hidden = after(hidden, proj_part)
+    attn_part = jnp.concatenate([proj_part, out_part], axis=1)
+    attn_rows = grads_to_rows(attn_part)
+    d_proj = after(d_proj, attn_part, up_rows)
     parted = (held, planes, chunk, model_width)
-    layer_own = (resid_mid + multiply_scatter(7, parts_of(hidden), down_w)).astype(bf16)
-    d_normed_attn, layer_out = multiply_scatter(
-        6, parts_of(d_proj), proj_w, to_outer(layer_own).reshape(parted), False
-    )
+    layer_own = (resid_mid + layer_rows).astype(bf16)
+    d_normed_attn = multiply_scatter(6, parts_of(d_proj), proj_w)
     gain_attn_term = jnp.sum(d_normed_attn * unit_attn, axis=(0, 1))
     tokens_grad = (d_resid + norm_back(d_normed_attn, unit_attn, root_attn, gain_attn)).astype(bf16)
     small_rows = shard_rows // 128
@@ -1484,12 +1556,13 @@
         None,
         3,
     )
-    proj_rows = after(proj_rows, tokens_grad)
-    proj_grad, out_grad, small = send_back(
-        None,
-        (proj_rows, out_rows),
-        (proj_segments, ((0, query_part, 0),)),
-        (2 * (query_total + key_total), query_total),
+    attn_rows = after(attn_rows, tokens_grad)
+    proj_width = 2 * (query_total + key_total)
+    layer_out, attn_grad, small = send_back(
+        to_outer(layer_own).reshape(parted),
+        (attn_rows,),
+        (proj_segments + ((piece_widths[0], query_part, proj_width),),),
+        (proj_width + query_total,),
         tiles,
         4,
     )
@@ -1504,9 +1577,9 @@
         layer_out,
         tokens_grad,
         attention_gain_grad,
-        proj_grad.astype(f32),
+        attn_grad[:, :proj_width].astype(f32),
         sum_head,
-        out_grad.astype(f32),
+        attn_grad[:, proj_width:].astype(f32),
         feedforward_gain_grad,
         up_grad[:, :ff_width].astype(f32),
         up_grad[:, ff_width:].astype(f32),

time: 750 us -> 709 us (0.945)
  waiting for transfers between devices: 35.6 us -> 4.86 us
  local copies, waits for them, and re-layouts: 36.1 us -> 27.7 us
    pallas_call x3 -> x2, Pallas kernels: 159 us -> 101 us  [multiply_scatter(): pl.pallas_call(functools.partial(scatter_kernel, outward, swap_plan), out...]
    pallas_call x1, Pallas kernels: 19.4 us -> 52.1 us  [attend_back(): pl.pallas_call(functools.partial(attend_back_kernel, heads, min(256, leng...]
    all_gather x3 -> x2, waiting for transfers between devices: 34.7 us -> 4.78 us  [whole_columns(): return lax.all_gather(piece, 'ctx', axis=0, tiled=True)]
    pallas_call x1, Pallas kernels: 91.9 us -> 106 us  [prologue(): pl.pallas_call(functools.partial(prologue_kernel, weight_plan, planes), o...]
    unnamed x123 -> x119, local copies, waits for them, and re-layouts: 32.4 us -> 22.1 us
  transfers between devices with their start and end apart: 7 -> 5, of which waited for: 2 -> 1; matrix products, arithmetic and copies ran while one was open for 11% -> 13% of each run, Pallas kernels for 60% -> 59%
where the time goes in v4:
time: 709 us; the launch traced here: 706 us
  Pallas kernels  564 us (80%)
  matrix products  59.3 us (8%)
  other arithmetic  34.1 us (5%)
  local copies, waits for them, and re-layouts  27.7 us (4%)
  between operations  15 us (2%)
    pallas_call x2, Pallas kernels, send_back(): pl.pallas_call(functools.partial(return_kernel, plans, values is not None...  108 us
    pallas_call x1, Pallas kernels, prologue(): pl.pallas_call(functools.partial(prologue_kernel, weight_plan, planes), o...  106 us
    pallas_call x2, Pallas kernels, multiply_scatter(): pl.pallas_call(functools.partial(scatter_kernel, outward, swap_plan), out...  101 us
    pallas_call x2, Pallas kernels, plane_gather(): pl.pallas_call(plain_gather_kernel if values is None else gather_kernel,...  87.5 us
    pallas_call x1, Pallas kernels, attend_back(): pl.pallas_call(functools.partial(attend_back_kernel, heads, min(256, leng...  52.1 us
    pallas_call x1, Pallas kernels, feed_back(): pl.pallas_call(backward_kernel, out_shape=(jax.ShapeDtypeStruct((groups,...  51.5 us
    pallas_call x1, Pallas kernels, gather_and_feed(): pl.pallas_call(forward_kernel, out_shape=(jax.ShapeDtypeStruct((groups, 8...  41.9 us
    unnamed x119, local copies, waits for them, and re-layouts  22.1 us
  transfers between devices with their start and end apart: 5, of which 1 were waited for; matrix products, arithmetic and copies ran while one was open for 13% of the time, Pallas kernels for 59%

profile of v4, /device:TPU:0, one launch (start us, length us, event | category | flops | bytes accessed | tf_op | source)
XLA Modules:
  0.0 705.8 jit_solution(448150560890887911)
XLA Ops:
  14.8 106.2 %prologue.1 = (bf16[2,4,32,2048]{3,2,1,0:T(8,128)(2,1)S(1)}, bf16[8,8,32,2048]{3,2,1,0:T(8,128)(2,1)}, f32[8,8,128]{2,1,0:T(8,128)S(1)}, f32[8,8,128]{2,1,0:T(8,...) custom-call(bf16[8,32,2048]{2,1,0:T(8,128)(2,1)S(1)} %bitcast.76, ...), custom_call_target="tpu_custom_call" | custom-call | tf_op jit(solution)/shard_map/prologue/pallas_call | solution.py:928
  122.8 1.9 fusion.1
  125.1 11.1 %fusion.10.p_ref = f32[2,1024,768]{2,1,0:T(8,128)} fusion(bf16[2,1024,2048]{2,1,0:T(8,128)(2,1)} %bitcast.109, bf16[2048,768,1]{1,0,2:T(8,128)(2,1)S(1)} %bitcast.112), kind=kOutput, calls=%fused_computation.90 | convolution fusion | flops 6442450944 | bytes 17825792 | tf_op jit(solution)/shard_map/dot_general | solution.py:1444
  136.6 16.1 %attend.1 = (bf16[2,1024,256]{2,1,0:T(8,128)(2,1)S(1)}, f32[2,1024,256]{2,1,0:T(8,128)}, bf16[2,1024,256]{2,1,0:T(8,128)(2,1)S(1)}, bf16[2,1024,128]{2,1,0:T(8,128)(2,1)S(1)}, f32[2,2,1024,128]{3,2,1,0:T(8,128)}) custom-call(f32[2,1024,768]{2,1,0:T(8,128)} %fusion.10.p_ref, f32[2,128]{1,0:T(2,128)S(1)} %convert_element_type.93.gain_ref, ...), custom_call_target="tpu_custom_call" | custom-call | flops 2147483648 | bytes 16777216 | tf_op jit(solution)/shard_map/attend/pallas_call | solution.py:1262
  154.9 59.2 %multiply_scatter.2 = (f32[8,32,2048]{2,1,0:T(8,128)S(1)}, bf16[2,4,16,2048]{3,2,1,0:T(8,128)(2,1)S(1)}, bf16[2,256,768]{2,1,0:T(8,128)(2,1)S(1)}) custom-call(bf16[8,8,32,256]{3,2,1,0:T(8,128)(2,1)S(1)} %bitcast.86, bf16[2048,256]{1,0:T(8,128)(2,1)S(1)} %bitcast.84, bf16[8,16,2048]{2,1,0:T(8,128)(2,1)S(1)} %get-tuple-element.107.refs_2_, ...), custom_call_target="tpu_custom_call" | custom-call | flops 2147483648 | bytes 9437184 | tf_op jit(solution)/shard_map/multiply_scatter/pallas_call | solution.py:433
  216.2 1.7 bitcast_multiply_fusion
  217.9 1.4 copy-done.24
  220.1 1.9 multiply_convert_fusion.x_ref
  222.0 47.9 %plane_gather.2 = (bf16[8,8,32,2048]{3,2,1,0:T(8,128)(2,1)}, bf16[2,4,16,2048]{3,2,1,0:T(8,128)(2,1)S(1)}) custom-call(bf16[8,32,2048]{2,1,0:T(8,128)(2,1)S(1)} %multiply_convert_fusion.x_ref, bf16[8,16,2048]{2,1,0:T(8,128)(2,1)S(1)} %copy-done.5), custom_call_target="tpu_custom_call" | custom-call | tf_op jit(solution)/shard_map/plane_gather/pallas_call | solution.py:164
  270.0 41.9 %gather_and_feed.1 = (bf16[8,8,32,2048]{3,2,1,0:T(8,128)(2,1)}, f32[8,8,32,1536]{3,2,1,0:T(8,128)}, bf16[8,8,32,768]{3,2,1,0:T(8,128)(2,1)S(1)}) custom-call(bf16[8,32,2048]{2,1,0:T(8,128)(2,1)S(1)} %bitcast.73, bf16[8,8,32,2048]{3,2,1,0:T(8,128)(2,1)} %get-tuple-element.68.h_ref, bf16[2048,1536]{1,0:T(8,128)(2,1)} %all-gather.3.cloned.1.call-done.w_ref.up_ref), custom_call_target="tpu_custom_call" | custom-call | flops 12884901888 | bytes 14680064 | tf_op jit(solution)/shard_map/gather_and_feed/pallas_call | solution.py:522
  311.9 1.7 copy-done.23
  313.6 10.4 %bitcast_convert_fusion.1 = bf16[2048,768]{1,0:T(8,128)(2,1)} fusion(bf16[8,8,32,2048]{3,2,1,0:T(8,128)(2,1)} %get-tuple-element.72.g_ref, bf16[8,8,32,768]{3,2,1,0:T(8,128)(2,1)S(1)} %get-tuple-element.71.a_ref), kind=kOutput, calls=%fused_computation.1 | convolution fusion | flops 6444023808 | bytes 14680064 | tf_op jit(solution)/shard_map/dot_general | solution.py:1488
  324.3 4.8 all-gather.5.cloned.1.call-done.down_ref.w_ref
  329.0 1.9 copy-done.14
  330.9 51.5 %feed_back.1 = (f32[8,32,2048]{2,1,0:T(8,128)S(1)}, bf16[8,8,32,1536]{3,2,1,0:T(8,128)(2,1)}) custom-call(bf16[8,8,32,2048]{3,2,1,0:T(8,128)(2,1)} %get-tuple-element.72.g_ref, f32[8,8,32,1536]{3,2,1,0:T(8,128)} %get-tuple-element.73.lin_ref, bf16[2048,768]{1,0:T(8,128)(2,1)S(1)} %copy-done.14, bf16[2048,1536]{1,0:T(8,128)(2,1)} %all-gather.3.cloned.1.call-done.w_ref.up_ref), custom_call_target="tpu_custom_call" | custom-call | flops 19327352832 | bytes 35651584 | tf_op jit(solution)/shard_map/feed_back/pallas_call | solution.py:622
  382.5 17.1 %bitcast_convert_fusion = bf16[2048,1536]{1,0:T(8,128)(2,1)} fusion(bf16[8,8,32,2048]{3,2,1,0:T(8,128)(2,1)S(1)} %copy-done.39, bf16[8,8,32,1536]{3,2,1,0:T(8,128)(2,1)} %get-tuple-element.76), kind=kOutput, calls=%fused_computation | convolution fusion | flops 12888047616 | bytes 20971520 | tf_op jit(solution)/shard_map/dot_general | solution.py:1494
  399.6 2.3 multiply_reduce_fusion
  402.6 39.6 %plane_gather.3 = bf16[8,8,32,2048]{3,2,1,0:T(8,128)(2,1)} custom-call(bf16[8,32,2048]{2,1,0:T(8,128)(2,1)S(1)} %fusion.7.x_ref), custom_call_target="tpu_custom_call" | custom-call | tf_op jit(solution)/shard_map/plane_gather/pallas_call | solution.py:164
  442.2 7.2 %fusion.11 = f32[2048,256]{1,0:T(8,128)} fusion(bf16[2048,2048]{1,0:T(8,128)(2,1)} %bitcast.90, bf16[2048,256]{1,0:T(8,128)(2,1)S(1)} %bitcast.85), kind=kOutput, calls=%fused_computation.91 | convolution fusion | flops 2147483648 | bytes 11534336 | tf_op jit(solution)/shard_map/dot_general | solution.py:1502
  449.5 3.3 convolution_convert_fusion.1
  452.8 52.1 %attend_back.1 = (bf16[2,1024,768]{2,1,0:T(8,128)(2,1)}, f32[8,128]{1,0:T(8,128)}, f32[8,32,2048]{2,1,0:T(8,128)}) custom-call(f32[2,1024,256]{2,1,0:T(8,128)} %bitcast.113, f32[2,1024,768]{2,1,0:T(8,128)} %fusion.10.p_ref, f32[2,128]{1,0:T(2,128)} %copy-done.13, f32[1024,128]{1,0:T(8,128)} %copy-done.3, f32[1024,128]{1,0:T(8,128)} %copy-done.4, ...), custom_call_target="tpu_custom_call" | custom-call | flops 11811160064 | bytes 33554432 | tf_op jit(solution)/shard_map/attend_back/pallas_call | solution.py:1297
  504.9 10.2 %convolution_convert_fusion = bf16[2048,768]{0,1:T(8,128)(2,1)S(1)} fusion(bf16[2048,2048]{1,0:T(8,128)(2,1)} %bitcast.110, bf16[2048,768]{1,0:T(8,128)(2,1)} %bitcast.88), kind=kOutput, calls=%fused_computation.3 | convolution fusion | flops 6444023808 | bytes 14680064 | tf_op jit(solution)/shard_map/dot_general | solution.py:1518
  515.2 2.3 pad_maximum_fusion
  518.3 1.9 copy-done.22
  520.2 41.7 %multiply_scatter.3 = f32[8,32,2048]{2,1,0:T(8,128)S(1)} custom-call(bf16[8,8,32,768]{3,2,1,0:T(8,128)(2,1)S(1)} %bitcast.89, bf16[2048,768]{1,0:T(8,128)(2,1)} %bitcast.111), custom_call_target="tpu_custom_call" | custom-call | flops 6442450944 | bytes 11534336 | tf_op jit(solution)/shard_map/multiply_scatter/pallas_call | solution.py:433
  566.9 65.4 %send_back.2 = (bf16[8,32,2048]{2,1,0:T(8,128)(2,1)S(1)}, bf16[256,12288]{1,0:T(8,128)(2,1)}, bf16[256,6144]{1,0:T(8,128)(2,1)}) custom-call(bf16[2,4,32,2048]{3,2,1,0:T(8,128)(2,1)S(1)} %bitcast.77, bf16[2,256,1536]{2,1,0:T(8,128)(2,1)S(1)} %bitcast.75, bf16[2,256,768]{2,1,0:T(8,128)(2,1)S(1)} %bitcast.82), custom_call_target="tpu_custom_call" | custom-call | tf_op jit(solution)/shard_map/send_back/pallas_call | solution.py:1061
  632.3 5.5 convert_element_type.115
  638.1 6.4 slice_convert_fusion
  644.5 1.5 copy.22
  646.0 42.4 %send_back.3 = (bf16[8,32,2048]{2,1,0:T(8,128)(2,1)S(1)}, bf16[256,8192]{1,0:T(8,128)(2,1)}, f32[8,128]{1,0:T(8,128)S(1)}) custom-call(bf16[2,4,32,2048]{3,2,1,0:T(8,128)(2,1)S(1)} %bitcast.78, bf16[2,256,1024]{2,1,0:T(8,128)(2,1)S(1)} %bitcast.74, f32[4,2,8,128]{3,2,1,0:T(8,128)S(1)} %maximum_maximum_fusion.refs_2_), custom_call_target="tpu_custom_call" | custom-call | tf_op jit(solution)/shard_map/send_back/pallas_call | solution.py:1061
  688.4 5.3 slice_convert_fusion.2
  693.7 2.8 slice_convert_fusion.3
  (166 shorter events, 24.4 us)
Async XLA Ops:
  7.2 7.5 %copy-start.35 = (s32[1024]{0:T(1024)S(1)}, s32[1024]{0:T(1024)}, u32[]{:S(2)}) copy-start(s32[1024]{0:T(1024)} %param.17) | copy-start | bytes 12292
  7.2 7.5 %copy-start.36 = (s32[1024]{0:T(1024)S(1)}, s32[1024]{0:T(1024)}, u32[]{:S(2)}) copy-start(s32[1024]{0:T(1024)} %param.16) | copy-start | bytes 12292
  7.2 7.6 %copy-start.38 = (bf16[256]{0:T(256)(128)(2,1)S(1)}, bf16[256]{0:T(256)(128)(2,1)}, u32[]{:S(2)}) copy-start(bf16[256]{0:T(256)(128)(2,1)} %param.18) | copy-start | bytes 1540
  7.2 7.6 %copy-start.37 = (bf16[256]{0:T(256)(128)(2,1)S(1)}, bf16[256]{0:T(256)(128)(2,1)}, u32[]{:S(2)}) copy-start(bf16[256]{0:T(256)(128)(2,1)} %param.22) | copy-start | bytes 1540
  7.2 7.6 %copy-start.7 = (bf16[256,2048]{1,0:T(8,128)(2,1)S(1)}, bf16[256,2048]{1,0:T(8,128)(2,1)}, u32[]{:S(2)}) copy-start(bf16[256,2048]{1,0:T(8,128)(2,1)} %out_ref.1) | copy-start | bytes 3145732
  7.2 262.8 %all-gather.3.cloned.1.call-start = ((), (), s32[]{:S(2)}) async-start(), calls=%async_computation.3 | async-start | bytes 7864320 | tf_op jit(solution)/shard_map/all_gather | solution.py:1393
  14.8 107.9 %copy-start.41 = (bf16[2,128]{1,0:T(2,128)(2,1)S(1)}, bf16[2,128]{1,0:T(2,128)(2,1)}, u32[]{:S(2)}) copy-start(bf16[2,128]{1,0:T(2,128)(2,1)} %param.20) | copy-start | bytes 1540
  122.0 94.1 %copy-start = (bf16[2,4,32,2048]{3,2,1,0:T(8,128)(2,1)}, bf16[2,4,32,2048]{3,2,1,0:T(8,128)(2,1)S(1)}, u32[]{:S(2)}) copy-start(bf16[2,4,32,2048]{3,2,1,0:T(8,128)(2,1)S(1)} %get-tuple-element.58) | copy-start | bytes 3145732
  122.0 207.0 %all-gather.5.cloned.1.call-start = ((), (), s32[]{:S(2)}) async-start(), calls=%async_computation.4 | async-start | bytes 3932160 | tf_op jit(solution)/shard_map/all_gather | solution.py:1393
  122.7 13.8 %copy-start.13 = (f32[2,128]{1,0:T(2,128)}, f32[2,128]{1,0:T(2,128)S(1)}, u32[]{:S(2)}) copy-start(f32[2,128]{1,0:T(2,128)S(1)} %convert_element_type.93.gain_ref) | copy-start | bytes 3076
  125.1 11.5 %copy-start.3 = (f32[1024,128]{1,0:T(8,128)}, f32[1024,128]{1,0:T(8,128)S(1)}, u32[]{:S(2)}) copy-start(f32[1024,128]{1,0:T(8,128)S(1)} %get-tuple-element.116.cos_ref) | copy-start | bytes 1572868
  125.1 11.5 %copy-start.4 = (f32[1024,128]{1,0:T(8,128)}, f32[1024,128]{1,0:T(8,128)S(1)}, u32[]{:S(2)}) copy-start(f32[1024,128]{1,0:T(8,128)S(1)} %get-tuple-element.117.sin_ref) | copy-start | bytes 1572868
  136.5 16.2 %copy-start.2 = (f32[2,1024,128]{2,1,0:T(8,128)}, f32[2,1024,128]{2,1,0:T(8,128)S(1)}, u32[]{:S(2)}) copy-start(f32[2,1024,128]{2,1,0:T(8,128)S(1)} %broadcast_in_dim.9.qcode_ref) | copy-start | bytes 3145732
  136.6 16.1 %copy-start.12 = (f32[2,8,1024]{2,1,0:T(8,128)}, f32[2,8,1024]{2,1,0:T(8,128)S(1)}, u32[]{:S(2)}) copy-start(f32[2,8,1024]{2,1,0:T(8,128)S(1)} %broadcast_in_dim.10.kcode_ref) | copy-start | bytes 196612
  136.6 16.1 %copy-start.30 = (bf16[256,2048]{1,0:T(8,128)(2,1)S(1)}, bf16[256,2048]{1,0:T(8,128)(2,1)}, u32[]{:S(2)}) copy-start(bf16[256,2048]{1,0:T(8,128)(2,1)} %param.15) | copy-start | bytes 3145732
  215.8 237.0 %reduce-scatter.4.cloned.1.call-start = ((), (), s32[]{:S(2)}) async-start(), calls=%async_computation.5 | async-start | bytes 3932160 | tf_op jit(solution)/shard_map/reduce_scatter | solution.py:1480
  219.4 2.6 copy-start.5
  220.1 49.8 %copy-start.11 = (bf16[2,4,16,2048]{3,2,1,0:T(8,128)(2,1)S(1)}, bf16[2,4,16,2048]{3,2,1,0:T(8,128)(2,1)}, u32[]{:S(2)}) copy-start(bf16[2,4,16,2048]{3,2,1,0:T(8,128)(2,1)} %copy-done.10) | copy-start | bytes 1572868
  324.0 194.3 %reduce-scatter.8.cloned.1.call-start = ((), (), s32[]{:S(2)}) async-start(), calls=%async_computation.7 | async-start | bytes 7864320 | tf_op jit(solution)/shard_map/reduce_scatter | solution.py:1480
  330.9 51.5 %copy-start.39 = (bf16[8,8,32,2048]{3,2,1,0:T(8,128)(2,1)S(1)}, bf16[8,8,32,2048]{3,2,1,0:T(8,128)(2,1)}, u32[]{:S(2)}) copy-start(bf16[8,8,32,2048]{3,2,1,0:T(8,128)(2,1)} %get-tuple-element.68.h_ref) | copy-start | bytes 25165828
  399.5 245.0 %reduce-scatter.6.cloned.1.call-start = ((), (), s32[]{:S(2)}) async-start(), calls=%async_computation.6 | async-start | bytes 5242880 | tf_op jit(solution)/shard_map/reduce_scatter | solution.py:1480
  399.6 2.3 copy-start.25
  402.6 39.7 %copy-start.17 = (bf16[4,2,256,256]{3,2,1,0:T(8,128)(2,1)S(1)}, bf16[4,2,256,256]{3,2,1,0:T(8,128)(2,1)}, u32[]{:S(2)}) copy-start(bf16[4,2,256,256]{3,2,1,0:T(8,128)(2,1)} %copy-done.15) | copy-start | bytes 3145732
  442.2 7.2 %copy-start.20 = (bf16[2,1024,256]{2,1,0:T(8,128)(2,1)S(1)}, bf16[2,1024,256]{2,1,0:T(8,128)(2,1)}, u32[]{:S(2)}) copy-start(bf16[2,1024,256]{2,1,0:T(8,128)(2,1)} %copy-done.19) | copy-start | bytes 3145732
  442.2 7.2 %copy-start.28 = (bf16[8,8,32,2048]{3,2,1,0:T(8,128)(2,1)S(1)}, bf16[8,8,32,2048]{3,2,1,0:T(8,128)(2,1)}, u32[]{:S(2)}) copy-start(bf16[8,8,32,2048]{3,2,1,0:T(8,128)(2,1)} %plane_gather.3) | copy-start | bytes 25165828
  504.9 10.2 %copy-start.31 = (bf16[2048,256]{0,1:T(8,128)(2,1)S(1)}, bf16[2048,256]{0,1:T(8,128)(2,1)}, u32[]{:S(2)}) copy-start(bf16[2048,256]{0,1:T(8,128)(2,1)} %convolution_convert_fusion.1) | copy-start | bytes 3145732
  520.2 41.7 %copy-start.1 = (bf16[2,4,32,2048]{3,2,1,0:T(8,128)(2,1)S(1)}, bf16[2,4,32,2048]{3,2,1,0:T(8,128)(2,1)}, u32[]{:S(2)}) copy-start(bf16[2,4,32,2048]{3,2,1,0:T(8,128)(2,1)} %copy-done) | copy-start | bytes 3145732
  520.2 41.7 %copy-start.27 = (f32[8,32,2048]{2,1,0:T(8,128)S(1)}, f32[8,32,2048]{2,1,0:T(8,128)}, u32[]{:S(2)}) copy-start(f32[8,32,2048]{2,1,0:T(8,128)} %get-tuple-element.104) | copy-start | bytes 6291460
  520.2 41.7 %copy-start.32 = (f32[8,1,256]{2,1,0:T(1,128)S(1)}, f32[8,1,256]{2,1,0:T(1,128)}, u32[]{:S(2)}) copy-start(f32[8,1,256]{2,1,0:T(1,128)} %get-tuple-element.108) | copy-start | bytes 24580
  520.2 41.7 %copy-start.34 = (f32[2,4,32]{2,1,0:T(4,128)S(1)}, f32[2,4,32]{2,1,0:T(4,128)}, u32[]{:S(2)}) copy-start(f32[2,4,32]{2,1,0:T(4,128)} %copy-done.33) | copy-start | bytes 3076
  632.3 5.8 slice-start
  632.3 5.8 slice-start.1
  (17 other events, 26.3 us)
Sparse Core Ops, SparseCore 0:
  122.2 143.0 all-gather.2
  267.3 61.6 all-gather.4
  331.9 58.8 reduce-scatter.3
  399.7 108.6 reduce-scatter.7
  517.6 91.3 reduce-scatter.5

commit v5 on v4

--- a/solution.py
+++ b/solution.py
@@ -85,7 +85,7 @@
         self.back = slot(1 - row, core, seq)
         self.diag = slot(1 - row, core, 1 - seq)
         self.send = sender(plane_neighbours(), send_sem, recv_sem)
-        self.x_ref, self.o_ref = x_ref, o_ref
+        self.x_ref, self.o_ref, self.waited = x_ref, o_ref, ()
         self.local = pltpu.make_async_copy(x_ref, o_ref.at[:, self.own], local_sem)
         half = o_ref.shape[0] // 2
         self.first = pl.ds(0, half)
@@ -109,6 +109,11 @@
         self.to_y.wait_recv()
         self.on_x = self.pass_on(5, self.second, self.back, "x")
         self.back_c = self.pass_on(6, None, self.back, "c")
+
+    def early(self):
+        self.waited = (self.to_c, self.side_c, self.back_c)
+        for copy in self.waited:
+            copy.wait_recv()
 
     def finish(self):
         self.on_y.wait_recv()
@@ -118,7 +123,8 @@
         self.local.wait()
         late = (self.to_c, self.side_c, self.back_c, diag_first, diag_second)
         for copy in late:
-            copy.wait_recv()
+            if all(copy is not other for other in self.waited):
+                copy.wait_recv()
         for copy in (self.to_x, self.to_y, self.on_y, self.on_x) + late:
             copy.wait_send()
 
@@ -141,40 +147,24 @@
     mover.finish()
 
 
-def plain_gather_kernel(x_ref, o_ref, local_sem, send_sem, recv_sem):
-    near = plane_neighbours()
-    greet([near["c"], near["x"], near["y"]])
-    gather = Gather(x_ref, o_ref, local_sem, send_sem, recv_sem)
-    gather.start()
-    gather.middle()
-    gather.finish()
-
-
-def plane_gather(block, values=None):
+def plane_gather(block, values):
     groups, rows, width = block.shape
     dma = pltpu.SemaphoreType.DMA
     anywhere = pl.BlockSpec(memory_space=pl.ANY)
-    ins = [block]
-    outs = [jax.ShapeDtypeStruct((groups, 8, rows, width), block.dtype)]
-    scratch = [dma, dma((9,)), dma((9,))]
-    if values is not None:
-        ins.append(values)
-        outs.append(exchanged(values, True))
-        scratch += exchange_scratch(values)
-    result = pl.pallas_call(
-        plain_gather_kernel if values is None else gather_kernel,
-        out_shape=tuple(outs),
-        in_specs=[anywhere] * len(ins),
-        out_specs=(anywhere,) * len(outs),
-        scratch_shapes=scratch,
+    return pl.pallas_call(
+        gather_kernel,
+        out_shape=(
+            jax.ShapeDtypeStruct((groups, 8, rows, width), block.dtype),
+            exchanged(values, True),
+        ),
+        in_specs=[anywhere] * 2,
+        out_specs=(anywhere,) * 2,
+        scratch_shapes=[dma, dma((9,)), dma((9,))] + exchange_scratch(values),
         compiler_params=pltpu.CompilerParams(
-            collective_id=0 if values is None else 9,
-            has_side_effects=True,
-            vmem_limit_bytes=VMEM_LIMIT,
+            collective_id=9, has_side_effects=True, vmem_limit_bytes=VMEM_LIMIT
         ),
         name="plane_gather",
-    )(*ins)
-    return result[0] if values is None else result
+    )(block, values)
 
 
 class Swap:
@@ -513,6 +503,89 @@
     gather.finish()
 
 
+def apply_kernel(
+    x_ref, w_ref, x_all, y_ref,
+    local_sem, send_sem, recv_sem, x_buf, w_buf, y_buf, x_sem, w_sem, y_sem,
+):
+    near = plane_neighbours()
+    slot_of, row, core, seq = plane_slots()
+    order = [
+        slot_of(r, c, s)
+        for r, s in ((row, seq), (row, 1 - seq), (1 - row, seq), (1 - row, 1 - seq))
+        for c in (core, 1 - core)
+    ]
+    w_load = pltpu.make_async_copy(w_ref, w_buf, w_sem)
+    w_load.start()
+    greet([near["c"], near["x"], near["y"]])
+    gather = Gather(x_ref, x_all, local_sem, send_sem, recv_sem)
+    gather.start()
+    w_load.wait()
+    groups, rows, depth = x_buf.shape[1:]
+
+    def store(index):
+        return pltpu.make_async_copy(
+            y_buf.at[index], y_ref.at[:, order[index]], y_sem.at[index]
+        )
+
+    def apply(indices):
+        copies = []
+        for index in indices:
+            source = x_ref if index == 0 else x_all.at[:, order[index]]
+            copy = pltpu.make_async_copy(source, x_buf.at[index], x_sem.at[index])
+            copy.start()
+            copies.append(copy)
+        for index, copy in zip(indices, copies):
+            copy.wait()
+            product = jnp.dot(
+                x_buf[index].reshape(groups * rows, depth),
+                w_buf[...],
+                preferred_element_type=jnp.float32,
+            )
+            y_buf[index] = product.reshape(y_buf.shape[1:])
+            store(index).start()
+
+    apply([0])
+    gather.middle()
+    gather.early()
+    apply([1, 2, 3, 4, 5])
+    gather.finish()
+    apply([6, 7])
+    for index in range(8):
+        store(index).wait()
+
+
+def gather_and_apply(block, weight):
+    groups, rows, width = block.shape
+    kind = block.dtype
+    columns = weight.shape[1]
+    dma = pltpu.SemaphoreType.DMA
+    anywhere = pl.BlockSpec(memory_space=pl.ANY)
+    return pl.pallas_call(
+        apply_kernel,
+        out_shape=(
+            jax.ShapeDtypeStruct((groups, 8, rows, width), kind),
+            jax.ShapeDtypeStruct((groups, 8, rows, columns), jnp.float32),
+        ),
+        in_specs=[anywhere] * 2,
+        out_specs=(anywhere,) * 2,
+        scratch_shapes=[
+            dma,
+            dma((9,)),
+            dma((9,)),
+            pltpu.VMEM((8, groups, rows, width), kind),
+            pltpu.VMEM(weight.shape, kind),
+            pltpu.VMEM((8, groups, rows, columns), jnp.float32),
+            dma((8,)),
+            dma,
+            dma((8,)),
+        ],
+        compiler_params=pltpu.CompilerParams(
+            collective_id=0, has_side_effects=True, vmem_limit_bytes=VMEM_LIMIT
+        ),
+        name="gather_and_apply",
+    )(block, weight)
+
+
 def gather_and_feed(block, normed, weight):
     groups, rows, width = block.shape
     kind = block.dtype
@@ -552,11 +625,12 @@
     )(block, normed, weight)
 
 
-def backward_kernel(
-    g_ref, lin_ref, down_ref, up_ref, o_ref, d_ref, *refs,
-):
+def backward_kernel(g_ref, lin_ref, down_ref, up_ref, h_ref, o_ref, part_ref, *refs):
     scatter = Scatter(*refs[:9])
-    g_buf, lin_buf, d_buf, down_buf, up_buf, g_sem, lin_sem, d_sem, w_sem = refs[9:]
+    (
+        g_buf, lin_buf, d_buf, down_buf, up_buf, h_buf, part_buf,
+        g_sem, lin_sem, w_sem, h_sem, part_sem,
+    ) = refs[9:]
     weights = (
         pltpu.make_async_copy(down_ref, down_buf, w_sem.at[0]),
         pltpu.make_async_copy(up_ref, up_buf, w_sem.at[1]),
@@ -568,10 +642,6 @@
             pltpu.make_async_copy(g_ref.at[:, d], g_buf.at[slot], g_sem.at[slot]),
             pltpu.make_async_copy(lin_ref.at[:, d], lin_buf.at[slot], lin_sem.at[slot]),
         )
-
-    def store(index):
-        slot, d = index % 2, scatter.order[index]
-        return pltpu.make_async_copy(d_buf.at[slot], d_ref.at[:, d], d_sem.at[slot])
 
     weights[0].start()
     for copy in loads(0):
@@ -590,8 +660,6 @@
         if index < 7:
             for copy in loads(index + 1):
                 copy.start()
-        if index > 1:
-            store(index - 2).wait()
         groups, rows, width = target.shape
         d_hidden = jnp.dot(
             g_buf[slot].reshape(groups * rows, width),
@@ -601,54 +669,103 @@
         gate, up, sig, silu = silu_parts(lin_buf[slot].reshape(groups * rows, 2 * part))
         d_gate = d_hidden * up * sig * (1.0 + gate * (1.0 - sig))
         d_up = d_hidden * silu
-        d_buf[slot, :, :, :part] = d_gate.astype(d_buf.dtype).reshape(groups, rows, part)
-        d_buf[slot, :, :, part:] = d_up.astype(d_buf.dtype).reshape(groups, rows, part)
-        store(index).start()
-        multiply_into(d_buf[slot].reshape(groups * rows, 2 * part), up_buf, target)
+        d_buf[index, :, :, :part] = d_gate.astype(d_buf.dtype).reshape(groups, rows, part)
+        d_buf[index, :, :, part:] = d_up.astype(d_buf.dtype).reshape(groups, rows, part)
+        multiply_into(d_buf[index].reshape(groups * rows, 2 * part), up_buf, target)
 
     scatter.start(produce)
     scatter.middle()
-    for index in (6, 7):
-        store(index).wait()
+
+    tile = h_buf.shape[-1]
+    count = h_ref.shape[-1] // tile
+    tokens = 8 * h_buf.shape[2] * h_buf.shape[3]
+
+    def tile_loads(k, slot):
+        columns = pl.ds(pl.multiple_of(k * tile, tile), tile)
+        return [
+            pltpu.make_async_copy(
+                h_ref.at[:, d, :, columns], h_buf.at[slot, index], h_sem.at[slot, index]
+            )
+            for index, d in enumerate(scatter.order)
+        ]
+
+    def store(k, slot):
+        rows = pl.ds(pl.multiple_of(k * tile, tile), tile)
+        return pltpu.make_async_copy(part_buf.at[slot], part_ref.at[rows, :], part_sem.at[slot])
+
+    for copy in tile_loads(0, 0):
+        copy.start()
+
+    def body(k, carry):
+        slot = lax.rem(k, 2)
+        for copy in tile_loads(k, slot):
+            copy.wait()
+
+        @pl.when(k < count - 1)
+        def _():
+            for copy in tile_loads(k + 1, 1 - slot):
+                copy.start()
+
+        @pl.when(k > 1)
+        def _():
+            store(k - 2, slot).wait()
+
+        product = lax.dot_general(
+            h_buf[slot].reshape(tokens, tile),
+            d_buf[...].reshape(tokens, 2 * part),
+            contract_rows,
+            preferred_element_type=jnp.float32,
+        )
+        part_buf[slot] = product.astype(part_buf.dtype)
+        store(k, slot).start()
+        return carry
+
+    lax.fori_loop(0, count, body, 0)
+    for k in (count - 2, count - 1):
+        store(k, k % 2).wait()
     scatter.finish(o_ref)
 
 
-def feed_back(grads, linear, down, up):
+def feed_back(grads, linear, down, up, normed):
     groups, _, rows, width = grads.shape
     kind = grads.dtype
     both = up.shape[1]
+    tile = 256
     dma = pltpu.SemaphoreType.DMA
     anywhere = pl.BlockSpec(memory_space=pl.ANY)
     return pl.pallas_call(
         backward_kernel,
         out_shape=(
             jax.ShapeDtypeStruct((groups, rows, width), jnp.float32),
-            jax.ShapeDtypeStruct((groups, 8, rows, both), kind),
+            jax.ShapeDtypeStruct((width, both), kind),
         ),
-        in_specs=[anywhere] * 4,
+        in_specs=[anywhere] * 5,
         out_specs=(pl.BlockSpec(memory_space=pltpu.VMEM), anywhere),
         scratch_shapes=scatter_scratch(groups, rows, width, kind)
         + [
             pltpu.VMEM((2, groups, rows, width), kind),
             pltpu.VMEM((2, groups, rows, both), jnp.float32),
-            pltpu.VMEM((2, groups, rows, both), kind),
+            pltpu.VMEM((8, groups, rows, both), kind),
             pltpu.VMEM(down.shape, kind),
             pltpu.VMEM(up.shape, kind),
+            pltpu.VMEM((2, 8, groups, rows, tile), kind),
+            pltpu.VMEM((2, tile, both), kind),
             dma((2,)),
             dma((2,)),
             dma((2,)),
+            dma((2, 8)),
             dma((2,)),
         ],
         compiler_params=pltpu.CompilerParams(
-            collective_id=1, has_side_effects=True, vmem_limit_bytes=VMEM_LIMIT
+            collective_id=1, has_side_effects=True, vmem_limit_bytes=58 * 1024 * 1024
         ),
         cost_estimate=pl.CostEstimate(
-            flops=24 * groups * rows * width * both,
+            flops=40 * groups * rows * width * both,
             bytes_accessed=16 * groups * rows * (2 * width + 3 * both),
             transcendentals=4 * groups * rows * both,
         ),
         name="feed_back",
-    )(grads, linear, down, up)
+    )(grads, linear, down, up, normed)
 
 
 class Exchange:
@@ -829,7 +946,7 @@
     weight_plan, planes,
     tokens_ref, layout_ref, gain_ref, proj_ref, out_ref, gate_ref, up_ref,
     own_tokens, normed_all, lay_out, gain_out, proj_full, out_full, up_piece,
-    normed, stage, small_send, small_recv, ex_send, ex_recv, local_sem, g_send, g_recv,
+    normed, stage, inner, inner_sem, small_send, small_recv, ex_send, ex_recv, local_sem, g_send, g_recv,
     w_local, w_send, w_recv, up_send, line_down, line_recv, out_up, out_down, out_recv,
 ):
     far, row, core, seq, ctx = place()
@@ -840,6 +957,18 @@
     owners = [
         (far, row, core, (line + k) % 2, ((line + k) % total) // 2) for k in range(1, total)
     ]
+    shard = tokens_ref.shape[-1] // total
+    reorders = [
+        pltpu.make_async_copy(
+            tokens_ref.at[:, :, pl.ds((x * planes + z) * shard, shard)],
+            inner.at[:, :, pl.ds((z * 2 + x) * shard, shard)],
+            inner_sem.at[z * 2 + x],
+        )
+        for z in range(planes)
+        for x in range(2)
+    ]
+    for copy in reorders:
+        copy.start()
     greet(mates + owners)
     weights = {"proj": proj_ref, "out": out_ref, "gate": gate_ref, "up": up_ref}
     pieces = {"proj": proj_full.at[ctx], "out": out_full.at[ctx], "up": up_piece}
@@ -849,7 +978,9 @@
     other_parts = [i for i, plan in enumerate(weight_plan) if plan[3] == "up"]
     for index in proj_parts:
         swap.start(index)
-    tokens = Exchange(True, tokens_ref, own_tokens, stage, ex_send, ex_recv)
+    for copy in reorders:
+        copy.wait()
+    tokens = Exchange(True, inner, own_tokens, stage, ex_send, ex_recv)
     tokens.start()
     lay_out[own] = layout_ref[...]
     gain_out[line] = gain_ref[...]
@@ -939,6 +1070,8 @@
         scratch_shapes=[
             pltpu.VMEM((8, rows, width), kind),
             pltpu.VMEM((8, rows, width), kind),
+            pltpu.VMEM((8, rows, width), kind),
+            dma((2 * planes,)),
             dma((count,)),
             dma((count,)),
             dma((16,)),
@@ -1403,7 +1536,7 @@
     grad_here = (cotangent.astype(f32) * pad_here.astype(f32)[:, None]).astype(bf16)
     chunked = (plane_size, chunk, model_width)
     tokens_own, normed_attn, layouts, gains, proj_w, out_w, up_piece = prologue(
-        to_inner(tokens).reshape(chunked),
+        tokens.reshape(chunked),
         layout_pack,
         gain_pack,
         (projection_weight, out_weight, gate_weight, up_weight),
@@ -1472,7 +1605,6 @@
         groups, chunk, model_width
     )
     grad_all, linear, hidden = gather_and_feed(own_grad, normed_all, up_w)
-    normed_mlp = normed_all.reshape(plane_tokens, model_width)
     grad_low = grad_all.reshape(plane_tokens, model_width)
     hidden = hidden.reshape(plane_tokens, ff_part)
 
@@ -1489,17 +1621,14 @@
         grad_low, hidden, contract_rows, preferred_element_type=f32
     ).astype(bf16)
     down_rows = grads_to_rows(down_part)
-    d_normed_mlp, d_both = feed_back(after(grad_all, down_part), linear, down_w, up_w)
-    d_both = d_both.reshape(plane_tokens, 2 * ff_part)
-    up_part = lax.dot_general(
-        normed_mlp, d_both, contract_rows, preferred_element_type=f32
-    ).astype(bf16)
+    d_normed_mlp, up_part = feed_back(
+        after(grad_all, down_part), linear, down_w, up_w, normed_all
+    )
     up_rows = grads_to_rows(up_part)
-    d_normed_mlp = after(d_normed_mlp, up_part)
     gain_mlp_term = jnp.sum(d_normed_mlp * unit_mlp, axis=(0, 1))
     d_resid = own_grad.astype(f32) + norm_back(d_normed_mlp, unit_mlp, root_mlp, gain_mlp)
-    d_attn_low = plane_gather(d_resid.astype(bf16)).reshape(plane_tokens, model_width)
-    mixed_grad = jnp.dot(d_attn_low, out_w, preferred_element_type=f32)
+    d_attn_low, mixed_grad = gather_and_apply(d_resid.astype(bf16), out_w)
+    d_attn_low = d_attn_low.reshape(plane_tokens, model_width)
     out_part = lax.dot_general(
         d_attn_low, mixed, contract_rows, preferred_element_type=f32
     ).astype(bf16)
@@ -1519,11 +1648,11 @@
         normed_attn, d_proj, contract_rows, preferred_element_type=f32
     ).astype(bf16)
     attn_part = jnp.concatenate([proj_part, out_part], axis=1)
-    attn_rows = grads_to_rows(attn_part)
     d_proj = after(d_proj, attn_part, up_rows)
     parted = (held, planes, chunk, model_width)
     layer_own = (resid_mid + layer_rows).astype(bf16)
     d_normed_attn = multiply_scatter(6, parts_of(d_proj), proj_w)
+    attn_rows = grads_to_rows(attn_part)
     gain_attn_term = jnp.sum(d_normed_attn * unit_attn, axis=(0, 1))
     tokens_grad = (d_resid + norm_back(d_normed_attn, unit_attn, root_attn, gain_attn)).astype(bf16)
     small_rows = shard_rows // 128

time: 709 us -> 693 us (0.977)
  matrix products: 59.3 us -> 37.4 us
    dot_general x2 -> x0, matrix products: 24.3 us -> none  [the longest x1 17.1 us: per_device(): lax.dot_general(normed_mlp, d_both, contract_rows, preferred_element_type...]
    unnamed x119 -> x94, local copies, waits for them, and re-layouts: 22.1 us -> 18.4 us
  transfers between devices with their start and end apart: 5 -> 5, of which waited for: 1 -> 2; matrix products, arithmetic and copies ran while one was open for 13% -> 10% of each run, Pallas kernels for 59% -> 61%
where the time goes in v5:
time: 693 us; the launch traced here: 689 us
  Pallas kernels  571 us (82%)
  matrix products  37.4 us (5%)
  other arithmetic  36.9 us (5%)
  local copies, waits for them, and re-layouts  22.5 us (3%)
  between operations  14.7 us (2%)
    pallas_call x2, Pallas kernels, send_back(): pl.pallas_call(functools.partial(return_kernel, plans, values is not None...  108 us
    pallas_call x1, Pallas kernels, prologue(): pl.pallas_call(functools.partial(prologue_kernel, weight_plan, planes), o...  106 us
    pallas_call x2, Pallas kernels, multiply_scatter(): pl.pallas_call(functools.partial(scatter_kernel, outward, swap_plan), out...  103 us
    pallas_call x1, Pallas kernels, feed_back(): pl.pallas_call(backward_kernel, out_shape=(jax.ShapeDtypeStruct((groups,...  54.1 us
    pallas_call x1, Pallas kernels, attend_back(): pl.pallas_call(functools.partial(attend_back_kernel, heads, min(256, leng...  50.3 us
    pallas_call x1, Pallas kernels, plane_gather(): pl.pallas_call(gather_kernel, out_shape=(jax.ShapeDtypeStruct((groups, 8,...  48 us
    pallas_call x1, Pallas kernels, gather_and_apply(): pl.pallas_call(apply_kernel, out_shape=(jax.ShapeDtypeStruct((groups, 8,...  44 us
    pallas_call x1, Pallas kernels, gather_and_feed(): pl.pallas_call(forward_kernel, out_shape=(jax.ShapeDtypeStruct((groups, 8...  41.9 us
  transfers between devices with their start and end apart: 5, of which 2 were waited for; matrix products, arithmetic and copies ran while one was open for 10% of the time, Pallas kernels for 61%

profile of v5, /device:TPU:0, one launch (start us, length us, event | category | flops | bytes accessed | tf_op | source)
XLA Modules:
  0.0 689.3 jit_solution(16794085975603989626)
XLA Ops:
  9.9 1.2 copy-done.6
  11.1 106.2 %prologue.1 = (bf16[2,4,32,2048]{3,2,1,0:T(8,128)(2,1)S(1)}, bf16[8,8,32,2048]{3,2,1,0:T(8,128)(2,1)}, f32[8,8,128]{2,1,0:T(8,128)S(1)}, f32[8,8,128]{2,1,0:T(8,...) custom-call(bf16[8,32,2048]{2,1,0:T(8,128)(2,1)S(1)} %bitcast.70, ...), custom_call_target="tpu_custom_call" | custom-call | tf_op jit(solution)/shard_map/prologue/pallas_call | solution.py:1059
  119.8 1.9 fusion.1
  122.1 11.1 %fusion.10.p_ref = f32[2,1024,768]{2,1,0:T(8,128)} fusion(bf16[2,1024,2048]{2,1,0:T(8,128)(2,1)} %bitcast.100, bf16[2048,768,1]{1,0,2:T(8,128)(2,1)S(1)} %bitcast.104), kind=kOutput, calls=%fused_computation.81 | convolution fusion | flops 6442450944 | bytes 17825792 | tf_op jit(solution)/shard_map/dot_general | solution.py:1577
  133.6 16.1 %attend.1 = (bf16[2,1024,256]{2,1,0:T(8,128)(2,1)S(1)}, f32[2,1024,256]{2,1,0:T(8,128)}, bf16[2,1024,256]{2,1,0:T(8,128)(2,1)S(1)}, bf16[2,1024,128]{2,1,0:T(8,128)(2,1)S(1)}, f32[2,2,1024,128]{3,2,1,0:T(8,128)}) custom-call(f32[2,1024,768]{2,1,0:T(8,128)} %fusion.10.p_ref, f32[2,128]{1,0:T(2,128)S(1)} %convert_element_type.90.gain_ref, ...), custom_call_target="tpu_custom_call" | custom-call | flops 2147483648 | bytes 16777216 | tf_op jit(solution)/shard_map/attend/pallas_call | solution.py:1395
  151.9 59.2 %multiply_scatter.2 = (f32[8,32,2048]{2,1,0:T(8,128)S(1)}, bf16[2,4,16,2048]{3,2,1,0:T(8,128)(2,1)S(1)}, bf16[2,256,768]{2,1,0:T(8,128)(2,1)S(1)}) custom-call(bf16[8,8,32,256]{3,2,1,0:T(8,128)(2,1)S(1)} %bitcast.79, bf16[2048,256]{1,0:T(8,128)(2,1)S(1)} %bitcast.71, bf16[8,16,2048]{2,1,0:T(8,128)(2,1)S(1)} %get-tuple-element.109.refs_2_, ...), custom_call_target="tpu_custom_call" | custom-call | flops 2147483648 | bytes 9437184 | tf_op jit(solution)/shard_map/multiply_scatter/pallas_call | solution.py:423
  213.2 1.7 bitcast_multiply_fusion
  214.8 1.4 copy-done.23
  216.5 1.9 multiply_convert_fusion.x_ref
  218.4 48.0 %plane_gather.1 = (bf16[8,8,32,2048]{3,2,1,0:T(8,128)(2,1)}, bf16[2,4,16,2048]{3,2,1,0:T(8,128)(2,1)S(1)}) custom-call(bf16[8,32,2048]{2,1,0:T(8,128)(2,1)S(1)} %multiply_convert_fusion.x_ref, bf16[8,16,2048]{2,1,0:T(8,128)(2,1)S(1)} %copy-done.3), custom_call_target="tpu_custom_call" | custom-call | tf_op jit(solution)/shard_map/plane_gather/pallas_call | solution.py:154
  266.5 41.9 %gather_and_feed.1 = (bf16[8,8,32,2048]{3,2,1,0:T(8,128)(2,1)}, f32[8,8,32,1536]{3,2,1,0:T(8,128)}, bf16[8,8,32,768]{3,2,1,0:T(8,128)(2,1)S(1)}) custom-call(bf16[8,32,2048]{2,1,0:T(8,128)(2,1)S(1)} %bitcast.65, bf16[8,8,32,2048]{3,2,1,0:T(8,128)(2,1)} %get-tuple-element.69.h_ref, bf16[2048,1536]{1,0:T(8,128)(2,1)} %all-gather.3.cloned.1.call-done.w_ref.up_ref), custom_call_target="tpu_custom_call" | custom-call | flops 12884901888 | bytes 14680064 | tf_op jit(solution)/shard_map/gather_and_feed/pallas_call | solution.py:595
  308.4 1.7 copy-done.22
  310.1 10.4 %bitcast_convert_fusion = bf16[2048,768]{1,0:T(8,128)(2,1)} fusion(bf16[8,8,32,2048]{3,2,1,0:T(8,128)(2,1)} %get-tuple-element.73.g_ref, bf16[8,8,32,768]{3,2,1,0:T(8,128)(2,1)S(1)} %get-tuple-element.72.a_ref), kind=kOutput, calls=%fused_computation | convolution fusion | flops 6444023808 | bytes 14680064 | tf_op jit(solution)/shard_map/dot_general | solution.py:1620
  320.6 4.2 all-gather.5.cloned.1.call-done.down_ref.w_ref
  324.7 54.1 %feed_back.1 = (f32[8,32,2048]{2,1,0:T(8,128)}, bf16[2048,1536]{1,0:T(8,128)(2,1)}) custom-call(bf16[8,8,32,2048]{3,2,1,0:T(8,128)(2,1)} %get-tuple-element.73.g_ref, f32[8,8,32,1536]{3,2,1,0:T(8,128)} %get-tuple-element.74.lin_ref, bf16[2048,768]{1,0:T(8,128)(2,1)} %all-gather.5.cloned.1.call-done.down_ref.w_ref, ...), custom_call_target="tpu_custom_call" | custom-call | flops 32212254720 | bytes 35651584 | tf_op jit(solution)/shard_map/feed_back/pallas_call | solution.py:736
  379.1 3.0 multiply_reduce_fusion
  383.8 44.0 %gather_and_apply.1 = (bf16[8,8,32,2048]{3,2,1,0:T(8,128)(2,1)}, f32[8,8,32,256]{3,2,1,0:T(8,128)S(1)}) custom-call(bf16[8,32,2048]{2,1,0:T(8,128)(2,1)S(1)} %fusion.7.x_ref, bf16[2048,256]{1,0:T(8,128)(2,1)S(1)} %bitcast.72), custom_call_target="tpu_custom_call" | custom-call | tf_op jit(solution)/shard_map/gather_and_apply/pallas_call | solution.py:563
  427.8 1.3 copy-done.16
  429.1 5.7 convolution_convert_fusion.1
  434.9 50.3 %attend_back.1 = (bf16[2,1024,768]{2,1,0:T(8,128)(2,1)}, f32[8,128]{1,0:T(8,128)}, f32[8,32,2048]{2,1,0:T(8,128)}) custom-call(f32[2,1024,256]{2,1,0:T(8,128)} %bitcast.78, f32[2,1024,768]{2,1,0:T(8,128)} %fusion.10.p_ref, f32[2,128]{1,0:T(2,128)} %copy-done.15, f32[1024,128]{1,0:T(8,128)} %copy-done.1, f32[1024,128]{1,0:T(8,128)} %copy-done.2, ...), custom_call_target="tpu_custom_call" | custom-call | flops 11811160064 | bytes 33554432 | tf_op jit(solution)/shard_map/attend_back/pallas_call | solution.py:1430
  485.2 10.2 %convolution_convert_fusion = bf16[2048,768]{0,1:T(8,128)(2,1)S(1)} fusion(bf16[2048,2048]{1,0:T(8,128)(2,1)} %bitcast.101, bf16[2048,768]{1,0:T(8,128)(2,1)} %bitcast.81), kind=kOutput, calls=%fused_computation.2 | convolution fusion | flops 6444023808 | bytes 14680064 | tf_op jit(solution)/shard_map/dot_general | solution.py:1647
  495.4 2.3 pad_maximum_fusion
  499.6 1.9 copy-done.21
  501.5 43.4 %multiply_scatter.3 = f32[8,32,2048]{2,1,0:T(8,128)S(1)} custom-call(bf16[8,8,32,768]{3,2,1,0:T(8,128)(2,1)S(1)} %bitcast.82, bf16[2048,768]{1,0:T(8,128)(2,1)} %bitcast.103), custom_call_target="tpu_custom_call" | custom-call | flops 6442450944 | bytes 11534336 | tf_op jit(solution)/shard_map/multiply_scatter/pallas_call | solution.py:423
  547.1 1.3 add_convert_fusion
  549.9 65.6 %send_back.2 = (bf16[8,32,2048]{2,1,0:T(8,128)(2,1)S(1)}, bf16[256,12288]{1,0:T(8,128)(2,1)}, bf16[256,6144]{1,0:T(8,128)(2,1)}) custom-call(bf16[2,4,32,2048]{3,2,1,0:T(8,128)(2,1)S(1)} %bitcast.68, bf16[2,256,1536]{2,1,0:T(8,128)(2,1)S(1)} %bitcast.67, bf16[2,256,768]{2,1,0:T(8,128)(2,1)S(1)} %bitcast.76), custom_call_target="tpu_custom_call" | custom-call | tf_op jit(solution)/shard_map/send_back/pallas_call | solution.py:1194
  615.6 5.5 convert_element_type.111
  621.4 6.4 slice_convert_fusion
  627.8 1.5 copy.22
  629.3 42.6 %send_back.3 = (bf16[8,32,2048]{2,1,0:T(8,128)(2,1)S(1)}, bf16[256,8192]{1,0:T(8,128)(2,1)}, f32[8,128]{1,0:T(8,128)S(1)}) custom-call(bf16[2,4,32,2048]{3,2,1,0:T(8,128)(2,1)S(1)} %bitcast.69, bf16[2,256,1024]{2,1,0:T(8,128)(2,1)S(1)} %bitcast.66, f32[4,2,8,128]{3,2,1,0:T(8,128)S(1)} %maximum_maximum_fusion.refs_2_), custom_call_target="tpu_custom_call" | custom-call | tf_op jit(solution)/shard_map/send_back/pallas_call | solution.py:1194
  671.9 5.3 slice_convert_fusion.2
  677.2 2.8 slice_convert_fusion.3
  (138 shorter events, 20.5 us)
Async XLA Ops:
  7.2 259.3 %all-gather.3.cloned.1.call-start = ((), (), s32[]{:S(2)}) async-start(), calls=%async_computation.3 | async-start | bytes 7864320 | tf_op jit(solution)/shard_map/all_gather | solution.py:1526
  11.1 107.9 %copy-start.32 = (bf16[2,128]{1,0:T(2,128)(2,1)S(1)}, bf16[2,128]{1,0:T(2,128)(2,1)}, u32[]{:S(2)}) copy-start(bf16[2,128]{1,0:T(2,128)(2,1)} %param.20) | copy-start | bytes 1540
  118.3 206.4 %all-gather.5.cloned.1.call-start = ((), (), s32[]{:S(2)}) async-start(), calls=%async_computation.4 | async-start | bytes 3932160 | tf_op jit(solution)/shard_map/all_gather | solution.py:1526
  119.0 14.6 %copy-start.15 = (f32[2,128]{1,0:T(2,128)}, f32[2,128]{1,0:T(2,128)S(1)}, u32[]{:S(2)}) copy-start(f32[2,128]{1,0:T(2,128)S(1)} %convert_element_type.90.gain_ref) | copy-start | bytes 3076
  119.8 2.3 copy-start.31
  122.1 11.5 %copy-start.1 = (f32[1024,128]{1,0:T(8,128)}, f32[1024,128]{1,0:T(8,128)S(1)}, u32[]{:S(2)}) copy-start(f32[1024,128]{1,0:T(8,128)S(1)} %get-tuple-element.118.cos_ref) | copy-start | bytes 1572868
  122.1 11.5 %copy-start.2 = (f32[1024,128]{1,0:T(8,128)}, f32[1024,128]{1,0:T(8,128)S(1)}, u32[]{:S(2)}) copy-start(f32[1024,128]{1,0:T(8,128)S(1)} %get-tuple-element.119.sin_ref) | copy-start | bytes 1572868
  133.5 16.2 %copy-start = (f32[2,1024,128]{2,1,0:T(8,128)}, f32[2,1024,128]{2,1,0:T(8,128)S(1)}, u32[]{:S(2)}) copy-start(f32[2,1024,128]{2,1,0:T(8,128)S(1)} %broadcast_in_dim.9.qcode_ref) | copy-start | bytes 3145732
  133.6 16.2 %copy-start.14 = (f32[2,8,1024]{2,1,0:T(8,128)}, f32[2,8,1024]{2,1,0:T(8,128)S(1)}, u32[]{:S(2)}) copy-start(f32[2,8,1024]{2,1,0:T(8,128)S(1)} %broadcast_in_dim.10.kcode_ref) | copy-start | bytes 196612
  133.6 16.1 %copy-start.30 = (bf16[256,2048]{1,0:T(8,128)(2,1)S(1)}, bf16[256,2048]{1,0:T(8,128)(2,1)}, u32[]{:S(2)}) copy-start(bf16[256,2048]{1,0:T(8,128)(2,1)} %param.15) | copy-start | bytes 3145732
  149.7 2.1 copy-start.18
  150.0 1.9 copy-start.8
  212.8 222.1 %reduce-scatter.4.cloned.1.call-start = ((), (), s32[]{:S(2)}) async-start(), calls=%async_computation.5 | async-start | bytes 3932160 | tf_op jit(solution)/shard_map/reduce_scatter | solution.py:1612
  214.8 1.4 copy-start.23
  216.4 2.0 copy-start.3
  216.5 49.9 %copy-start.13 = (bf16[2,4,16,2048]{3,2,1,0:T(8,128)(2,1)S(1)}, bf16[2,4,16,2048]{3,2,1,0:T(8,128)(2,1)}, u32[]{:S(2)}) copy-start(bf16[2,4,16,2048]{3,2,1,0:T(8,128)(2,1)} %copy-done.12) | copy-start | bytes 1572868
  308.4 1.7 copy-start.22
  320.5 179.0 %reduce-scatter.8.cloned.1.call-start = ((), (), s32[]{:S(2)}) async-start(), calls=%async_computation.7 | async-start | bytes 7864320 | tf_op jit(solution)/shard_map/reduce_scatter | solution.py:1612
  378.8 249.0 %reduce-scatter.6.cloned.1.call-start = ((), (), s32[]{:S(2)}) async-start(), calls=%async_computation.6 | async-start | bytes 5242880 | tf_op jit(solution)/shard_map/reduce_scatter | solution.py:1612
  379.1 3.0 copy-start.24
  379.1 3.5 copy-start.26
  383.8 45.3 %copy-start.19 = (bf16[2,1024,256]{2,1,0:T(8,128)(2,1)S(1)}, bf16[2,1024,256]{2,1,0:T(8,128)(2,1)}, u32[]{:S(2)}) copy-start(bf16[2,1024,256]{2,1,0:T(8,128)(2,1)} %copy-done.18) | copy-start | bytes 3145732
  427.8 1.3 copy-start.16
  499.6 1.9 copy-start.21
  501.5 43.4 %copy-start.28 = (f32[8,32,2048]{2,1,0:T(8,128)S(1)}, f32[8,32,2048]{2,1,0:T(8,128)}, u32[]{:S(2)}) copy-start(f32[8,32,2048]{2,1,0:T(8,128)} %get-tuple-element.106) | copy-start | bytes 6291460
  501.5 44.0 %copy-start.29 = (f32[8,32,2048]{2,1,0:T(8,128)S(1)}, f32[8,32,2048]{2,1,0:T(8,128)}, u32[]{:S(2)}) copy-start(f32[8,32,2048]{2,1,0:T(8,128)} %get-tuple-element.84) | copy-start | bytes 6291460
  544.8 1.6 copy-start.25
  544.9 2.2 copy-start.27
  547.1 1.6 copy-start.11
  548.4 1.5 copy-start.4
  615.5 5.8 slice-start
  615.5 5.8 slice-start.1
  (8 other events, 8.5 us)
Sparse Core Ops, SparseCore 0:
  118.4 143.0 all-gather.2
  263.1 61.6 all-gather.4
  327.6 58.8 reduce-scatter.3
  388.7 110.7 reduce-scatter.7
  502.3 94.0 reduce-scatter.5

commit v6 on v5

--- a/solution.py
+++ b/solution.py
@@ -1023,8 +1023,13 @@
         swap.sent[index].wait_recv()
     for k in range(2):
         out_relay.begin(k)
+    for distance in range(2, min(3, planes)):
+        for k in range(2):
+            relay.hop(distance, k)
+        for k in range(2):
+            out_relay.hop(distance - 1, k)
     gather.middle()
-    for distance in range(2, planes):
+    for distance in range(3, planes):
         for k in range(2):
             relay.hop(distance, k)
         for k in range(2):
@@ -1271,13 +1276,16 @@
 def attend_back_kernel(
     heads, block, held,
     da_ref, p_ref, gain_ref, cos_ref, sin_ref, qcode_ref, kcode_ref,
-    saved_o_ref, q_ref, k_ref, lse_ref, a_ref, w_ref,
-    out_ref, hg_ref, sum_ref, *refs,
+    saved_o_ref, q_ref, k_ref, lse_ref, a_ref, w_ref, normed_ref, grad_ref, mixed_ref,
+    out_ref, hg_ref, sum_ref, part_ref, *refs,
 ):
     scatter = Scatter(*refs[:9])
     a_buf, w_buf, a_sem, w_sem, *refs = refs[9:]
     dq_acc, dk_acc, dv_acc, *refs = refs
     buffers, dp_buf, load_sem, store_sem = refs[:6], refs[6], refs[7], refs[8]
+    tile_buf, part_buf, mixed_buf, tile_sem, part_sem, mixed_sem = refs[9:]
+    mixed_load = pltpu.make_async_copy(mixed_ref, mixed_buf, mixed_sem)
+    mixed_load.start()
     hbm = (p_ref, da_ref, saved_o_ref, q_ref, k_ref, lse_ref)
     w_load = pltpu.make_async_copy(w_ref, w_buf, w_sem)
     w_load.start()
@@ -1366,6 +1374,55 @@
         stores.append(store)
         if s == 0:
             scatter.middle()
+
+    tile = tile_buf.shape[2]
+    count = normed_ref.shape[1] // tile
+
+    def weigh(left_ref, right, base):
+        columns = right.shape[1]
+
+        def tile_load(k, slot):
+            at_k = pl.ds(pl.multiple_of(k * tile, tile), tile)
+            return pltpu.make_async_copy(
+                left_ref.at[:, at_k], tile_buf.at[slot], tile_sem.at[slot]
+            )
+
+        def tile_store(k, slot):
+            at_k = pl.ds(pl.multiple_of(k * tile, tile), tile)
+            return pltpu.make_async_copy(
+                part_buf.at[slot, :, pl.ds(0, columns)],
+                part_ref.at[at_k, pl.ds(base, columns)],
+                part_sem.at[slot],
+            )
+
+        tile_load(0, 0).start()
+
+        def body(k, carry):
+            slot = lax.rem(k, 2)
+            tile_load(k, slot).wait()
+
+            @pl.when(k < count - 1)
+            def _():
+                tile_load(k + 1, 1 - slot).start()
+
+            @pl.when(k > 1)
+            def _():
+                tile_store(k - 2, slot).wait()
+
+            product = lax.dot_general(
+                tile_buf[slot], right[...], contract_rows, preferred_element_type=f32
+            )
+            part_buf[slot, :, :columns] = product.astype(bf16)
+            tile_store(k, slot).start()
+            return carry
+
+        lax.fori_loop(0, count, body, 0)
+        for k in (count - 2, count - 1):
+            tile_store(k, k % 2).wait()
+
+    mixed_load.wait()
+    weigh(normed_ref, dp_buf.reshape(held * length, dp_buf.shape[2]), 0)
+    weigh(grad_ref, mixed_buf, dp_buf.shape[2])
     scatter.finish(sum_ref)
     for store in stores:
         store.wait()
@@ -1416,10 +1473,12 @@
 
 
 def attend_back(
-    da, projected, gain, cosine, sine, query_code, key_code, saved, heads, a, weight
+    da, projected, gain, cosine, sine, query_code, key_code, saved, heads, a, weight, normed, grads
 ):
     held, length, columns = projected.shape
-    _, attended, queries, keys, lse = saved
+    mixed, attended, queries, keys, lse = saved
+    mixed = mixed.reshape(held * length, -1)
+    tile = 256
     groups, _, rows, depth = a.shape
     width = weight.shape[0]
     kind = a.dtype
@@ -1433,9 +1492,10 @@
             jax.ShapeDtypeStruct((held, length, columns), kind),
             jax.ShapeDtypeStruct((8, HEAD_SIZE), jnp.float32),
             jax.ShapeDtypeStruct((groups, rows, width), jnp.float32),
+            jax.ShapeDtypeStruct((width, columns + mixed.shape[1]), kind),
         ),
-        in_specs=[anywhere] * 2 + [vmem] * 5 + [anywhere] * 6,
-        out_specs=(anywhere, vmem, vmem),
+        in_specs=[anywhere] * 2 + [vmem] * 5 + [anywhere] * 9,
+        out_specs=(anywhere, vmem, vmem, anywhere),
         scratch_shapes=scatter_scratch(groups, rows, width, kind)
         + [
             pltpu.VMEM((8, groups, rows, depth), kind),
@@ -1447,7 +1507,17 @@
             pltpu.VMEM((length, HEAD_SIZE), jnp.float32),
         ]
         + [pltpu.VMEM(value.shape, value.dtype) for value in big]
-        + [pltpu.VMEM(projected.shape, kind), dma((held, 6)), dma((held,))],
+        + [
+            pltpu.VMEM(projected.shape, kind),
+            dma((held, 6)),
+            dma((held,)),
+            pltpu.VMEM((2, held * length, tile), kind),
+            pltpu.VMEM((2, tile, columns), kind),
+            pltpu.VMEM(mixed.shape, kind),
+            dma((2,)),
+            dma((2,)),
+            dma,
+        ],
         compiler_params=pltpu.CompilerParams(
             collective_id=7, has_side_effects=True, vmem_limit_bytes=58 * 1024 * 1024
         ),
@@ -1460,7 +1530,7 @@
         name="attend_back",
     )(
         da, projected, gain, cosine, sine, query_code, key_code,
-        attended, queries, keys, lse, a, weight,
+        attended, queries, keys, lse, a, weight, normed, grads, mixed,
     )
 
 
@@ -1629,11 +1699,8 @@
     d_resid = own_grad.astype(f32) + norm_back(d_normed_mlp, unit_mlp, root_mlp, gain_mlp)
     d_attn_low, mixed_grad = gather_and_apply(d_resid.astype(bf16), out_w)
     d_attn_low = d_attn_low.reshape(plane_tokens, model_width)
-    out_part = lax.dot_general(
-        d_attn_low, mixed, contract_rows, preferred_element_type=f32
-    ).astype(bf16)
-    mixed_grad = after(mixed_grad, out_part, down_rows)
-    d_proj, head_term, layer_rows = attend_back(
+    mixed_grad = after(mixed_grad, down_rows)
+    d_proj, head_term, layer_rows, attn_part = attend_back(
         mixed_grad.reshape(held, sequence_length, query_part),
         projected,
         *tables,
@@ -1641,13 +1708,11 @@
         heads,
         parts_of(hidden),
         down_w,
+        normed_attn,
+        d_attn_low,
     )
     d_proj = d_proj.reshape(plane_tokens, -1)
     head_term = head_term[:2]
-    proj_part = lax.dot_general(
-        normed_attn, d_proj, contract_rows, preferred_element_type=f32
-    ).astype(bf16)
-    attn_part = jnp.concatenate([proj_part, out_part], axis=1)
     d_proj = after(d_proj, attn_part, up_rows)
     parted = (held, planes, chunk, model_width)
     layer_own = (resid_mid + layer_rows).astype(bf16)

time: 693 us -> 693 us (level)
  Pallas kernels: 571 us -> 588 us
  matrix products: 37.4 us -> 21.5 us
    pallas_call x1, Pallas kernels: 50.3 us -> 67 us  [attend_back(): pl.pallas_call(functools.partial(attend_back_kernel, heads, min(256, leng...]
    dot_general x2 -> x0, matrix products: 15.9 us -> none  [the longest x1 10.2 us: per_device(): lax.dot_general(normed_attn, d_proj, contract_rows, preferred_element_typ...]
  transfers between devices with their start and end apart: 5 -> 5, of which waited for: 2 -> 2; matrix products, arithmetic and copies ran while one was open for 10% -> 7% of each run, Pallas kernels for 61% -> 64%
where the time goes in v6:
time: 693 us; the launch traced here: 689 us
  Pallas kernels  588 us (85%)
  other arithmetic  34.6 us (5%)
  local copies, waits for them, and re-layouts  22.2 us (3%)
  matrix products  21.5 us (3%)
  between operations  14.8 us (2%)
  waiting for transfers between devices  7.33 us (1%)
    pallas_call x2, Pallas kernels, send_back(): pl.pallas_call(functools.partial(return_kernel, plans, values is not None...  108 us
    pallas_call x1, Pallas kernels, prologue(): pl.pallas_call(functools.partial(prologue_kernel, weight_plan, planes), o...  106 us
    pallas_call x2, Pallas kernels, multiply_scatter(): pl.pallas_call(functools.partial(scatter_kernel, outward, swap_plan), out...  103 us
    pallas_call x1, Pallas kernels, attend_back(): pl.pallas_call(functools.partial(attend_back_kernel, heads, min(256, leng...  67 us
    pallas_call x1, Pallas kernels, feed_back(): pl.pallas_call(backward_kernel, out_shape=(jax.ShapeDtypeStruct((groups,...  54 us
    pallas_call x1, Pallas kernels, plane_gather(): pl.pallas_call(gather_kernel, out_shape=(jax.ShapeDtypeStruct((groups, 8,...  47.9 us
    pallas_call x1, Pallas kernels, gather_and_apply(): pl.pallas_call(apply_kernel, out_shape=(jax.ShapeDtypeStruct((groups, 8,...  44 us
    pallas_call x1, Pallas kernels, gather_and_feed(): pl.pallas_call(forward_kernel, out_shape=(jax.ShapeDtypeStruct((groups, 8...  41.9 us
  transfers between devices with their start and end apart: 5, of which 2 were waited for; matrix products, arithmetic and copies ran while one was open for 7% of the time, Pallas kernels for 64%

profile of v6, /device:TPU:0, one launch (start us, length us, event | category | flops | bytes accessed | tf_op | source)
XLA Modules:
  0.0 689.2 jit_solution(13376635876281469032)
XLA Ops:
  8.6 1.2 copy-done.5
  9.9 1.2 copy-done.6
  11.1 106.2 %prologue.1 = (bf16[2,4,32,2048]{3,2,1,0:T(8,128)(2,1)S(1)}, bf16[8,8,32,2048]{3,2,1,0:T(8,128)(2,1)}, f32[8,8,128]{2,1,0:T(8,128)S(1)}, f32[8,8,128]{2,1,0:T(8,...) custom-call(bf16[8,32,2048]{2,1,0:T(8,128)(2,1)S(1)} %bitcast.65, ...), custom_call_target="tpu_custom_call" | custom-call | tf_op jit(solution)/shard_map/prologue/pallas_call | solution.py:1064
  119.5 1.9 fusion.1
  121.7 11.1 %fusion.10.p_ref = f32[2,1024,768]{2,1,0:T(8,128)} fusion(bf16[2,1024,2048]{2,1,0:T(8,128)(2,1)} %bitcast.95, bf16[2048,768,1]{1,0,2:T(8,128)(2,1)S(1)} %bitcast.99), kind=kOutput, calls=%fused_computation.78 | convolution fusion | flops 6442450944 | bytes 17825792 | tf_op jit(solution)/shard_map/dot_general | solution.py:1647
  133.3 16.1 %attend.1 = (bf16[2,1024,256]{2,1,0:T(8,128)(2,1)S(1)}, f32[2,1024,256]{2,1,0:T(8,128)}, bf16[2,1024,256]{2,1,0:T(8,128)(2,1)S(1)}, bf16[2,1024,128]{2,1,0:T(8,128)(2,1)S(1)}, f32[2,2,1024,128]{3,2,1,0:T(8,128)}) custom-call(f32[2,1024,768]{2,1,0:T(8,128)} %fusion.10.p_ref, f32[2,128]{1,0:T(2,128)S(1)} %convert_element_type.84.gain_ref, ...), custom_call_target="tpu_custom_call" | custom-call | flops 2147483648 | bytes 16777216 | tf_op jit(solution)/shard_map/attend/pallas_call | solution.py:1452
  151.6 59.2 %multiply_scatter.2 = (f32[8,32,2048]{2,1,0:T(8,128)S(1)}, bf16[2,4,16,2048]{3,2,1,0:T(8,128)(2,1)S(1)}, bf16[2,256,768]{2,1,0:T(8,128)(2,1)S(1)}) custom-call(bf16[8,8,32,256]{3,2,1,0:T(8,128)(2,1)S(1)} %bitcast.75, bf16[2048,256]{1,0:T(8,128)(2,1)S(1)} %bitcast.66, bf16[8,16,2048]{2,1,0:T(8,128)(2,1)S(1)} %get-tuple-element.111.refs_2_, ...), custom_call_target="tpu_custom_call" | custom-call | flops 2147483648 | bytes 9437184 | tf_op jit(solution)/shard_map/multiply_scatter/pallas_call | solution.py:423
  212.8 1.7 bitcast_multiply_fusion
  214.5 1.4 copy-done.23
  216.2 1.9 multiply_convert_fusion.x_ref
  218.1 47.9 %plane_gather.1 = (bf16[8,8,32,2048]{3,2,1,0:T(8,128)(2,1)}, bf16[2,4,16,2048]{3,2,1,0:T(8,128)(2,1)S(1)}) custom-call(bf16[8,32,2048]{2,1,0:T(8,128)(2,1)S(1)} %multiply_convert_fusion.x_ref, bf16[8,16,2048]{2,1,0:T(8,128)(2,1)S(1)} %copy-done.3), custom_call_target="tpu_custom_call" | custom-call | tf_op jit(solution)/shard_map/plane_gather/pallas_call | solution.py:154
  266.2 41.9 %gather_and_feed.1 = (bf16[8,8,32,2048]{3,2,1,0:T(8,128)(2,1)}, f32[8,8,32,1536]{3,2,1,0:T(8,128)}, bf16[8,8,32,768]{3,2,1,0:T(8,128)(2,1)S(1)}) custom-call(bf16[8,32,2048]{2,1,0:T(8,128)(2,1)S(1)} %bitcast.61, bf16[8,8,32,2048]{3,2,1,0:T(8,128)(2,1)} %get-tuple-element.70.h_ref, bf16[2048,1536]{1,0:T(8,128)(2,1)} %all-gather.3.cloned.1.call-done.w_ref.up_ref), custom_call_target="tpu_custom_call" | custom-call | flops 12884901888 | bytes 14680064 | tf_op jit(solution)/shard_map/gather_and_feed/pallas_call | solution.py:595
  308.1 1.7 copy-done.22
  309.7 10.4 %bitcast_convert_fusion = bf16[2048,768]{1,0:T(8,128)(2,1)} fusion(bf16[8,8,32,2048]{3,2,1,0:T(8,128)(2,1)} %get-tuple-element.74.g_ref, bf16[8,8,32,768]{3,2,1,0:T(8,128)(2,1)S(1)} %get-tuple-element.73.a_ref), kind=kOutput, calls=%fused_computation | convolution fusion | flops 6444023808 | bytes 14680064 | tf_op jit(solution)/shard_map/dot_general | solution.py:1690
  320.2 4.6 all-gather.5.cloned.1.call-done.down_ref.w_ref
  324.7 54.0 %feed_back.1 = (f32[8,32,2048]{2,1,0:T(8,128)}, bf16[2048,1536]{1,0:T(8,128)(2,1)}) custom-call(bf16[8,8,32,2048]{3,2,1,0:T(8,128)(2,1)} %get-tuple-element.74.g_ref, f32[8,8,32,1536]{3,2,1,0:T(8,128)} %get-tuple-element.75.lin_ref, bf16[2048,768]{1,0:T(8,128)(2,1)} %all-gather.5.cloned.1.call-done.down_ref.w_ref, ...), custom_call_target="tpu_custom_call" | custom-call | flops 32212254720 | bytes 35651584 | tf_op jit(solution)/shard_map/feed_back/pallas_call | solution.py:736
  379.0 3.0 multiply_reduce_fusion
  383.7 44.0 %gather_and_apply.1 = (bf16[8,8,32,2048]{3,2,1,0:T(8,128)(2,1)}, f32[8,8,32,256]{3,2,1,0:T(8,128)S(1)}) custom-call(bf16[8,32,2048]{2,1,0:T(8,128)(2,1)S(1)} %fusion.7.x_ref, bf16[2048,256]{1,0:T(8,128)(2,1)S(1)} %bitcast.67), custom_call_target="tpu_custom_call" | custom-call | tf_op jit(solution)/shard_map/gather_and_apply/pallas_call | solution.py:563
  427.8 1.4 copy-done.17
  429.1 67.0 %attend_back.1 = (bf16[2,1024,768]{2,1,0:T(8,128)(2,1)}, f32[8,128]{1,0:T(8,128)}, f32[8,32,2048]{2,1,0:T(8,128)}, bf16[2048,1024]{1,0:T(8,128)(2,1)}) custom-call(f32[2,1024,256]{2,1,0:T(8,128)} %bitcast.74, f32[2,1024,768]{2,1,0:T(8,128)} %fusion.10.p_ref, f32[2,128]{1,0:T(2,128)} %copy-done.16, f32[1024,128]{1,0:T(8,128)} %copy-done.1, ...), custom_call_target="tpu_custom_call" | custom-call | flops 11811160064 | bytes 33554432 | tf_op jit(solution)/shard_map/attend_back/pallas_call | solution.py:1489
  496.9 2.7 reduce-scatter.8.cloned.1.call-done
  499.5 1.9 copy-done.21
  501.4 43.6 %multiply_scatter.3 = f32[8,32,2048]{2,1,0:T(8,128)S(1)} custom-call(bf16[8,8,32,768]{3,2,1,0:T(8,128)(2,1)S(1)} %bitcast.77, bf16[2048,768]{1,0:T(8,128)(2,1)} %bitcast.98), custom_call_target="tpu_custom_call" | custom-call | flops 6442450944 | bytes 11534336 | tf_op jit(solution)/shard_map/multiply_scatter/pallas_call | solution.py:423
  547.3 1.3 add_convert_fusion
  548.9 1.2 copy-done.4
  550.1 65.7 %send_back.2 = (bf16[8,32,2048]{2,1,0:T(8,128)(2,1)S(1)}, bf16[256,12288]{1,0:T(8,128)(2,1)}, bf16[256,6144]{1,0:T(8,128)(2,1)}) custom-call(bf16[2,4,32,2048]{3,2,1,0:T(8,128)(2,1)S(1)} %bitcast.63, bf16[2,256,1536]{2,1,0:T(8,128)(2,1)S(1)} %bitcast.62, bf16[2,256,768]{2,1,0:T(8,128)(2,1)S(1)} %bitcast.72), custom_call_target="tpu_custom_call" | custom-call | tf_op jit(solution)/shard_map/send_back/pallas_call | solution.py:1199
  615.8 5.5 convert_element_type.103
  621.6 6.4 slice_convert_fusion
  628.0 1.2 copy-done.10
  629.2 42.5 %send_back.3 = (bf16[8,32,2048]{2,1,0:T(8,128)(2,1)S(1)}, bf16[256,8192]{1,0:T(8,128)(2,1)}, f32[8,128]{1,0:T(8,128)S(1)}) custom-call(bf16[2,4,32,2048]{3,2,1,0:T(8,128)(2,1)S(1)} %bitcast.64, bf16[2,256,1024]{2,1,0:T(8,128)(2,1)S(1)} %bitcast.68, f32[4,2,8,128]{3,2,1,0:T(8,128)S(1)} %maximum_maximum_fusion.refs_2_), custom_call_target="tpu_custom_call" | custom-call | tf_op jit(solution)/shard_map/send_back/pallas_call | solution.py:1199
  671.8 5.3 slice_convert_fusion.2
  677.1 2.8 slice_convert_fusion.3
  (134 shorter events, 16.6 us)
Async XLA Ops:
  7.2 259.0 %all-gather.3.cloned.1.call-start = ((), (), s32[]{:S(2)}) async-start(), calls=%async_computation.3 | async-start | bytes 7864320 | tf_op jit(solution)/shard_map/all_gather | solution.py:1596
  11.1 107.6 %copy-start.32 = (bf16[2,128]{1,0:T(2,128)(2,1)S(1)}, bf16[2,128]{1,0:T(2,128)(2,1)}, u32[]{:S(2)}) copy-start(bf16[2,128]{1,0:T(2,128)(2,1)} %param.20) | copy-start | bytes 1540
  118.3 206.4 %all-gather.5.cloned.1.call-start = ((), (), s32[]{:S(2)}) async-start(), calls=%async_computation.4 | async-start | bytes 3932160 | tf_op jit(solution)/shard_map/all_gather | solution.py:1596
  118.7 14.6 %copy-start.16 = (f32[2,128]{1,0:T(2,128)}, f32[2,128]{1,0:T(2,128)S(1)}, u32[]{:S(2)}) copy-start(f32[2,128]{1,0:T(2,128)S(1)} %convert_element_type.84.gain_ref) | copy-start | bytes 3076
  119.5 2.3 copy-start.31
  121.7 11.5 %copy-start.1 = (f32[1024,128]{1,0:T(8,128)}, f32[1024,128]{1,0:T(8,128)S(1)}, u32[]{:S(2)}) copy-start(f32[1024,128]{1,0:T(8,128)S(1)} %get-tuple-element.120.cos_ref) | copy-start | bytes 1572868
  121.7 11.5 %copy-start.2 = (f32[1024,128]{1,0:T(8,128)}, f32[1024,128]{1,0:T(8,128)S(1)}, u32[]{:S(2)}) copy-start(f32[1024,128]{1,0:T(8,128)S(1)} %get-tuple-element.121.sin_ref) | copy-start | bytes 1572868
  133.2 16.2 %copy-start = (f32[2,1024,128]{2,1,0:T(8,128)}, f32[2,1024,128]{2,1,0:T(8,128)S(1)}, u32[]{:S(2)}) copy-start(f32[2,1024,128]{2,1,0:T(8,128)S(1)} %broadcast_in_dim.9.qcode_ref) | copy-start | bytes 3145732
  133.2 16.2 %copy-start.15 = (f32[2,8,1024]{2,1,0:T(8,128)}, f32[2,8,1024]{2,1,0:T(8,128)S(1)}, u32[]{:S(2)}) copy-start(f32[2,8,1024]{2,1,0:T(8,128)S(1)} %broadcast_in_dim.10.kcode_ref) | copy-start | bytes 196612
  133.2 16.1 %copy-start.30 = (bf16[256,2048]{1,0:T(8,128)(2,1)S(1)}, bf16[256,2048]{1,0:T(8,128)(2,1)}, u32[]{:S(2)}) copy-start(bf16[256,2048]{1,0:T(8,128)(2,1)} %param.15) | copy-start | bytes 3145732
  149.4 2.1 copy-start.18
  149.6 1.9 copy-start.8
  212.5 216.7 %reduce-scatter.4.cloned.1.call-start = ((), (), s32[]{:S(2)}) async-start(), calls=%async_computation.5 | async-start | bytes 3932160 | tf_op jit(solution)/shard_map/reduce_scatter | solution.py:1682
  214.5 1.4 copy-start.23
  216.1 2.0 copy-start.3
  216.2 49.9 %copy-start.14 = (bf16[2,4,16,2048]{3,2,1,0:T(8,128)(2,1)S(1)}, bf16[2,4,16,2048]{3,2,1,0:T(8,128)(2,1)}, u32[]{:S(2)}) copy-start(bf16[2,4,16,2048]{3,2,1,0:T(8,128)(2,1)} %copy-done.13) | copy-start | bytes 1572868
  308.1 1.7 copy-start.22
  320.1 179.4 %reduce-scatter.8.cloned.1.call-start = ((), (), s32[]{:S(2)}) async-start(), calls=%async_computation.7 | async-start | bytes 7864320 | tf_op jit(solution)/shard_map/reduce_scatter | solution.py:1682
  378.8 249.3 %reduce-scatter.6.cloned.1.call-start = ((), (), s32[]{:S(2)}) async-start(), calls=%async_computation.6 | async-start | bytes 5242880 | tf_op jit(solution)/shard_map/reduce_scatter | solution.py:1682
  379.0 3.0 copy-start.24
  379.0 3.5 copy-start.26
  427.7 1.4 copy-start.17
  499.5 1.9 copy-start.21
  501.4 43.7 %copy-start.28 = (f32[8,32,2048]{2,1,0:T(8,128)S(1)}, f32[8,32,2048]{2,1,0:T(8,128)}, u32[]{:S(2)}) copy-start(f32[8,32,2048]{2,1,0:T(8,128)} %get-tuple-element.108) | copy-start | bytes 6291460
  501.4 44.3 %copy-start.29 = (f32[8,32,2048]{2,1,0:T(8,128)S(1)}, f32[8,32,2048]{2,1,0:T(8,128)}, u32[]{:S(2)}) copy-start(f32[8,32,2048]{2,1,0:T(8,128)} %get-tuple-element.85) | copy-start | bytes 6291460
  545.1 1.6 copy-start.25
  545.1 2.2 copy-start.27
  547.3 1.6 copy-start.12
  548.7 1.4 copy-start.4
  615.8 5.8 slice-start
  615.8 5.8 slice-start.1
  628.0 1.2 copy-start.10
  (8 other events, 8.5 us)
Sparse Core Ops, SparseCore 0:
  118.4 143.0 all-gather.2
  263.1 61.6 all-gather.4
  327.6 58.8 reduce-scatter.3
  388.7 110.7 reduce-scatter.7
  501.7 93.7 reduce-scatter.5

commit v7 on v6

--- a/solution.py
+++ b/solution.py
@@ -1274,16 +1274,17 @@
 
 
 def attend_back_kernel(
-    heads, block, held,
+    heads, block, held, plan,
     da_ref, p_ref, gain_ref, cos_ref, sin_ref, qcode_ref, kcode_ref,
     saved_o_ref, q_ref, k_ref, lse_ref, a_ref, w_ref, normed_ref, grad_ref, mixed_ref,
-    out_ref, hg_ref, sum_ref, part_ref, *refs,
+    r_ref, out_ref, hg_ref, sum_ref, part_ref, g_ref, *refs,
 ):
     scatter = Scatter(*refs[:9])
     a_buf, w_buf, a_sem, w_sem, *refs = refs[9:]
     dq_acc, dk_acc, dv_acc, *refs = refs
     buffers, dp_buf, load_sem, store_sem = refs[:6], refs[6], refs[7], refs[8]
-    tile_buf, part_buf, mixed_buf, tile_sem, part_sem, mixed_sem = refs[9:]
+    tile_buf, part_buf, mixed_buf, tile_sem, part_sem, mixed_sem = refs[9:15]
+    rows = Rows(plan, r_ref, g_ref, *refs[15:])
     mixed_load = pltpu.make_async_copy(mixed_ref, mixed_buf, mixed_sem)
     mixed_load.start()
     hbm = (p_ref, da_ref, saved_o_ref, q_ref, k_ref, lse_ref)
@@ -1374,6 +1375,7 @@
         stores.append(store)
         if s == 0:
             scatter.middle()
+            rows.start()
 
     tile = tile_buf.shape[2]
     count = normed_ref.shape[1] // tile
@@ -1422,7 +1424,9 @@
 
     mixed_load.wait()
     weigh(normed_ref, dp_buf.reshape(held * length, dp_buf.shape[2]), 0)
+    rows.middle()
     weigh(grad_ref, mixed_buf, dp_buf.shape[2])
+    rows.finish()
     scatter.finish(sum_ref)
     for store in stores:
         store.wait()
@@ -1473,7 +1477,8 @@
 
 
 def attend_back(
-    da, projected, gain, cosine, sine, query_code, key_code, saved, heads, a, weight, normed, grads
+    da, projected, gain, cosine, sine, query_code, key_code, saved, heads, a, weight, normed, grads,
+    parts, plan,
 ):
     held, length, columns = projected.shape
     mixed, attended, queries, keys, lse = saved
@@ -1487,15 +1492,16 @@
     anywhere = pl.BlockSpec(memory_space=pl.ANY)
     big = (projected, da, attended, queries, keys, lse)
     return pl.pallas_call(
-        functools.partial(attend_back_kernel, heads, min(256, length), held),
+        functools.partial(attend_back_kernel, heads, min(256, length), held, plan),
         out_shape=(
             jax.ShapeDtypeStruct((held, length, columns), kind),
             jax.ShapeDtypeStruct((8, HEAD_SIZE), jnp.float32),
             jax.ShapeDtypeStruct((groups, rows, width), jnp.float32),
             jax.ShapeDtypeStruct((width, columns + mixed.shape[1]), kind),
+            jax.ShapeDtypeStruct((parts.shape[1], 8 * plan[0][1]), parts.dtype),
         ),
-        in_specs=[anywhere] * 2 + [vmem] * 5 + [anywhere] * 9,
-        out_specs=(anywhere, vmem, vmem, anywhere),
+        in_specs=[anywhere] * 2 + [vmem] * 5 + [anywhere] * 10,
+        out_specs=(anywhere, vmem, vmem, anywhere, anywhere),
         scratch_shapes=scatter_scratch(groups, rows, width, kind)
         + [
             pltpu.VMEM((8, groups, rows, depth), kind),
@@ -1517,6 +1523,9 @@
             dma((2,)),
             dma((2,)),
             dma,
+            dma((len(plan),)),
+            dma((7 * len(plan),)),
+            dma((7 * len(plan),)),
         ],
         compiler_params=pltpu.CompilerParams(
             collective_id=7, has_side_effects=True, vmem_limit_bytes=58 * 1024 * 1024
@@ -1530,7 +1539,7 @@
         name="attend_back",
     )(
         da, projected, gain, cosine, sine, query_code, key_code,
-        attended, queries, keys, lse, a, weight, normed, grads, mixed,
+        attended, queries, keys, lse, a, weight, normed, grads, mixed, parts,
     )
 
 
@@ -1700,7 +1709,7 @@
     d_attn_low, mixed_grad = gather_and_apply(d_resid.astype(bf16), out_w)
     d_attn_low = d_attn_low.reshape(plane_tokens, model_width)
     mixed_grad = after(mixed_grad, down_rows)
-    d_proj, head_term, layer_rows, attn_part = attend_back(
+    d_proj, head_term, layer_rows, attn_part, down_grad = attend_back(
         mixed_grad.reshape(held, sequence_length, query_part),
         projected,
         *tables,
@@ -1710,6 +1719,8 @@
         down_w,
         normed_attn,
         d_attn_low,
+        down_rows,
+        ((0, ff_part, 0),),
     )
     d_proj = d_proj.reshape(plane_tokens, -1)
     head_term = head_term[:2]
@@ -1742,13 +1753,8 @@
     )
     ff_width = plane_size * ff_part
     up_segments = ((0, ff_part, 0), (ff_part, ff_part, ff_width))
-    tokens_grad, up_grad, down_grad = send_back(
-        to_outer(tokens_grad).reshape(parted),
-        (up_rows, down_rows),
-        (up_segments, ((0, ff_part, 0),)),
-        (2 * ff_width, ff_width),
-        None,
-        3,
+    tokens_grad, up_grad = send_back(
+        to_outer(tokens_grad).reshape(parted), (up_rows,), (up_segments,), (2 * ff_width,), None, 3
     )
     attn_rows = after(attn_rows, tokens_grad)
     proj_width = 2 * (query_total + key_total)

time: 693 us -> 685 us (0.988)
  Pallas kernels: 588 us -> 578 us
  other arithmetic: 34.6 us -> 42.8 us
    pallas_call x2, Pallas kernels: 108 us -> 92.7 us  [send_back(): pl.pallas_call(functools.partial(return_kernel, plans, values is not None...]
    unnamed x94 -> x82, local copies, waits for them, and re-layouts: 19.6 us -> 17.8 us
  transfers between devices with their start and end apart: 5 -> 5, of which waited for: 2 -> 1; matrix products, arithmetic and copies ran while one was open for 7% -> 8% of each run, Pallas kernels for 64% -> 63%
where the time goes in v7:
time: 685 us; the launch traced here: 682 us
  Pallas kernels  578 us (84%)
  other arithmetic  42.8 us (6%)
  matrix products  21.5 us (3%)
  local copies, waits for them, and re-layouts  20.4 us (3%)
  between operations  14.7 us (2%)
    pallas_call x1, Pallas kernels, prologue(): pl.pallas_call(functools.partial(prologue_kernel, weight_plan, planes), o...  106 us
    pallas_call x2, Pallas kernels, multiply_scatter(): pl.pallas_call(functools.partial(scatter_kernel, outward, swap_plan), out...  103 us
    pallas_call x2, Pallas kernels, send_back(): pl.pallas_call(functools.partial(return_kernel, plans, values is not None...  92.7 us
    pallas_call x1, Pallas kernels, attend_back(): pl.pallas_call(functools.partial(attend_back_kernel, heads, min(256, leng...  72 us
    pallas_call x1, Pallas kernels, feed_back(): pl.pallas_call(backward_kernel, out_shape=(jax.ShapeDtypeStruct((groups,...  54 us
    pallas_call x1, Pallas kernels, plane_gather(): pl.pallas_call(gather_kernel, out_shape=(jax.ShapeDtypeStruct((groups, 8,...  47.9 us
    pallas_call x1, Pallas kernels, gather_and_apply(): pl.pallas_call(apply_kernel, out_shape=(jax.ShapeDtypeStruct((groups, 8,...  44.1 us
    pallas_call x1, Pallas kernels, gather_and_feed(): pl.pallas_call(forward_kernel, out_shape=(jax.ShapeDtypeStruct((groups, 8...  41.9 us
  transfers between devices with their start and end apart: 5, of which 1 were waited for; matrix products, arithmetic and copies ran while one was open for 8% of the time, Pallas kernels for 63%

profile of v7, /device:TPU:0, one launch (start us, length us, event | category | flops | bytes accessed | tf_op | source)
XLA Modules:
  0.0 681.5 jit_solution(17870067788065398061)
XLA Ops:
  8.6 1.2 copy-done.5
  9.9 1.2 copy-done.6
  11.1 106.2 %prologue.1 = (bf16[2,4,32,2048]{3,2,1,0:T(8,128)(2,1)S(1)}, bf16[8,8,32,2048]{3,2,1,0:T(8,128)(2,1)}, f32[8,8,128]{2,1,0:T(8,128)S(1)}, f32[8,8,128]{2,1,0:T(8,...) custom-call(bf16[8,32,2048]{2,1,0:T(8,128)(2,1)S(1)} %bitcast.65, ...), custom_call_target="tpu_custom_call" | custom-call | tf_op jit(solution)/shard_map/prologue/pallas_call | solution.py:1064
  119.5 1.9 fusion.1
  121.7 11.1 %fusion.10.p_ref = f32[2,1024,768]{2,1,0:T(8,128)} fusion(bf16[2,1024,2048]{2,1,0:T(8,128)(2,1)} %bitcast.92, bf16[2048,768,1]{1,0,2:T(8,128)(2,1)S(1)} %bitcast.96), kind=kOutput, calls=%fused_computation.78 | convolution fusion | flops 6442450944 | bytes 17825792 | tf_op jit(solution)/shard_map/dot_general | solution.py:1656
  133.2 16.1 %attend.1 = (bf16[2,1024,256]{2,1,0:T(8,128)(2,1)S(1)}, f32[2,1024,256]{2,1,0:T(8,128)}, bf16[2,1024,256]{2,1,0:T(8,128)(2,1)S(1)}, bf16[2,1024,128]{2,1,0:T(8,128)(2,1)S(1)}, f32[2,2,1024,128]{3,2,1,0:T(8,128)}) custom-call(f32[2,1024,768]{2,1,0:T(8,128)} %fusion.10.p_ref, f32[2,128]{1,0:T(2,128)S(1)} %convert_element_type.84.gain_ref, ...), custom_call_target="tpu_custom_call" | custom-call | flops 2147483648 | bytes 16777216 | tf_op jit(solution)/shard_map/attend/pallas_call | solution.py:1456
  151.6 59.2 %multiply_scatter.2 = (f32[8,32,2048]{2,1,0:T(8,128)S(1)}, bf16[2,4,16,2048]{3,2,1,0:T(8,128)(2,1)S(1)}, bf16[2,256,768]{2,1,0:T(8,128)(2,1)S(1)}) custom-call(bf16[8,8,32,256]{3,2,1,0:T(8,128)(2,1)S(1)} %bitcast.74, bf16[2048,256]{1,0:T(8,128)(2,1)S(1)} %bitcast.66, bf16[8,16,2048]{2,1,0:T(8,128)(2,1)S(1)} %get-tuple-element.111.refs_2_, ...), custom_call_target="tpu_custom_call" | custom-call | flops 2147483648 | bytes 9437184 | tf_op jit(solution)/shard_map/multiply_scatter/pallas_call | solution.py:423
  212.8 2.4 bitcast_multiply_fusion
  215.2 1.8 multiply_reduce_fusion.4
  217.1 1.9 multiply_convert_fusion.x_ref
  219.0 47.9 %plane_gather.1 = (bf16[8,8,32,2048]{3,2,1,0:T(8,128)(2,1)}, bf16[2,4,16,2048]{3,2,1,0:T(8,128)(2,1)S(1)}) custom-call(bf16[8,32,2048]{2,1,0:T(8,128)(2,1)S(1)} %multiply_convert_fusion.x_ref, bf16[8,16,2048]{2,1,0:T(8,128)(2,1)S(1)} %copy-done.3), custom_call_target="tpu_custom_call" | custom-call | tf_op jit(solution)/shard_map/plane_gather/pallas_call | solution.py:154
  267.0 41.9 %gather_and_feed.1 = (bf16[8,8,32,2048]{3,2,1,0:T(8,128)(2,1)}, f32[8,8,32,1536]{3,2,1,0:T(8,128)}, bf16[8,8,32,768]{3,2,1,0:T(8,128)(2,1)S(1)}) custom-call(bf16[8,32,2048]{2,1,0:T(8,128)(2,1)S(1)} %bitcast.61, bf16[8,8,32,2048]{3,2,1,0:T(8,128)(2,1)} %get-tuple-element.70.h_ref, bf16[2048,1536]{1,0:T(8,128)(2,1)} %all-gather.3.cloned.1.call-done.w_ref.up_ref), custom_call_target="tpu_custom_call" | custom-call | flops 12884901888 | bytes 14680064 | tf_op jit(solution)/shard_map/gather_and_feed/pallas_call | solution.py:595
  309.0 1.7 copy-done.21
  310.6 10.4 %bitcast_convert_fusion = bf16[2048,768]{1,0:T(8,128)(2,1)} fusion(bf16[8,8,32,2048]{3,2,1,0:T(8,128)(2,1)} %get-tuple-element.74.g_ref, bf16[8,8,32,768]{3,2,1,0:T(8,128)(2,1)S(1)} %get-tuple-element.73.a_ref), kind=kOutput, calls=%fused_computation | convolution fusion | flops 6444023808 | bytes 14680064 | tf_op jit(solution)/shard_map/dot_general | solution.py:1699
  321.1 3.6 all-gather.5.cloned.1.call-done.down_ref.w_ref
  324.7 54.0 %feed_back.1 = (f32[8,32,2048]{2,1,0:T(8,128)}, bf16[2048,1536]{1,0:T(8,128)(2,1)}) custom-call(bf16[8,8,32,2048]{3,2,1,0:T(8,128)(2,1)} %get-tuple-element.74.g_ref, f32[8,8,32,1536]{3,2,1,0:T(8,128)} %get-tuple-element.75.lin_ref, bf16[2048,768]{1,0:T(8,128)(2,1)} %all-gather.5.cloned.1.call-done.down_ref.w_ref, ...), custom_call_target="tpu_custom_call" | custom-call | flops 32212254720 | bytes 35651584 | tf_op jit(solution)/shard_map/feed_back/pallas_call | solution.py:736
  379.0 3.0 multiply_reduce_fusion
  382.0 2.3 fusion.7.x_ref
  384.3 44.1 %gather_and_apply.1 = (bf16[8,8,32,2048]{3,2,1,0:T(8,128)(2,1)}, f32[8,8,32,256]{3,2,1,0:T(8,128)S(1)}) custom-call(bf16[8,32,2048]{2,1,0:T(8,128)(2,1)S(1)} %fusion.7.x_ref, bf16[2048,256]{1,0:T(8,128)(2,1)S(1)} %bitcast.67), custom_call_target="tpu_custom_call" | custom-call | tf_op jit(solution)/shard_map/gather_and_apply/pallas_call | solution.py:563
  428.4 1.4 copy-done.16
  429.8 72.0 %attend_back.1 = (bf16[2,1024,768]{2,1,0:T(8,128)(2,1)}, f32[8,128]{1,0:T(8,128)}, f32[8,32,2048]{2,1,0:T(8,128)}, bf16[2048,1024]{1,0:T(8,128)(2,1)}, bf16[256,6144]{1,0:T(8,128)(2,1)}) custom-call(f32[2,1024,256]{2,1,0:T(8,128)} %bitcast.73, f32[2,1024,768]{2,1,0:T(8,128)} %fusion.10.p_ref, f32[2,128]{1,0:T(2,128)} %copy-done.15, f32[1024,128]{1,0:T(8,128)} %copy-done.1, ...), custom_call_target="tpu_custom_call" | custom-call | flops 11811160064 | bytes 33554432 | tf_op jit(solution)/shard_map/attend_back/pallas_call | solution.py:1494
  502.5 5.3 convert_element_type.103
  507.8 2.3 copy-done.20
  510.2 43.7 %multiply_scatter.3 = f32[8,32,2048]{2,1,0:T(8,128)S(1)} custom-call(bf16[8,8,32,768]{3,2,1,0:T(8,128)(2,1)S(1)} %bitcast.76, bf16[2048,768]{1,0:T(8,128)(2,1)} %bitcast.95), custom_call_target="tpu_custom_call" | custom-call | flops 6442450944 | bytes 11534336 | tf_op jit(solution)/shard_map/multiply_scatter/pallas_call | solution.py:423
  556.2 2.9 add_convert_fusion
  559.4 1.2 copy-done.4
  560.5 47.5 %send_back.2 = (bf16[8,32,2048]{2,1,0:T(8,128)(2,1)S(1)}, bf16[256,12288]{1,0:T(8,128)(2,1)}) custom-call(bf16[2,4,32,2048]{3,2,1,0:T(8,128)(2,1)S(1)} %bitcast.63, bf16[2,256,1536]{2,1,0:T(8,128)(2,1)S(1)} %bitcast.62), custom_call_target="tpu_custom_call" | custom-call | tf_op jit(solution)/shard_map/send_back/pallas_call | solution.py:1199
  608.4 9.3 %slice_convert_fusion = (f32[256,6144]{1,0:T(8,128)}, f32[256,6144]{1,0:T(8,128)}) fusion(bf16[256,12288]{1,0:T(8,128)(2,1)} %get-tuple-element.96), kind=kLoop, calls=%fused_computation.1 | loop fusion | flops 3145728 | bytes 18874368 | tf_op jit(solution)/shard_map/convert_element_type | solution.py:1785
  617.6 1.2 copy-done.10
  618.9 45.2 %send_back.3 = (bf16[8,32,2048]{2,1,0:T(8,128)(2,1)S(1)}, bf16[256,8192]{1,0:T(8,128)(2,1)}, f32[8,128]{1,0:T(8,128)S(1)}) custom-call(bf16[2,4,32,2048]{3,2,1,0:T(8,128)(2,1)S(1)} %bitcast.64, bf16[2,256,1024]{2,1,0:T(8,128)(2,1)S(1)} %bitcast.68, f32[4,2,8,128]{3,2,1,0:T(8,128)S(1)} %maximum_maximum_fusion.refs_2_), custom_call_target="tpu_custom_call" | custom-call | tf_op jit(solution)/shard_map/send_back/pallas_call | solution.py:1199
  664.1 5.3 slice_convert_fusion.2
  669.4 2.8 slice_convert_fusion.3
  (121 shorter events, 14.7 us)
Async XLA Ops:
  7.2 259.8 %all-gather.3.cloned.1.call-start = ((), (), s32[]{:S(2)}) async-start(), calls=%async_computation.3 | async-start | bytes 7864320 | tf_op jit(solution)/shard_map/all_gather | solution.py:1605
  8.6 1.2 copy-start.5
  9.9 1.2 copy-start.6
  11.1 107.6 %copy-start.28 = (bf16[2,128]{1,0:T(2,128)(2,1)S(1)}, bf16[2,128]{1,0:T(2,128)(2,1)}, u32[]{:S(2)}) copy-start(bf16[2,128]{1,0:T(2,128)(2,1)} %param.20) | copy-start | bytes 1540
  117.3 1.0 copy-start.7
  118.3 206.4 %all-gather.5.cloned.1.call-start = ((), (), s32[]{:S(2)}) async-start(), calls=%async_computation.4 | async-start | bytes 3932160 | tf_op jit(solution)/shard_map/all_gather | solution.py:1605
  118.7 14.5 %copy-start.15 = (f32[2,128]{1,0:T(2,128)}, f32[2,128]{1,0:T(2,128)S(1)}, u32[]{:S(2)}) copy-start(f32[2,128]{1,0:T(2,128)S(1)} %convert_element_type.84.gain_ref) | copy-start | bytes 3076
  119.5 2.3 copy-start.27
  121.7 11.5 %copy-start.1 = (f32[1024,128]{1,0:T(8,128)}, f32[1024,128]{1,0:T(8,128)S(1)}, u32[]{:S(2)}) copy-start(f32[1024,128]{1,0:T(8,128)S(1)} %get-tuple-element.120.cos_ref) | copy-start | bytes 1572868
  121.7 11.5 %copy-start.2 = (f32[1024,128]{1,0:T(8,128)}, f32[1024,128]{1,0:T(8,128)S(1)}, u32[]{:S(2)}) copy-start(f32[1024,128]{1,0:T(8,128)S(1)} %get-tuple-element.121.sin_ref) | copy-start | bytes 1572868
  133.2 16.2 %copy-start = (f32[2,1024,128]{2,1,0:T(8,128)}, f32[2,1024,128]{2,1,0:T(8,128)S(1)}, u32[]{:S(2)}) copy-start(f32[2,1024,128]{2,1,0:T(8,128)S(1)} %broadcast_in_dim.9.qcode_ref) | copy-start | bytes 3145732
  133.2 16.2 %copy-start.14 = (f32[2,8,1024]{2,1,0:T(8,128)}, f32[2,8,1024]{2,1,0:T(8,128)S(1)}, u32[]{:S(2)}) copy-start(f32[2,8,1024]{2,1,0:T(8,128)S(1)} %broadcast_in_dim.10.kcode_ref) | copy-start | bytes 196612
  133.2 16.1 %copy-start.26 = (bf16[256,2048]{1,0:T(8,128)(2,1)S(1)}, bf16[256,2048]{1,0:T(8,128)(2,1)}, u32[]{:S(2)}) copy-start(bf16[256,2048]{1,0:T(8,128)(2,1)} %param.15) | copy-start | bytes 3145732
  149.4 1.0 copy-start.18
  149.4 1.2 copy-start.19
  149.4 2.0 copy-start.17
  149.6 1.9 copy-start.8
  212.4 217.3 %reduce-scatter.4.cloned.1.call-start = ((), (), s32[]{:S(2)}) async-start(), calls=%async_computation.5 | async-start | bytes 3932160 | tf_op jit(solution)/shard_map/reduce_scatter | solution.py:1691
  217.0 2.0 copy-start.3
  217.1 49.8 %copy-start.13 = (bf16[2,4,16,2048]{3,2,1,0:T(8,128)(2,1)S(1)}, bf16[2,4,16,2048]{3,2,1,0:T(8,128)(2,1)}, u32[]{:S(2)}) copy-start(bf16[2,4,16,2048]{3,2,1,0:T(8,128)(2,1)} %copy-done.12) | copy-start | bytes 1572868
  309.0 1.7 copy-start.21
  321.1 186.8 %reduce-scatter.8.cloned.1.call-start = ((), (), s32[]{:S(2)}) async-start(), calls=%async_computation.7 | async-start | bytes 7864320 | tf_op jit(solution)/shard_map/reduce_scatter | solution.py:1691
  378.8 238.9 %reduce-scatter.6.cloned.1.call-start = ((), (), s32[]{:S(2)}) async-start(), calls=%async_computation.6 | async-start | bytes 5242880 | tf_op jit(solution)/shard_map/reduce_scatter | solution.py:1691
  379.0 3.0 copy-start.22
  381.9 2.3 copy-start.9
  428.4 1.4 copy-start.16
  507.8 2.3 copy-start.20
  510.2 43.8 %copy-start.24 = (f32[8,32,2048]{2,1,0:T(8,128)S(1)}, f32[8,32,2048]{2,1,0:T(8,128)}, u32[]{:S(2)}) copy-start(f32[8,32,2048]{2,1,0:T(8,128)} %get-tuple-element.108) | copy-start | bytes 6291460
  554.0 1.6 copy-start.23
  554.0 2.2 copy-start.25
  559.1 1.4 copy-start.4
  617.6 1.2 copy-start.10
  (2 other events, 1.7 us)
Sparse Core Ops, SparseCore 0:
  118.4 143.0 all-gather.2
  263.1 61.6 all-gather.4
  327.6 58.8 reduce-scatter.3
  388.7 110.7 reduce-scatter.7
  501.9 91.1 reduce-scatter.5

commit v8 on v7

--- a/solution.py
+++ b/solution.py
@@ -1423,9 +1423,9 @@
             tile_store(k, k % 2).wait()
 
     mixed_load.wait()
+    weigh(grad_ref, mixed_buf, dp_buf.shape[2])
+    rows.middle()
     weigh(normed_ref, dp_buf.reshape(held * length, dp_buf.shape[2]), 0)
-    rows.middle()
-    weigh(grad_ref, mixed_buf, dp_buf.shape[2])
     rows.finish()
     scatter.finish(sum_ref)
     for store in stores:

time: 685 us -> 685 us (level)
  no operation moved by 1% of the time
where the time goes in v8:
time: 685 us; the launch traced here: 682 us
  Pallas kernels  578 us (84%)
  other arithmetic  42.8 us (6%)
  matrix products  21.5 us (3%)
  local copies, waits for them, and re-layouts  20 us (3%)
  between operations  14.7 us (2%)
    pallas_call x1, Pallas kernels, prologue(): pl.pallas_call(functools.partial(prologue_kernel, weight_plan, planes), o...  106 us
    pallas_call x2, Pallas kernels, multiply_scatter(): pl.pallas_call(functools.partial(scatter_kernel, outward, swap_plan), out...  103 us
    pallas_call x2, Pallas kernels, send_back(): pl.pallas_call(functools.partial(return_kernel, plans, values is not None...  92.5 us
    pallas_call x1, Pallas kernels, attend_back(): pl.pallas_call(functools.partial(attend_back_kernel, heads, min(256, leng...  72.6 us
    pallas_call x1, Pallas kernels, feed_back(): pl.pallas_call(backward_kernel, out_shape=(jax.ShapeDtypeStruct((groups,...  54 us
    pallas_call x1, Pallas kernels, plane_gather(): pl.pallas_call(gather_kernel, out_shape=(jax.ShapeDtypeStruct((groups, 8,...  47.9 us
    pallas_call x1, Pallas kernels, gather_and_apply(): pl.pallas_call(apply_kernel, out_shape=(jax.ShapeDtypeStruct((groups, 8,...  44.1 us
    pallas_call x1, Pallas kernels, gather_and_feed(): pl.pallas_call(forward_kernel, out_shape=(jax.ShapeDtypeStruct((groups, 8...  41.9 us
  transfers between devices with their start and end apart: 5, of which 1 were waited for; matrix products, arithmetic and copies ran while one was open for 8% of the time, Pallas kernels for 63%

profile of v8, /device:TPU:0, one launch (start us, length us, event | category | flops | bytes accessed | tf_op | source)
XLA Modules:
  0.0 681.6 jit_solution(10035546465599571667)
XLA Ops:
  8.6 1.2 copy-done.5
  9.9 1.2 copy-done.6
  11.1 106.2 %prologue.1 = (bf16[2,4,32,2048]{3,2,1,0:T(8,128)(2,1)S(1)}, bf16[8,8,32,2048]{3,2,1,0:T(8,128)(2,1)}, f32[8,8,128]{2,1,0:T(8,128)S(1)}, f32[8,8,128]{2,1,0:T(8,...) custom-call(bf16[8,32,2048]{2,1,0:T(8,128)(2,1)S(1)} %bitcast.65, ...), custom_call_target="tpu_custom_call" | custom-call | tf_op jit(solution)/shard_map/prologue/pallas_call | solution.py:1064
  119.5 1.9 fusion.1
  121.7 11.1 %fusion.10.p_ref = f32[2,1024,768]{2,1,0:T(8,128)} fusion(bf16[2,1024,2048]{2,1,0:T(8,128)(2,1)} %bitcast.92, bf16[2048,768,1]{1,0,2:T(8,128)(2,1)S(1)} %bitcast.96), kind=kOutput, calls=%fused_computation.78 | convolution fusion | flops 6442450944 | bytes 17825792 | tf_op jit(solution)/shard_map/dot_general | solution.py:1656
  133.2 16.1 %attend.1 = (bf16[2,1024,256]{2,1,0:T(8,128)(2,1)S(1)}, f32[2,1024,256]{2,1,0:T(8,128)}, bf16[2,1024,256]{2,1,0:T(8,128)(2,1)S(1)}, bf16[2,1024,128]{2,1,0:T(8,128)(2,1)S(1)}, f32[2,2,1024,128]{3,2,1,0:T(8,128)}) custom-call(f32[2,1024,768]{2,1,0:T(8,128)} %fusion.10.p_ref, f32[2,128]{1,0:T(2,128)S(1)} %convert_element_type.84.gain_ref, ...), custom_call_target="tpu_custom_call" | custom-call | flops 2147483648 | bytes 16777216 | tf_op jit(solution)/shard_map/attend/pallas_call | solution.py:1456
  151.6 59.2 %multiply_scatter.2 = (f32[8,32,2048]{2,1,0:T(8,128)S(1)}, bf16[2,4,16,2048]{3,2,1,0:T(8,128)(2,1)S(1)}, bf16[2,256,768]{2,1,0:T(8,128)(2,1)S(1)}) custom-call(bf16[8,8,32,256]{3,2,1,0:T(8,128)(2,1)S(1)} %bitcast.74, bf16[2048,256]{1,0:T(8,128)(2,1)S(1)} %bitcast.66, bf16[8,16,2048]{2,1,0:T(8,128)(2,1)S(1)} %get-tuple-element.111.refs_2_, ...), custom_call_target="tpu_custom_call" | custom-call | flops 2147483648 | bytes 9437184 | tf_op jit(solution)/shard_map/multiply_scatter/pallas_call | solution.py:423
  212.8 2.4 bitcast_multiply_fusion
  215.2 1.8 multiply_reduce_fusion.4
  217.1 1.9 multiply_convert_fusion.x_ref
  219.0 47.9 %plane_gather.1 = (bf16[8,8,32,2048]{3,2,1,0:T(8,128)(2,1)}, bf16[2,4,16,2048]{3,2,1,0:T(8,128)(2,1)S(1)}) custom-call(bf16[8,32,2048]{2,1,0:T(8,128)(2,1)S(1)} %multiply_convert_fusion.x_ref, bf16[8,16,2048]{2,1,0:T(8,128)(2,1)S(1)} %copy-done.3), custom_call_target="tpu_custom_call" | custom-call | tf_op jit(solution)/shard_map/plane_gather/pallas_call | solution.py:154
  267.0 41.9 %gather_and_feed.1 = (bf16[8,8,32,2048]{3,2,1,0:T(8,128)(2,1)}, f32[8,8,32,1536]{3,2,1,0:T(8,128)}, bf16[8,8,32,768]{3,2,1,0:T(8,128)(2,1)S(1)}) custom-call(bf16[8,32,2048]{2,1,0:T(8,128)(2,1)S(1)} %bitcast.61, bf16[8,8,32,2048]{3,2,1,0:T(8,128)(2,1)} %get-tuple-element.70.h_ref, bf16[2048,1536]{1,0:T(8,128)(2,1)} %all-gather.3.cloned.1.call-done.w_ref.up_ref), custom_call_target="tpu_custom_call" | custom-call | flops 12884901888 | bytes 14680064 | tf_op jit(solution)/shard_map/gather_and_feed/pallas_call | solution.py:595
  309.0 1.7 copy-done.21
  310.6 10.4 %bitcast_convert_fusion = bf16[2048,768]{1,0:T(8,128)(2,1)} fusion(bf16[8,8,32,2048]{3,2,1,0:T(8,128)(2,1)} %get-tuple-element.74.g_ref, bf16[8,8,32,768]{3,2,1,0:T(8,128)(2,1)S(1)} %get-tuple-element.73.a_ref), kind=kOutput, calls=%fused_computation | convolution fusion | flops 6444023808 | bytes 14680064 | tf_op jit(solution)/shard_map/dot_general | solution.py:1699
  321.1 3.6 all-gather.5.cloned.1.call-done.down_ref.w_ref
  324.7 54.0 %feed_back.1 = (f32[8,32,2048]{2,1,0:T(8,128)}, bf16[2048,1536]{1,0:T(8,128)(2,1)}) custom-call(bf16[8,8,32,2048]{3,2,1,0:T(8,128)(2,1)} %get-tuple-element.74.g_ref, f32[8,8,32,1536]{3,2,1,0:T(8,128)} %get-tuple-element.75.lin_ref, bf16[2048,768]{1,0:T(8,128)(2,1)} %all-gather.5.cloned.1.call-done.down_ref.w_ref, ...), custom_call_target="tpu_custom_call" | custom-call | flops 32212254720 | bytes 35651584 | tf_op jit(solution)/shard_map/feed_back/pallas_call | solution.py:736
  379.0 3.0 multiply_reduce_fusion
  382.0 2.3 fusion.7.x_ref
  384.3 44.1 %gather_and_apply.1 = (bf16[8,8,32,2048]{3,2,1,0:T(8,128)(2,1)}, f32[8,8,32,256]{3,2,1,0:T(8,128)S(1)}) custom-call(bf16[8,32,2048]{2,1,0:T(8,128)(2,1)S(1)} %fusion.7.x_ref, bf16[2048,256]{1,0:T(8,128)(2,1)S(1)} %bitcast.67), custom_call_target="tpu_custom_call" | custom-call | tf_op jit(solution)/shard_map/gather_and_apply/pallas_call | solution.py:563
  428.4 1.4 copy-done.16
  429.8 72.6 %attend_back.1 = (bf16[2,1024,768]{2,1,0:T(8,128)(2,1)}, f32[8,128]{1,0:T(8,128)}, f32[8,32,2048]{2,1,0:T(8,128)}, bf16[2048,1024]{1,0:T(8,128)(2,1)}, bf16[256,6144]{1,0:T(8,128)(2,1)}) custom-call(f32[2,1024,256]{2,1,0:T(8,128)} %bitcast.73, f32[2,1024,768]{2,1,0:T(8,128)} %fusion.10.p_ref, f32[2,128]{1,0:T(2,128)} %copy-done.15, f32[1024,128]{1,0:T(8,128)} %copy-done.1, ...), custom_call_target="tpu_custom_call" | custom-call | flops 11811160064 | bytes 33554432 | tf_op jit(solution)/shard_map/attend_back/pallas_call | solution.py:1494
  503.1 5.4 convert_element_type.103
  508.5 2.0 copy-done.20
  510.5 43.7 %multiply_scatter.3 = f32[8,32,2048]{2,1,0:T(8,128)S(1)} custom-call(bf16[8,8,32,768]{3,2,1,0:T(8,128)(2,1)S(1)} %bitcast.76, bf16[2048,768]{1,0:T(8,128)(2,1)} %bitcast.95), custom_call_target="tpu_custom_call" | custom-call | flops 6442450944 | bytes 11534336 | tf_op jit(solution)/shard_map/multiply_scatter/pallas_call | solution.py:423
  556.5 2.9 add_convert_fusion
  559.7 1.2 copy-done.4
  560.8 47.6 %send_back.2 = (bf16[8,32,2048]{2,1,0:T(8,128)(2,1)S(1)}, bf16[256,12288]{1,0:T(8,128)(2,1)}) custom-call(bf16[2,4,32,2048]{3,2,1,0:T(8,128)(2,1)S(1)} %bitcast.63, bf16[2,256,1536]{2,1,0:T(8,128)(2,1)S(1)} %bitcast.62), custom_call_target="tpu_custom_call" | custom-call | tf_op jit(solution)/shard_map/send_back/pallas_call | solution.py:1199
  608.7 9.3 %slice_convert_fusion = (f32[256,6144]{1,0:T(8,128)}, f32[256,6144]{1,0:T(8,128)}) fusion(bf16[256,12288]{1,0:T(8,128)(2,1)} %get-tuple-element.96), kind=kLoop, calls=%fused_computation.1 | loop fusion | flops 3145728 | bytes 18874368 | tf_op jit(solution)/shard_map/convert_element_type | solution.py:1785
  618.0 1.2 copy-done.10
  619.2 44.9 %send_back.3 = (bf16[8,32,2048]{2,1,0:T(8,128)(2,1)S(1)}, bf16[256,8192]{1,0:T(8,128)(2,1)}, f32[8,128]{1,0:T(8,128)S(1)}) custom-call(bf16[2,4,32,2048]{3,2,1,0:T(8,128)(2,1)S(1)} %bitcast.64, bf16[2,256,1024]{2,1,0:T(8,128)(2,1)S(1)} %bitcast.68, f32[4,2,8,128]{3,2,1,0:T(8,128)S(1)} %maximum_maximum_fusion.refs_2_), custom_call_target="tpu_custom_call" | custom-call | tf_op jit(solution)/shard_map/send_back/pallas_call | solution.py:1199
  664.1 5.3 slice_convert_fusion.2
  669.5 2.8 slice_convert_fusion.3
  (121 shorter events, 14.7 us)
Async XLA Ops:
  7.2 259.8 %all-gather.3.cloned.1.call-start = ((), (), s32[]{:S(2)}) async-start(), calls=%async_computation.3 | async-start | bytes 7864320 | tf_op jit(solution)/shard_map/all_gather | solution.py:1605
  8.6 1.2 copy-start.5
  9.9 1.2 copy-start.6
  11.1 107.6 %copy-start.28 = (bf16[2,128]{1,0:T(2,128)(2,1)S(1)}, bf16[2,128]{1,0:T(2,128)(2,1)}, u32[]{:S(2)}) copy-start(bf16[2,128]{1,0:T(2,128)(2,1)} %param.20) | copy-start | bytes 1540
  117.3 1.0 copy-start.7
  118.3 206.4 %all-gather.5.cloned.1.call-start = ((), (), s32[]{:S(2)}) async-start(), calls=%async_computation.4 | async-start | bytes 3932160 | tf_op jit(solution)/shard_map/all_gather | solution.py:1605
  118.7 14.5 %copy-start.15 = (f32[2,128]{1,0:T(2,128)}, f32[2,128]{1,0:T(2,128)S(1)}, u32[]{:S(2)}) copy-start(f32[2,128]{1,0:T(2,128)S(1)} %convert_element_type.84.gain_ref) | copy-start | bytes 3076
  119.5 2.3 copy-start.27
  121.7 11.5 %copy-start.1 = (f32[1024,128]{1,0:T(8,128)}, f32[1024,128]{1,0:T(8,128)S(1)}, u32[]{:S(2)}) copy-start(f32[1024,128]{1,0:T(8,128)S(1)} %get-tuple-element.120.cos_ref) | copy-start | bytes 1572868
  121.7 11.5 %copy-start.2 = (f32[1024,128]{1,0:T(8,128)}, f32[1024,128]{1,0:T(8,128)S(1)}, u32[]{:S(2)}) copy-start(f32[1024,128]{1,0:T(8,128)S(1)} %get-tuple-element.121.sin_ref) | copy-start | bytes 1572868
  133.2 16.2 %copy-start = (f32[2,1024,128]{2,1,0:T(8,128)}, f32[2,1024,128]{2,1,0:T(8,128)S(1)}, u32[]{:S(2)}) copy-start(f32[2,1024,128]{2,1,0:T(8,128)S(1)} %broadcast_in_dim.9.qcode_ref) | copy-start | bytes 3145732
  133.2 16.2 %copy-start.14 = (f32[2,8,1024]{2,1,0:T(8,128)}, f32[2,8,1024]{2,1,0:T(8,128)S(1)}, u32[]{:S(2)}) copy-start(f32[2,8,1024]{2,1,0:T(8,128)S(1)} %broadcast_in_dim.10.kcode_ref) | copy-start | bytes 196612
  133.2 16.1 %copy-start.26 = (bf16[256,2048]{1,0:T(8,128)(2,1)S(1)}, bf16[256,2048]{1,0:T(8,128)(2,1)}, u32[]{:S(2)}) copy-start(bf16[256,2048]{1,0:T(8,128)(2,1)} %param.15) | copy-start | bytes 3145732
  149.4 1.0 copy-start.18
  149.4 1.2 copy-start.19
  149.4 2.0 copy-start.17
  149.6 1.9 copy-start.8
  212.4 217.3 %reduce-scatter.4.cloned.1.call-start = ((), (), s32[]{:S(2)}) async-start(), calls=%async_computation.5 | async-start | bytes 3932160 | tf_op jit(solution)/shard_map/reduce_scatter | solution.py:1691
  217.0 2.0 copy-start.3
  217.1 49.8 %copy-start.13 = (bf16[2,4,16,2048]{3,2,1,0:T(8,128)(2,1)S(1)}, bf16[2,4,16,2048]{3,2,1,0:T(8,128)(2,1)}, u32[]{:S(2)}) copy-start(bf16[2,4,16,2048]{3,2,1,0:T(8,128)(2,1)} %copy-done.12) | copy-start | bytes 1572868
  309.0 1.7 copy-start.21
  321.1 187.4 %reduce-scatter.8.cloned.1.call-start = ((), (), s32[]{:S(2)}) async-start(), calls=%async_computation.7 | async-start | bytes 7864320 | tf_op jit(solution)/shard_map/reduce_scatter | solution.py:1691
  378.8 239.2 %reduce-scatter.6.cloned.1.call-start = ((), (), s32[]{:S(2)}) async-start(), calls=%async_computation.6 | async-start | bytes 5242880 | tf_op jit(solution)/shard_map/reduce_scatter | solution.py:1691
  379.0 3.0 copy-start.22
  381.9 2.3 copy-start.9
  428.4 1.4 copy-start.16
  508.5 2.0 copy-start.20
  510.5 43.8 %copy-start.24 = (f32[8,32,2048]{2,1,0:T(8,128)S(1)}, f32[8,32,2048]{2,1,0:T(8,128)}, u32[]{:S(2)}) copy-start(f32[8,32,2048]{2,1,0:T(8,128)} %get-tuple-element.108) | copy-start | bytes 6291460
  554.3 1.6 copy-start.23
  554.3 2.2 copy-start.25
  559.4 1.4 copy-start.4
  618.0 1.2 copy-start.10
  (2 other events, 1.7 us)
Sparse Core Ops, SparseCore 0:
  118.4 143.0 all-gather.2
  263.1 61.6 all-gather.4
  327.6 58.8 reduce-scatter.3
  388.7 110.7 reduce-scatter.7
  502.5 90.5 reduce-scatter.5
